TPU v7x, 32 devices: a whole 2x2x4 slice. The times are simulated.
32 devices in a mesh: fsdp: 4 (over y, x), ctx: 2 (over core), tp: 4 (over z).
Axes of the slice: x: 2, y: 2, z: 4, core: 2. Of those that a mesh axis runs over, the one named last changes fastest.
Arguments:
- tokens: bfloat16 [8192, 2048], P(('fsdp', 'ctx')), may hold values from -6 to 6
- segments: int32 [8192], P('fsdp'), may hold values from 0 to 171, as said below
- cotangent: bfloat16 [8192, 2048], P(('fsdp', 'ctx')), may hold values from -6 to 6
- w_recur: bfloat16 [2048, 2560], P('fsdp', 'tp'), may hold values from -0.125 to 0.125
- w_gelu: bfloat16 [2048, 2560], P('fsdp', 'tp'), may hold values from -0.125 to 0.125
- w_merge: bfloat16 [2560, 2048], P('tp', 'fsdp'), may hold values from -0.3125 to 0.3125
- w_gate: bfloat16 [2048, 6144], P('fsdp', 'tp'), may hold values from -0.125 to 0.125
- w_up: bfloat16 [2048, 6144], P('fsdp', 'tp'), may hold values from -0.125 to 0.125
- w_down: bfloat16 [6144, 2048], P('tp', 'fsdp'), may hold values from -0.15625 to 0.15625
- norm_mix: bfloat16 [2048], P('fsdp'), may hold values from 0.5 to 1.5
- norm_feed: bfloat16 [2048], P('fsdp'), may hold values from 0.5 to 1.5
- conv_taps: bfloat16 [4, 2560], P(None, 'tp'), may hold values from -3 to 3
- conv_bias: bfloat16 [2560], P('tp'), may hold values from -3 to 3
- rate_gate: bfloat16 [16, 160, 160], P('tp'), may hold values from -0.5 to 0.5
- entry_gate: bfloat16 [16, 160, 160], P('tp'), may hold values from -0.5 to 0.5
- rate_bias: bfloat16 [2560], P('tp'), may hold values from -2 to 4
- entry_bias: bfloat16 [2560], P('tp'), may hold values from -4 to 4
- decay_logit: float32 [2560], P('tp'), may hold values from 4.5 to 8.5
Outputs:
- output: bfloat16 [8192, 2048], P(('fsdp', 'ctx'), 'tp')
- grad_tokens: bfloat16 [8192, 2048], P(('fsdp', 'ctx'), 'tp')
- grad_recur: float32 [2048, 2560], P('fsdp', 'tp')
- grad_gelu: float32 [2048, 2560], P('fsdp', 'tp')
- grad_merge: float32 [2560, 2048], P('tp', 'fsdp')
- grad_gate: float32 [2048, 6144], P('fsdp', 'tp')
- grad_up: float32 [2048, 6144], P('fsdp', 'tp')
- grad_down: float32 [6144, 2048], P('tp', 'fsdp')
- grad_mix: float32 [2048], P('fsdp')
- grad_feed: float32 [2048], P('fsdp')
- grad_taps: float32 [4, 2560], P(None, 'tp')
- grad_conv_bias: float32 [2560], P('tp')
- grad_rate_gate: float32 [16, 160, 160], P('tp')
- grad_entry_gate: float32 [16, 160, 160], P('tp')
- grad_rate_bias: float32 [2560], P('tp')
- grad_entry_bias: float32 [2560], P('tp')
- grad_decay: float32 [2560], P('tp')
Inputs may be any that keep to these rules, and one draw needn't show every extreme that they name: `segments`: in each sequence of 2048 tokens the ids never fall and change exactly at each document's first token; the first document has id 0 and the last document has id 2048 // 12 + 1; no document begins within 24 tokens of a border between two pieces of 1024 tokens.
All inputs are finite; a program needn't handle non-finite values.
Results may differ from a plain program's by a relative error of at most 0.019.
Values may be sent and summed in bfloat16 or wider, within the bound.
A program may use at most 256 MiB of HBM per device.

v0:
```python
import jax
import jax.numpy as jnp
from jax import lax
from jax.sharding import PartitionSpec as P

EPS = 1e-06
CGAIN = 8.0


def shifted(block, axis, distance):
    devices = range(lax.axis_size(axis))
    route = [(i - distance, i) for i in devices if i - distance in devices]
    return lax.ppermute(block, axis, route)


def entering(part, axis, combine, identity, reverse):
    count = lax.axis_size(axis)
    place = lax.axis_index(axis)
    ahead = count - 1 - place if reverse else place
    gathered = jax.tree.map(lambda a: lax.all_gather(a, axis), part)
    state = jax.tree.map(lambda a, e: jnp.zeros_like(a) + jnp.asarray(e, a.dtype), part, identity)

    def one(lap, state):
        source = count - 1 - lap if reverse else lap
        return combine(
            state, jax.tree.map(lambda a: lax.dynamic_index_in_dim(a, source, 0, False), gathered)
        )

    return lax.fori_loop(0, ahead, one, state)


def combine(first, second):
    return (first[0] * second[0], second[0] * first[1] + second[1])


def rms_scale(values):
    return lax.rsqrt(jnp.mean(values * values, axis=-1, keepdims=True) + EPS)


def norm_back(values, scale, upstream, gain):
    weighted = upstream * gain
    return scale * weighted - values * scale**3 * jnp.mean(
        values * weighted, axis=-1, keepdims=True
    )


def block_apply(rows, blocks):
    length = rows.shape[0]
    shaped = rows.reshape(length, blocks.shape[0], blocks.shape[1])
    return jnp.einsum("thi,hij->thj", shaped, blocks, preferred_element_type=jnp.float32).reshape(
        length, -1
    )


def block_back(grads, blocks):
    length = grads.shape[0]
    shaped = grads.reshape(length, blocks.shape[0], blocks.shape[2])
    return jnp.einsum("thj,hij->thi", shaped, blocks, preferred_element_type=jnp.float32).reshape(
        length, -1
    )


def block_grad(rows, grads, heads):
    length = rows.shape[0]
    left = rows.reshape(length, heads, -1)
    right = grads.reshape(length, heads, -1)
    return jnp.einsum("thi,thj->hij", left, right, preferred_element_type=jnp.float32)


def shards(
    tokens,
    segments,
    cotangent,
    w_recur,
    w_gelu,
    w_merge,
    w_gate,
    w_up,
    w_down,
    norm_mix,
    norm_feed,
    conv_taps,
    conv_bias,
    rate_gate,
    entry_gate,
    rate_bias,
    entry_bias,
    decay_logit,
):
    piece = tokens.shape[0]
    width = conv_taps.shape[0]
    edge = width - 1
    heads = rate_gate.shape[0]
    channels = conv_taps.shape[1]
    feat_local = tokens.shape[1] // lax.axis_size("tp")
    feat_start = lax.axis_index("tp") * feat_local
    padded_ids = jnp.concatenate([jnp.full((edge,), -1, jnp.int32), segments])
    local_ids = lax.dynamic_slice_in_dim(padded_ids, lax.axis_index("ctx") * piece, piece + edge)
    own_ids = local_ids[edge:]
    keep = (own_ids == local_ids[edge - 1 : edge - 1 + piece])[:, None]
    masks = [
        (local_ids[edge - shift : edge - shift + piece] == own_ids).astype(jnp.float32)[:, None]
        for shift in range(width)
    ]
    whole_recur, whole_gelu, whole_merge, whole_gate, whole_up, whole_down, gain_mix, gain_feed = (
        lax.all_gather(w_recur, "fsdp", axis=0, tiled=True),
        lax.all_gather(w_gelu, "fsdp", axis=0, tiled=True),
        lax.all_gather(w_merge, "fsdp", axis=1, tiled=True),
        lax.all_gather(w_gate, "fsdp", axis=0, tiled=True),
        lax.all_gather(w_up, "fsdp", axis=0, tiled=True),
        lax.all_gather(w_down, "fsdp", axis=1, tiled=True),
        lax.all_gather(norm_mix, "fsdp", axis=0, tiled=True),
        lax.all_gather(norm_feed, "fsdp", axis=0, tiled=True),
    )
    inputs = tokens.astype(jnp.float32)
    scale_one = rms_scale(inputs)
    gain_one = gain_mix.astype(jnp.float32)
    normed = (inputs * scale_one * gain_one).astype(jnp.bfloat16)
    branch = jnp.dot(normed, whole_recur, preferred_element_type=jnp.float32).astype(jnp.bfloat16)
    pre_gelu = jnp.dot(normed, whole_gelu, preferred_element_type=jnp.float32)
    gelu_out, gelu_back = jax.vjp(jax.nn.gelu, pre_gelu)
    before = shifted(branch[piece - edge :], "ctx", 1)
    extended = jnp.concatenate([before, branch], axis=0)
    taps = conv_taps.astype(jnp.float32)
    windows = [
        extended[edge - shift : edge - shift + piece].astype(jnp.float32) * masks[shift]
        for shift in range(width)
    ]
    mixed = conv_bias.astype(jnp.float32) + taps[0] * windows[0]
    for shift in range(1, width):
        mixed = mixed + taps[shift] * windows[shift]
    conv_out = mixed.astype(jnp.bfloat16)
    conv_vals = conv_out.astype(jnp.float32)
    rate = jax.nn.sigmoid(block_apply(conv_out, rate_gate) + rate_bias.astype(jnp.float32))
    entry = jax.nn.sigmoid(block_apply(conv_out, entry_gate) + entry_bias.astype(jnp.float32))
    softer = jax.nn.softplus(-decay_logit)
    log_rate = -CGAIN * rate * softer
    decay_step = jnp.where(keep, jnp.exp(log_rate), 0.0)
    multiplier = jnp.where(keep, jnp.sqrt(-jnp.expm1(2.0 * log_rate)), 1.0)
    running, local_state = lax.associative_scan(
        combine, (decay_step, multiplier * entry * conv_vals)
    )
    unity = jnp.ones((channels,), jnp.float32)
    nothing = jnp.zeros((channels,), jnp.float32)
    _, state_in = entering((running[-1], local_state[-1]), "ctx", combine, (unity, nothing), False)
    states = local_state + running * state_in[None, :]
    gated = (states * gelu_out).astype(jnp.bfloat16)
    merged = lax.psum(jnp.dot(gated, whole_merge, preferred_element_type=jnp.float32), "tp")
    resid = inputs + merged
    scale_two = rms_scale(resid)
    gain_two = gain_feed.astype(jnp.float32)
    normed_two = (resid * scale_two * gain_two).astype(jnp.bfloat16)
    gate_pre = jnp.dot(normed_two, whole_gate, preferred_element_type=jnp.float32)
    up_vals = jnp.dot(normed_two, whole_up, preferred_element_type=jnp.float32)
    gate_act, gate_back = jax.vjp(jax.nn.gelu, gate_pre)
    hidden = (gate_act * up_vals).astype(jnp.bfloat16)
    feed = lax.psum_scatter(
        jnp.dot(hidden, whole_down, preferred_element_type=jnp.float32).astype(jnp.bfloat16),
        "tp",
        scatter_dimension=1,
        tiled=True,
    ).astype(jnp.float32)
    output = (lax.dynamic_slice_in_dim(resid, feat_start, feat_local, 1) + feed).astype(
        jnp.bfloat16
    )
    grad_down = jnp.dot(hidden.T, cotangent, preferred_element_type=jnp.float32)
    d_hidden = jnp.dot(cotangent, whole_down.T, preferred_element_type=jnp.float32)
    d_gate = gate_back(d_hidden * up_vals)[0].astype(jnp.bfloat16)
    d_up = (d_hidden * gate_act).astype(jnp.bfloat16)
    grad_gate = jnp.dot(normed_two.T, d_gate, preferred_element_type=jnp.float32)
    grad_up = jnp.dot(normed_two.T, d_up, preferred_element_type=jnp.float32)
    part_two = jnp.dot(d_gate, whole_gate.T, preferred_element_type=jnp.float32) + jnp.dot(
        d_up, whole_up.T, preferred_element_type=jnp.float32
    )
    d_normed_two = lax.psum(part_two.astype(jnp.bfloat16), "tp").astype(jnp.float32)
    grad_feed = jnp.sum(d_normed_two * resid * scale_two, axis=0)
    d_resid = cotangent.astype(jnp.float32) + norm_back(resid, scale_two, d_normed_two, gain_two)
    d_merge_in = d_resid.astype(jnp.bfloat16)
    grad_merge = jnp.dot(gated.T, d_merge_in, preferred_element_type=jnp.float32)
    d_gated = jnp.dot(d_merge_in, whole_merge.T, preferred_element_type=jnp.float32)
    d_states = d_gated * gelu_out
    d_gelu_pre = gelu_back(d_gated * states)[0].astype(jnp.bfloat16)
    following = jnp.concatenate([decay_step[1:], unity[None, :]], axis=0)
    carried, local_grad = lax.associative_scan(combine, (following, d_states), reverse=True)
    _, grad_in = entering(
        (decay_step[0] * carried[0], decay_step[0] * local_grad[0]),
        "ctx",
        combine,
        (unity, nothing),
        True,
    )
    d_state = local_grad + carried * grad_in[None, :]
    previous = jnp.concatenate([state_in[None, :], states[:-1]], axis=0)
    d_log = jnp.where(
        keep,
        d_state * previous * decay_step
        - d_state * entry * conv_vals * jnp.exp(2.0 * log_rate) / multiplier,
        0.0,
    )
    d_rate = (-CGAIN * softer * d_log * rate * (1.0 - rate)).astype(jnp.bfloat16)
    d_entry = (d_state * multiplier * conv_vals * entry * (1.0 - entry)).astype(jnp.bfloat16)
    grad_decay = jnp.sum(CGAIN * d_log * rate, axis=0) * jax.nn.sigmoid(-decay_logit)
    grad_rate_gate = block_grad(conv_out, d_rate, heads)
    grad_entry_gate = block_grad(conv_out, d_entry, heads)
    grad_rate_bias = jnp.sum(d_rate.astype(jnp.float32), axis=0)
    grad_entry_bias = jnp.sum(d_entry.astype(jnp.float32), axis=0)
    d_conv = (
        d_state * multiplier * entry
        + block_back(d_rate, rate_gate)
        + block_back(d_entry, entry_gate)
    )
    grad_conv_bias = jnp.sum(d_conv, axis=0)
    grad_taps = jnp.stack([jnp.sum(d_conv * windows[shift], axis=0) for shift in range(width)])
    d_extended = jnp.pad(taps[0] * d_conv * masks[0], ((edge, 0), (0, 0)))
    for shift in range(1, width):
        d_extended = d_extended + jnp.pad(
            taps[shift] * d_conv * masks[shift], ((edge - shift, shift), (0, 0))
        )
    returned = shifted(d_extended[:edge], "ctx", -1)
    d_branch = (d_extended[edge:] + jnp.pad(returned, ((piece - edge, 0), (0, 0)))).astype(
        jnp.bfloat16
    )
    grad_recur = jnp.dot(normed.T, d_branch, preferred_element_type=jnp.float32)
    grad_gelu = jnp.dot(normed.T, d_gelu_pre, preferred_element_type=jnp.float32)
    part_one = jnp.dot(d_branch, whole_recur.T, preferred_element_type=jnp.float32) + jnp.dot(
        d_gelu_pre, whole_gelu.T, preferred_element_type=jnp.float32
    )
    d_normed = lax.psum(part_one.astype(jnp.bfloat16), "tp").astype(jnp.float32)
    grad_mix = jnp.sum(d_normed * inputs * scale_one, axis=0)
    d_inputs = d_resid + norm_back(inputs, scale_one, d_normed, gain_one)
    grad_tokens = lax.dynamic_slice_in_dim(d_inputs, feat_start, feat_local, 1).astype(jnp.bfloat16)
    (
        shard_recur,
        shard_gelu,
        shard_merge,
        shard_gate,
        shard_up,
        shard_down,
        shard_mix,
        shard_feed,
    ) = (
        lax.psum_scatter(
            grad_recur.astype(jnp.bfloat16), "fsdp", scatter_dimension=0, tiled=True
        ).astype(jnp.float32),
        lax.psum_scatter(
            grad_gelu.astype(jnp.bfloat16), "fsdp", scatter_dimension=0, tiled=True
        ).astype(jnp.float32),
        lax.psum_scatter(
            grad_merge.astype(jnp.bfloat16), "fsdp", scatter_dimension=1, tiled=True
        ).astype(jnp.float32),
        lax.psum_scatter(
            grad_gate.astype(jnp.bfloat16), "fsdp", scatter_dimension=0, tiled=True
        ).astype(jnp.float32),
        lax.psum_scatter(
            grad_up.astype(jnp.bfloat16), "fsdp", scatter_dimension=0, tiled=True
        ).astype(jnp.float32),
        lax.psum_scatter(
            grad_down.astype(jnp.bfloat16), "fsdp", scatter_dimension=1, tiled=True
        ).astype(jnp.float32),
        lax.psum_scatter(
            grad_mix.astype(jnp.bfloat16), "fsdp", scatter_dimension=0, tiled=True
        ).astype(jnp.float32),
        lax.psum_scatter(
            grad_feed.astype(jnp.bfloat16), "fsdp", scatter_dimension=0, tiled=True
        ).astype(jnp.float32),
    )
    sum_recur, sum_gelu, sum_merge, sum_gate, sum_up, sum_down, sum_mix, sum_feed = (
        lax.psum(shard_recur.astype(jnp.bfloat16), "ctx").astype(jnp.float32),
        lax.psum(shard_gelu.astype(jnp.bfloat16), "ctx").astype(jnp.float32),
        lax.psum(shard_merge.astype(jnp.bfloat16), "ctx").astype(jnp.float32),
        lax.psum(shard_gate.astype(jnp.bfloat16), "ctx").astype(jnp.float32),
        lax.psum(shard_up.astype(jnp.bfloat16), "ctx").astype(jnp.float32),
        lax.psum(shard_down.astype(jnp.bfloat16), "ctx").astype(jnp.float32),
        lax.psum(shard_mix.astype(jnp.bfloat16), "ctx").astype(jnp.float32),
        lax.psum(shard_feed.astype(jnp.bfloat16), "ctx").astype(jnp.float32),
    )
    (
        sum_taps,
        sum_conv_bias,
        sum_rate_gate,
        sum_entry_gate,
        sum_rate_bias,
        sum_entry_bias,
        sum_decay,
    ) = (
        lax.psum(grad_taps.astype(jnp.bfloat16), ("fsdp", "ctx")).astype(jnp.float32),
        lax.psum(grad_conv_bias.astype(jnp.bfloat16), ("fsdp", "ctx")).astype(jnp.float32),
        lax.psum(grad_rate_gate.astype(jnp.bfloat16), ("fsdp", "ctx")).astype(jnp.float32),
        lax.psum(grad_entry_gate.astype(jnp.bfloat16), ("fsdp", "ctx")).astype(jnp.float32),
        lax.psum(grad_rate_bias.astype(jnp.bfloat16), ("fsdp", "ctx")).astype(jnp.float32),
        lax.psum(grad_entry_bias.astype(jnp.bfloat16), ("fsdp", "ctx")).astype(jnp.float32),
        lax.psum(grad_decay.astype(jnp.bfloat16), ("fsdp", "ctx")).astype(jnp.float32),
    )
    return (
        output,
        grad_tokens,
        sum_recur,
        sum_gelu,
        sum_merge,
        sum_gate,
        sum_up,
        sum_down,
        sum_mix,
        sum_feed,
        sum_taps,
        sum_conv_bias,
        sum_rate_gate,
        sum_entry_gate,
        sum_rate_bias,
        sum_entry_bias,
        sum_decay,
    )


def solution(mesh):
    placed = (
        P(("fsdp", "ctx"), None),
        P("fsdp"),
        P(("fsdp", "ctx"), None),
        P("fsdp", "tp"),
        P("fsdp", "tp"),
        P("tp", "fsdp"),
        P("fsdp", "tp"),
        P("fsdp", "tp"),
        P("tp", "fsdp"),
        P("fsdp"),
        P("fsdp"),
        P(None, "tp"),
        P("tp"),
        P("tp", None, None),
        P("tp", None, None),
        P("tp"),
        P("tp"),
        P("tp"),
    )
    return jax.shard_map(
        shards,
        mesh=mesh,
        in_specs=placed,
        out_specs=(
            P(("fsdp", "ctx"), "tp"),
            P(("fsdp", "ctx"), "tp"),
            P("fsdp", "tp"),
            P("fsdp", "tp"),
            P("tp", "fsdp"),
            P("fsdp", "tp"),
            P("fsdp", "tp"),
            P("tp", "fsdp"),
            P("fsdp"),
            P("fsdp"),
            P(None, "tp"),
            P("tp"),
            P("tp", None, None),
            P("tp", None, None),
            P("tp"),
            P("tp"),
            P("tp"),
        ),
        check_vma=False,
    )
```

profile of v0, /device:TPU:0, one launch (start us, length us, event | category | flops | bytes accessed | tf_op | source)
XLA Modules:
  0.0 2098.7 jit_solution(5306248175570880598)
XLA Ops:
  22.9 29.2 %all-gather.13.cloned.1.call-done = bf16[2048,640]{1,0:T(8,128)(2,1)} async-done(((bf16[512,640]{1,0:T(8,128)(2,1)}), bf16[2048,640]{1,0:T(8,128)(2,1)}) %all-gather.13.cloned.1.call-update) | async-done | bytes 2621456 | tf_op jit(solution)/shard_map/all_gather | solution.py:106
  352.1 12.9 multiply_convert_fusion.4
  383.7 281.0 %all-reduce.101.cloned.1.call-done = f32[1024,2048]{1,0:T(8,128)} async-done(((f32[1024,2048]{1,0:T(8,128)}), f32[1024,2048]{1,0:T(8,128)}) %all-reduce.101.cloned.1.call-update) | async-done | bytes 8388624 | tf_op jit(solution)/shard_map/psum | solution.py:148
  677.2 58.3 %all-gather.19.cloned.1.call-done = bf16[2048,1536]{1,0:T(8,128)(2,1)} async-done(((bf16[512,1536]{1,0:T(8,128)(2,1)}), bf16[2048,1536]{1,0:T(8,128)(2,1)}) %all-gather.19.cloned.1.call-update) | async-done | bytes 6291472 | tf_op jit(solution)/shard_map/all_gather | solution.py:109
  735.4 11.8 fusion.113
  747.3 59.9 %all-gather.21.cloned.1.call-done = bf16[2048,1536]{1,0:T(8,128)(2,1)} async-done(((bf16[512,1536]{1,0:T(8,128)(2,1)}), bf16[2048,1536]{1,0:T(8,128)(2,1)}) %all-gather.21.cloned.1.call-update) | async-done | bytes 6291472 | tf_op jit(solution)/shard_map/all_gather | solution.py:110
  807.2 11.8 fusion.114
  819.0 60.0 %all-gather.23.cloned.1.call-done = bf16[1536,2048]{1,0:T(8,128)(2,1)} async-done(((bf16[1536,512]{1,0:T(8,128)(2,1)}), bf16[1536,2048]{1,0:T(8,128)(2,1)}) %all-gather.23.cloned.1.call-update) | async-done | bytes 6291472 | tf_op jit(solution)/shard_map/all_gather | solution.py:111
  878.9 18.5 multiply_convert_fusion.1
  974.3 98.9 %all-reduce.103.cloned.1.call-done = bf16[1024,2048]{1,0:T(8,128)(2,1)} async-done(((bf16[1024,2048]{1,0:T(8,128)(2,1)}), bf16[1024,2048]{1,0:T(8,128)(2,1)}) %all-reduce.103.cloned.1.call-update) | async-done | bytes 4194320 | tf_op jit(solution)/shard_map/psum | solution.py:175
  1259.2 11.0 slice.857
  1398.9 20.9 rev.9
  1419.8 13.0 rev.8
  1492.7 11.5 convolution_convert_fusion.2
  1504.3 12.0 convolution_convert_fusion.1
  1516.3 11.3 convolution_convert_fusion
  1533.0 11.1 convolution_convert_fusion.3
  1555.3 49.2 %reduce-scatter.16.cloned.1.call-done = bf16[512,1536]{1,0:T(8,128)(2,1)} async-done(((bf16[2048,1536]{1,0:T(8,128)(2,1)}), bf16[512,1536]{1,0:T(8,128)(2,1)}) %reduce-scatter.16.cloned.1.call-update) | async-done | bytes 1572880 | tf_op jit(solution)/shard_map/reduce_scatter | solution.py:251
  1604.5 73.0 %reduce-scatter.18.cloned.1.call-done = bf16[512,1536]{1,0:T(8,128)(2,1)} async-done(((bf16[2048,1536]{1,0:T(8,128)(2,1)}), bf16[512,1536]{1,0:T(8,128)(2,1)}) %reduce-scatter.18.cloned.1.call-update) | async-done | bytes 1572880 | tf_op jit(solution)/shard_map/reduce_scatter | solution.py:254
  1677.6 72.9 %reduce-scatter.20.cloned.1.call-done = bf16[1536,512]{1,0:T(8,128)(2,1)} async-done(((bf16[1536,2048]{1,0:T(8,128)(2,1)}), bf16[1536,512]{1,0:T(8,128)(2,1)}) %reduce-scatter.20.cloned.1.call-update) | async-done | bytes 1572880 | tf_op jit(solution)/shard_map/reduce_scatter | solution.py:257
  1758.5 23.0 %all-reduce.90 = (bf16[4,640]{1,0:T(4,128)(2,1)S(1)}, bf16[640]{0:T(1024)(128)(2,1)S(1)}, bf16[640]{0:T(1024)(128)(2,1)S(1)}, bf16[640]{0:T(1024)(128)(2,1)S(1)}, bf16[640]{0:T(1024)(128)(2,1)S(1)}) all-reduce(bf16[4,640]{1,0:T(4,128)(2,1)S(1)} %pad_maximum_fusion.36, ...), channel_id=1, replica_groups=mesh['fsdp'=4,'ctx'=2,'tp'=4] {'fsdp','ctx'}, use_global_device_ids=true, to_apply=%region_34.35 | all-reduce | flops 5120 | bytes 20480 | tf_op jit(solution)/shard_map/psum | solution.py:286
  1784.5 25.0 %all-reduce.107.cloned.1.call-done = (bf16[4,160,160]{2,1,0:T(8,128)(2,1)}, bf16[4,160,160]{2,1,0:T(8,128)(2,1)}) async-done(((bf16[4,160,160]{2,1,0:T(8,128)(2,1)}, bf16[4,160,160]{2,1,0:T(8,128)(2,1)}), (bf16[4,160,160]{2,1,0:T(8,128)(2,1)}, bf16[4,160,160]{2,1,0:T(8,128)(2,1)})) %all-reduce.107.cloned.1.call-update) | async-done | bytes 409616 | tf_op jit(solution)/shard_map/psum | solution.py:288
  1813.1 74.6 %reduce-scatter.8.cloned.1.call-done = bf16[1024,512]{1,0:T(8,128)(2,1)} async-done(((bf16[1024,2048]{1,0:T(8,128)(2,1)}), bf16[1024,512]{1,0:T(8,128)(2,1)}) %reduce-scatter.8.cloned.1.call-update) | async-done | bytes 1048592 | tf_op jit(solution)/shard_map/reduce_scatter | solution.py:157
  1890.9 154.5 %all-reduce.105.cloned.1.call-done = bf16[1024,2048]{1,0:T(8,128)(2,1)} async-done(((bf16[1024,2048]{1,0:T(8,128)(2,1)}), bf16[1024,2048]{1,0:T(8,128)(2,1)}) %all-reduce.105.cloned.1.call-update) | async-done | bytes 4194320 | tf_op jit(solution)/shard_map/psum | solution.py:228
  (766 shorter events, 876.3 us)
Async XLA Ops:
  7.2 61.4 %copy-start = (bf16[4,160,160]{2,1,0:T(8,128)(2,1)S(1)}, bf16[4,160,160]{2,1,0:T(8,128)(2,1)}, u32[]{:S(2)}) copy-start(bf16[4,160,160]{2,1,0:T(8,128)(2,1)} %param.35) | copy-start | bytes 614404
  7.2 44.9 %all-gather.13.cloned.1.call-start = ((), (), s32[]{:S(2)}) async-start(), calls=%async_computation.7 | async-start | bytes 3276800 | tf_op jit(solution)/shard_map/all_gather | solution.py:106
  7.9 344.1 %all-gather.15.cloned.1.call-start = ((), (), s32[]{:S(2)}) async-start(), calls=%async_computation.8 | async-start | bytes 3276800 | tf_op jit(solution)/shard_map/all_gather | solution.py:107
  8.7 356.2 %all-gather.17.cloned.1.call-start = ((), (), s32[]{:S(2)}) async-start(), calls=%async_computation.9 | async-start | bytes 3276800 | tf_op jit(solution)/shard_map/all_gather | solution.py:108
  9.5 655.3 %all-reduce.101.cloned.1.call-start = ((), (), s32[]{:S(2)}) async-start(), calls=%async_computation.10 | async-start | bytes 16777216 | tf_op jit(solution)/shard_map/psum | solution.py:148
  22.9 53.2 %copy-start.71 = (f32[640]{0:T(1024)}, f32[640]{0:T(1024)S(1)}, u32[]{:S(2)}) copy-start(f32[640]{0:T(1024)S(1)} %fusion.70) | copy-start | bytes 7684
  58.7 2.4 collective-permute-start
  373.9 361.6 %all-gather.19.cloned.1.call-start = ((), (), s32[]{:S(2)}) async-start(), calls=%async_computation.11 | async-start | bytes 7864320 | tf_op jit(solution)/shard_map/all_gather | solution.py:109
  374.5 432.7 %all-gather.21.cloned.1.call-start = ((), (), s32[]{:S(2)}) async-start(), calls=%async_computation.12 | async-start | bytes 7864320 | tf_op jit(solution)/shard_map/all_gather | solution.py:110
  375.0 503.9 %all-gather.23.cloned.1.call-start = ((), (), s32[]{:S(2)}) async-start(), calls=%async_computation.13 | async-start | bytes 7864320 | tf_op jit(solution)/shard_map/all_gather | solution.py:111
  375.8 697.5 %all-reduce.103.cloned.1.call-start = ((), (), s32[]{:S(2)}) async-start(), calls=%async_computation.15 | async-start | bytes 8388608 | tf_op jit(solution)/shard_map/psum | solution.py:175
  918.1 637.1 %reduce-scatter.14.cloned.1.call-start = ((), (), s32[]{:S(2)}) async-start(), calls=%async_computation.19 | async-start | bytes 3276800 | tf_op jit(solution)/shard_map/reduce_scatter | solution.py:248
  1270.3 285.0 %reduce-scatter.12.cloned.1.call-start = ((), (), s32[]{:S(2)}) async-start(), calls=%async_computation.18 | async-start | bytes 3276800 | tf_op jit(solution)/shard_map/reduce_scatter | solution.py:245
  1440.8 114.5 %reduce-scatter.10.cloned.1.call-start = ((), (), s32[]{:S(2)}) async-start(), calls=%async_computation.17 | async-start | bytes 3276800 | tf_op jit(solution)/shard_map/reduce_scatter | solution.py:242
  1483.4 3.3 collective-permute-start.1
  1492.5 112.0 %reduce-scatter.16.cloned.1.call-start = ((), (), s32[]{:S(2)}) async-start(), calls=%async_computation.20 | async-start | bytes 7864320 | tf_op jit(solution)/shard_map/reduce_scatter | solution.py:251
  1504.2 173.3 %reduce-scatter.18.cloned.1.call-start = ((), (), s32[]{:S(2)}) async-start(), calls=%async_computation.21 | async-start | bytes 7864320 | tf_op jit(solution)/shard_map/reduce_scatter | solution.py:254
  1516.3 234.2 %reduce-scatter.20.cloned.1.call-start = ((), (), s32[]{:S(2)}) async-start(), calls=%async_computation.22 | async-start | bytes 7864320 | tf_op jit(solution)/shard_map/reduce_scatter | solution.py:257
  1527.7 281.8 %all-reduce.107.cloned.1.call-start = ((), (), s32[]{:S(2)}) async-start(), calls=%async_computation.23 | async-start | bytes 1310720 | tf_op jit(solution)/shard_map/psum | solution.py:288
  1532.8 354.9 %reduce-scatter.8.cloned.1.call-start = ((), (), s32[]{:S(2)}) async-start(), calls=%async_computation.14 | async-start | bytes 5242880 | tf_op jit(solution)/shard_map/reduce_scatter | solution.py:157
  1544.2 501.3 %all-reduce.105.cloned.1.call-start = ((), (), s32[]{:S(2)}) async-start(), calls=%async_computation.16 | async-start | bytes 8388608 | tf_op jit(solution)/shard_map/psum | solution.py:228
  1555.2 525.1 %all-reduce.109.cloned.1.call-start = ((), (), s32[]{:S(2)}) async-start(), calls=%async_computation.24 | async-start | bytes 13369344 | tf_op jit(solution)/shard_map/psum | solution.py:268
  1890.9 162.2 %copy-start.98 = (bf16[2048]{0:T(1024)(128)(2,1)S(1)}, bf16[2048]{0:T(1024)(128)(2,1)}, u32[]{:S(2)}) copy-start(bf16[2048]{0:T(1024)(128)(2,1)} %get-tuple-element.147) | copy-start | bytes 12292
  1890.9 176.0 %copy-start.97 = (f32[1024]{0:T(1024)S(1)}, f32[1024]{0:T(1024)}, u32[]{:S(2)}) copy-start(f32[1024]{0:T(1024)} %get-tuple-element.318) | copy-start | bytes 12292
  (143 other events, 1278.0 us)
Sparse Core Ops, SparseCore 0:
  9.8 42.2 all-gather.12
  54.0 39.4 all-gather.14
  95.3 39.3 all-gather.16
  374.0 290.6 all-reduce.100
  666.4 68.9 all-gather.18
  737.1 70.0 all-gather.20
  809.0 69.8 all-gather.22
  918.2 154.9 all-reduce.102
  1270.4 38.5 reduce-scatter.13
  1440.9 38.5 reduce-scatter.11
  1492.6 38.9 reduce-scatter.9
  1534.5 70.0 reduce-scatter.15
  1607.5 70.0 reduce-scatter.17
  1680.4 70.0 reduce-scatter.19
  1754.0 55.3 all-reduce.106
  1811.6 76.0 reduce-scatter.7
  1889.9 155.5 all-reduce.104
  2048.5 31.7 all-reduce.108
where the time goes:
time: 2120 us; the launch traced here: 2100 us
  waiting for transfers between devices  1050 us (50%)
  local copies, waits for them, and re-layouts  551 us (26%)
  other arithmetic  222 us (10%)
  matrix products  193 us (9%)
  blocking collectives  60.2 us (3%)
    psum x1, waiting for transfers between devices, shards(): lax.psum(jnp.dot(gated, whole_merge, preferred_element_type=jnp.float32),...  281 us
    slice x73, local copies, waits for them, and re-layouts, shards(): lax.associative_scan(combine, (following, d_states), reverse=True)  202 us
    psum x1, waiting for transfers between devices, shards(): d_normed = lax.psum(part_one.astype(jnp.bfloat16), 'tp').astype(jnp.float32)  155 us
    slice x68, local copies, waits for them, and re-layouts, shards(): lax.associative_scan(combine, (decay_step, multiplier * entry * conv_vals))  129 us
    psum x1, waiting for transfers between devices, shards(): lax.psum(part_two.astype(jnp.bfloat16), 'tp').astype(jnp.float32)  98.9 us
    pad x36, local copies, waits for them, and re-layouts, shards(): lax.associative_scan(combine, (following, d_states), reverse=True)  77.8 us
    pad x36, local copies, waits for them, and re-layouts, shards(): lax.associative_scan(combine, (decay_step, multiplier * entry * conv_vals))  77 us
    reduce_scatter x1, waiting for transfers between devices, shards(): lax.psum_scatter(jnp.dot(hidden, whole_down, preferred_element_type=jnp.f...  74.6 us
  transfers between devices with their start and end apart: 20, of which 15 were waited for; matrix products, arithmetic and copies ran while one was open for 33% of the time, Pallas kernels for 0%

commit v1 on v0

v1 whole, which is shorter than its diff:
```python
import jax
import jax.numpy as jnp
from jax import lax
from jax.experimental import pallas as pl
from jax.experimental.pallas import tpu as pltpu
from jax.sharding import PartitionSpec as P

EPS = 1e-06
CGAIN = 8.0
ROOT = 0.7978845608
CUBE = 0.044715
TILE = 128
SEGS = 8
F32 = jnp.float32
BF16 = jnp.bfloat16


def swap_cores(block):
    size = lax.axis_size("ctx")
    return lax.ppermute(block, "ctx", [(i, size - 1 - i) for i in range(size)])


def shifted(block, axis, distance):
    devices = range(lax.axis_size(axis))
    route = [(i - distance, i) for i in devices if i - distance in devices]
    return lax.ppermute(block, axis, route)


def gather_rows(shard):
    half = shard.shape[0] // 2
    core = lax.axis_index("ctx")
    mine = lax.dynamic_slice_in_dim(shard, core * half, half, 0)
    mine = lax.all_gather(mine, "fsdp", axis=0)
    other = swap_cores(mine)
    first = jnp.where(core == 0, mine, other)
    second = jnp.where(core == 0, other, mine)
    return jnp.stack([first, second], axis=1).reshape(-1, shard.shape[1])


def scatter_rows(grad):
    shards = lax.axis_size("fsdp")
    core = lax.axis_index("ctx")
    halves = grad.reshape(shards, 2, grad.shape[0] // shards // 2, grad.shape[1])
    mine = lax.dynamic_index_in_dim(halves, core, 1, False)
    send = lax.dynamic_index_in_dim(halves, 1 - core, 1, False).astype(BF16)
    pair = (mine + swap_cores(send).astype(F32)).astype(BF16)
    total = lax.psum_scatter(pair.reshape(-1, grad.shape[1]), "fsdp", scatter_dimension=0, tiled=True)
    other = swap_cores(total)
    first = jnp.where(core == 0, total, other)
    second = jnp.where(core == 0, other, total)
    return jnp.concatenate([first, second], axis=0).astype(F32)


def gelu_pair(q):
    tanh = jnp.tanh(ROOT * (q + CUBE * q * q * q))
    value = 0.5 * q * (1.0 + tanh)
    slope = 0.5 * (1.0 + tanh) + 0.5 * q * (1.0 - tanh * tanh) * ROOT * (1.0 + 3.0 * CUBE * q * q)
    return value, slope


def rms_scale(values):
    return lax.rsqrt(jnp.mean(values * values, axis=-1, keepdims=True) + EPS)


def decay_parts(rate, softer, keep):
    gap = 2.0 * CGAIN * rate * softer
    decay = jnp.exp(-0.5 * gap)
    series = gap * (
        1.0
        - gap / 2.0
        * (1.0 - gap / 3.0 * (1.0 - gap / 4.0 * (1.0 - gap / 5.0 * (1.0 - gap / 6.0 * (1.0 - gap / 7.0)))))
    )
    square = jnp.where(gap < 0.25, series, 1.0 - decay * decay)
    return jnp.where(keep, decay, 0.0), jnp.where(keep, square, 1.0)


LANES = 128


def put_lanes(ref, block, rows):
    for lane in range(ref.shape[0]):
        ref[lane, 0:rows, :] = block[:, lane * LANES : (lane + 1) * LANES]


def sweep(decay_ref, value_ref, state_ref, product_ref, out_ref, run_ref, carry_ref, reverse, offset):
    groups, rows, _ = value_ref.shape
    steps = rows // SEGS
    place = lax.broadcasted_iota(jnp.int32, (SEGS, LANES), 0)
    if reverse:
        place = SEGS - 1 - place

    def moved(block, by, fill):
        turned = pltpu.roll(block, SEGS - by if reverse else by, 0)
        return jnp.where(place >= by, turned, fill)

    for lane in range(groups):
        lanes = slice(lane * LANES, (lane + 1) * LANES)
        state = jnp.zeros((SEGS, LANES), F32)
        product = jnp.ones((SEGS, LANES), F32)
        for step in reversed(range(steps)) if reverse else range(steps):
            spot = pl.ds(step, SEGS, stride=steps)
            decay = decay_ref[lane, pl.ds(step + offset, SEGS, stride=steps), :]
            state = decay * state + value_ref[lane, spot, :]
            product = product * decay
            state_ref[lane, spot, :] = state
            product_ref[lane, spot, :] = product
        for by in (1, 2, 4):
            state = state + product * moved(state, by, 0.0)
            product = product * moved(product, by, 1.0)
        carry = carry_ref[0:1, lanes]
        carry_run = carry_ref[8:9, lanes]
        state = state + product * carry
        product = product * carry_run
        enter = moved(state, 1, carry)
        enter_run = moved(product, 1, carry_run)
        for seg in range(SEGS):
            span = slice(seg * steps, (seg + 1) * steps)
            inner = product_ref[lane, span, :]
            out_ref[span, lanes] = state_ref[lane, span, :] + inner * enter[seg : seg + 1, :]
            run_ref[span, lanes] = inner * enter_run[seg : seg + 1, :]
        last = 0 if reverse else SEGS - 1
        carry_ref[0:1, lanes] = state[last : last + 1, :]
        carry_ref[8:9, lanes] = product[last : last + 1, :]


def forward_kernel(
    branch_ref, halo_ref, mask_ref, taps_ref, bias_ref, gates_ref, gate_bias_ref, softer_ref,
    conv_ref, rate_ref, entry_ref, state_ref, run_ref,
    window, decay, value, inner, product, carry,
):
    rows, chans = conv_ref.shape
    spot = pl.program_id(0)

    @pl.when(spot == 0)
    def _():
        window[0:8, :] = halo_ref[...].astype(F32)
        carry[0:8, :] = jnp.zeros((8, chans), F32)
        carry[8:16, :] = jnp.ones((8, chans), F32)

    @pl.when(spot > 0)
    def _():
        window[0:8, :] = window[rows : rows + 8, :]

    window[8 : rows + 8, :] = branch_ref[...].astype(F32)
    mixed = bias_ref[...] + taps_ref[0:1, :] * window[8 : rows + 8, :]
    for shift in range(1, taps_ref.shape[0]):
        moved = window[8 - shift : 8 - shift + rows, :]
        mixed = mixed + taps_ref[shift : shift + 1, :] * (moved * mask_ref[:, shift : shift + 1])
    conv = mixed.astype(BF16)
    conv_ref[...] = conv
    pre = jnp.dot(conv, gates_ref[...], preferred_element_type=F32) + gate_bias_ref[...]
    rate = jax.nn.sigmoid(pre[:, :chans])
    entry = jax.nn.sigmoid(pre[:, chans:])
    rate_ref[...] = rate
    entry_ref[...] = entry
    keep = jnp.broadcast_to(mask_ref[:, 0:1], (rows, chans)) > 0.5
    step, square = decay_parts(rate, softer_ref[...], keep)
    put_lanes(decay, step, rows)
    put_lanes(value, jnp.sqrt(square) * entry * conv.astype(F32), rows)
    sweep(decay, value, inner, product, state_ref, run_ref, carry, False, 0)


def tile_spec(width, count=None):
    if count is None:
        return pl.BlockSpec((TILE, width), lambda i: (i, 0))
    return pl.BlockSpec((TILE, width), lambda i: (count - 1 - i, 0))


def fixed_spec(shape):
    return pl.BlockSpec(shape, lambda i: (0, 0))


def recur_forward(branch, halo, masks, taps, bias, gates, gate_bias, softer):
    rows, chans = branch.shape
    wide = jax.ShapeDtypeStruct((rows, chans), F32)
    return pl.pallas_call(
        forward_kernel,
        grid=(rows // TILE,),
        out_shape=(jax.ShapeDtypeStruct((rows, chans), BF16), wide, wide, wide, wide),
        in_specs=[
            tile_spec(chans),
            fixed_spec((8, chans)),
            tile_spec(masks.shape[1]),
            fixed_spec(taps.shape),
            fixed_spec((1, chans)),
            fixed_spec(gates.shape),
            fixed_spec((1, 2 * chans)),
            fixed_spec((1, chans)),
        ],
        out_specs=[tile_spec(chans)] * 5,
        scratch_shapes=[
            pltpu.VMEM((TILE + 8, chans), F32),
            pltpu.VMEM((chans // LANES, TILE, LANES), F32),
            pltpu.VMEM((chans // LANES, TILE, LANES), F32),
            pltpu.VMEM((chans // LANES, TILE, LANES), F32),
            pltpu.VMEM((chans // LANES, TILE, LANES), F32),
            pltpu.VMEM((16, chans), F32),
        ],
        cost_estimate=pl.CostEstimate(
            flops=2 * rows * chans * 2 * chans, bytes_accessed=24 * rows * chans, transcendentals=5 * rows * chans
        ),
        name="recur_forward",
    )(branch, halo, masks, taps, bias, gates, gate_bias, softer)


def adjoint_kernel(
    rate_ref, up_ref, mask_ref, softer_ref, grad_ref, run_ref, head_ref, decay, value, inner, product, carry
):
    rows, chans = rate_ref.shape
    groups = chans // LANES
    spot = pl.program_id(0)

    @pl.when(spot == 0)
    def _():
        for lane in range(groups):
            decay[lane, rows : rows + 8, :] = jnp.ones((8, LANES), F32)
        carry[0:8, :] = jnp.zeros((8, chans), F32)
        carry[8:16, :] = jnp.ones((8, chans), F32)

    @pl.when(spot > 0)
    def _():
        for lane in range(groups):
            decay[lane, rows : rows + 8, :] = decay[lane, 0:8, :]

    keep = jnp.broadcast_to(mask_ref[:, 0:1], (rows, chans)) > 0.5
    gap = CGAIN * rate_ref[...] * softer_ref[...]
    step = jnp.where(keep, jnp.exp(-gap), 0.0)
    put_lanes(decay, step, rows)
    put_lanes(value, up_ref[...], rows)
    sweep(decay, value, inner, product, grad_ref, run_ref, carry, True, 1)
    head_ref[...] = jnp.broadcast_to(step[0:1, :] * carry[0:1, :], (8, chans))


def recur_adjoint(rate, up, masks, softer):
    rows, chans = rate.shape
    count = rows // TILE
    wide = jax.ShapeDtypeStruct((rows, chans), F32)
    return pl.pallas_call(
        adjoint_kernel,
        grid=(count,),
        out_shape=(wide, wide, jax.ShapeDtypeStruct((8, chans), F32)),
        in_specs=[
            tile_spec(chans, count),
            tile_spec(chans, count),
            tile_spec(masks.shape[1], count),
            fixed_spec((1, chans)),
        ],
        out_specs=[tile_spec(chans, count), tile_spec(chans, count), fixed_spec((8, chans))],
        scratch_shapes=[
            pltpu.VMEM((chans // LANES, TILE + 8, LANES), F32),
            pltpu.VMEM((chans // LANES, TILE, LANES), F32),
            pltpu.VMEM((chans // LANES, TILE, LANES), F32),
            pltpu.VMEM((chans // LANES, TILE, LANES), F32),
            pltpu.VMEM((16, chans), F32),
        ],
        cost_estimate=pl.CostEstimate(
            flops=8 * rows * chans, bytes_accessed=16 * rows * chans, transcendentals=rows * chans
        ),
        name="recur_adjoint",
    )(rate, up, masks, softer)


def backward_kernel(
    grad_ref, run_ref, enter_ref, rate_ref, entry_ref, conv_ref, state_ref, mask_ref,
    branch_ref, halo_ref, taps_ref, gates_ref, softer_ref,
    back_ref, tail_ref, head_ref, gate_grad_ref, sums_ref,
    shifts, edge,
):
    rows, chans = conv_ref.shape
    width = taps_ref.shape[0]
    spot = pl.program_id(0)
    last = pl.num_programs(0) - 1

    @pl.when(spot == 0)
    def _():
        for shift in range(1, width):
            shifts[shift - 1, rows : rows + 8, :] = jnp.zeros((8, chans), F32)
        gate_grad_ref[...] = jnp.zeros_like(gate_grad_ref)
        sums_ref[...] = jnp.zeros_like(sums_ref)

    @pl.when(spot > 0)
    def _():
        for shift in range(1, width):
            shifts[shift - 1, rows : rows + 8, :] = shifts[shift - 1, 0:8, :]

    keep = jnp.broadcast_to(mask_ref[:, 0:1], (rows, chans)) > 0.5
    softer = softer_ref[...]
    rate = rate_ref[...]
    entry = entry_ref[...]
    conv = conv_ref[...].astype(F32)
    grad = grad_ref[...] + run_ref[...] * enter_ref[0:1, :]
    step, square = decay_parts(rate, softer, keep)
    inverse = lax.rsqrt(square)
    mult = square * inverse
    driven = entry * conv
    carried = state_ref[...] - mult * driven
    d_log = jnp.where(keep, grad * (carried - driven * step * step * inverse), 0.0)
    d_rate = (-CGAIN * softer * d_log * rate * (1.0 - rate)).astype(BF16)
    lifted = grad * mult * entry
    d_entry = (lifted * conv * (1.0 - entry)).astype(BF16)
    both = jnp.concatenate([d_rate, d_entry], axis=1)
    d_conv = lifted + lax.dot_general(
        both, gates_ref[...], (((1,), (1,)), ((), ())), preferred_element_type=F32
    )
    gate_grad_ref[...] += lax.dot_general(
        conv_ref[...], both, (((0,), (0,)), ((), ())), preferred_element_type=F32
    )

    def add_row(row, block):
        sums_ref[row : row + 1, :] += jnp.sum(block, axis=0, keepdims=True)

    branch = branch_ref[...].astype(F32)
    add_row(0, d_log * rate)
    add_row(1, d_rate.astype(F32))
    add_row(2, d_entry.astype(F32))
    add_row(3, d_conv)
    add_row(4, d_conv * branch)
    back = taps_ref[0:1, :] * d_conv
    for shift in range(1, width):
        shifts[shift - 1, 0:rows, :] = d_conv * mask_ref[:, shift : shift + 1]
        moved = shifts[shift - 1, shift : shift + rows, :]
        add_row(4 + shift, moved * branch)
        back = back + taps_ref[shift : shift + 1, :] * moved
    back_ref[...] = back.astype(BF16)

    @pl.when(spot == 0)
    def _():
        tail_ref[...] = back[rows - 8 :, :]

    @pl.when(spot == last)
    def _():
        halo = halo_ref[...].astype(F32)
        head = jnp.zeros((8, chans), F32)
        edge[0:8, :] = head
        for shift in range(1, width):
            edge[8:16, :] = shifts[shift - 1, 0:8, :]
            moved = edge[shift : shift + 8, :]
            add_row(4 + shift, moved * halo)
            head = head + taps_ref[shift : shift + 1, :] * moved
        head_ref[...] = head


def recur_backward(grad, run, enter, rate, entry, conv, state, masks, branch, halo, taps, gates, softer):
    rows, chans = rate.shape
    count = rows // TILE
    edge = jax.ShapeDtypeStruct((8, chans), F32)
    wide = tile_spec(chans, count)
    return pl.pallas_call(
        backward_kernel,
        grid=(count,),
        out_shape=(
            jax.ShapeDtypeStruct((rows, chans), BF16),
            edge,
            edge,
            jax.ShapeDtypeStruct((chans, 2 * chans), F32),
            jax.ShapeDtypeStruct((16, chans), F32),
        ),
        in_specs=[
            wide, wide, fixed_spec((1, chans)), wide, wide, wide, wide,
            tile_spec(masks.shape[1], count),
            wide,
            fixed_spec((8, chans)),
            fixed_spec(taps.shape),
            fixed_spec(gates.shape),
            fixed_spec((1, chans)),
        ],
        out_specs=[
            wide,
            fixed_spec((8, chans)),
            fixed_spec((8, chans)),
            fixed_spec((chans, 2 * chans)),
            fixed_spec((16, chans)),
        ],
        scratch_shapes=[
            pltpu.VMEM((taps.shape[0] - 1, TILE + 8, chans), F32),
            pltpu.VMEM((16, chans), F32),
        ],
        cost_estimate=pl.CostEstimate(
            flops=8 * rows * chans * chans, bytes_accessed=28 * rows * chans, transcendentals=2 * rows * chans
        ),
        name="recur_backward",
    )(grad, run, enter, rate, entry, conv, state, masks, branch, halo, taps, gates, softer)


def spread_blocks(blocks):
    count, size = blocks.shape[0], blocks.shape[1]
    rows = [
        jnp.pad(blocks[i], ((0, 0), (i * size, (count - 1 - i) * size))) for i in range(count)
    ]
    return jnp.concatenate(rows, axis=0)


def shards(
    tokens,
    segments,
    cotangent,
    w_recur,
    w_gelu,
    w_merge,
    w_gate,
    w_up,
    w_down,
    norm_mix,
    norm_feed,
    conv_taps,
    conv_bias,
    rate_gate,
    entry_gate,
    rate_bias,
    entry_bias,
    decay_logit,
):
    piece = tokens.shape[0]
    width = conv_taps.shape[0]
    edge = width - 1
    heads, block = rate_gate.shape[0], rate_gate.shape[1]
    chans = conv_taps.shape[1]
    features = tokens.shape[1]
    feat_local = features // lax.axis_size("tp")
    feat_start = lax.axis_index("tp") * feat_local

    whole_recur = gather_rows(w_recur)
    whole_gelu = gather_rows(w_gelu)
    gains = lax.all_gather(jnp.stack([norm_mix, norm_feed]), "fsdp", axis=1, tiled=True).astype(F32)
    gain_one, gain_two = gains[0:1], gains[1:2]
    whole_merge = gather_rows(w_merge.T)
    whole_gate = gather_rows(w_gate)
    whole_up = gather_rows(w_up)
    whole_down = gather_rows(w_down.T)

    padded_ids = jnp.concatenate([jnp.full((edge,), -1, jnp.int32), segments])
    local_ids = lax.dynamic_slice_in_dim(padded_ids, lax.axis_index("ctx") * piece, piece + edge)
    own_ids = local_ids[edge:]
    masks = jnp.stack(
        [(local_ids[edge - max(shift, 1) : edge - max(shift, 1) + piece] == own_ids) for shift in range(width)],
        axis=1,
    ).astype(F32)
    taps = conv_taps.astype(F32)
    gates = jnp.concatenate([spread_blocks(rate_gate), spread_blocks(entry_gate)], axis=1)
    gate_bias = jnp.concatenate([rate_bias, entry_bias]).astype(F32)[None, :]
    softer = jax.nn.softplus(-decay_logit)[None, :]

    inputs = tokens.astype(F32)
    scale_one = rms_scale(inputs)
    normed = (inputs * scale_one * gain_one).astype(BF16)
    branch = jnp.dot(normed, whole_recur, preferred_element_type=F32).astype(BF16)
    halo = shifted(branch[piece - 8 :], "ctx", 1)
    pre_gelu = jnp.dot(normed, whole_gelu, preferred_element_type=F32)
    conv, rate, entry, local_state, run = recur_forward(
        branch, halo, masks, taps, conv_bias.astype(F32)[None, :], gates, gate_bias, softer
    )
    state_in = shifted(local_state[piece - 8 :], "ctx", 1)[7:8]
    states = local_state + run * state_in
    gelu_out, gelu_slope = gelu_pair(pre_gelu)
    gated = (states * gelu_out).astype(BF16)
    part_merge = lax.dot_general(gated, whole_merge, (((1,), (1,)), ((), ())), preferred_element_type=F32)
    merged = lax.psum(part_merge.astype(BF16), "tp").astype(F32)

    d_hidden = lax.dot_general(cotangent, whole_down, (((1,), (0,)), ((), ())), preferred_element_type=F32)
    resid = inputs + merged
    scale_two = rms_scale(resid)
    normed_two = (resid * scale_two * gain_two).astype(BF16)
    gate_pre = jnp.dot(normed_two, whole_gate, preferred_element_type=F32)
    up_vals = jnp.dot(normed_two, whole_up, preferred_element_type=F32)
    gate_act, gate_slope = gelu_pair(gate_pre)
    hidden = (gate_act * up_vals).astype(BF16)
    d_gate = (d_hidden * up_vals * gate_slope).astype(BF16)
    d_up = (d_hidden * gate_act).astype(BF16)
    part_two = lax.dot_general(
        d_gate, whole_gate, (((1,), (1,)), ((), ())), preferred_element_type=F32
    ) + lax.dot_general(d_up, whole_up, (((1,), (1,)), ((), ())), preferred_element_type=F32)
    d_normed_two = lax.psum(part_two.astype(BF16), "tp").astype(F32)
    feed = lax.psum_scatter(
        lax.dot_general(
            hidden, whole_down, (((1,), (1,)), ((), ())), preferred_element_type=F32
        ).astype(BF16),
        "tp",
        scatter_dimension=1,
        tiled=True,
    ).astype(F32)
    output = (lax.dynamic_slice_in_dim(resid, feat_start, feat_local, 1) + feed).astype(BF16)

    rows_to_rows = (((0,), (0,)), ((), ()))
    grad_down = lax.dot_general(cotangent, hidden, rows_to_rows, preferred_element_type=F32)
    grad_gate = lax.dot_general(normed_two, d_gate, rows_to_rows, preferred_element_type=F32)
    grad_up = lax.dot_general(normed_two, d_up, rows_to_rows, preferred_element_type=F32)
    shard_down = scatter_rows(grad_down).T
    shard_gate = scatter_rows(grad_gate)
    shard_up = scatter_rows(grad_up)

    grad_feed = jnp.sum(d_normed_two * resid * scale_two, axis=0)
    weighted = d_normed_two * gain_two
    d_resid = (
        cotangent.astype(F32)
        + scale_two * weighted
        - resid * scale_two**3 * jnp.mean(resid * weighted, axis=-1, keepdims=True)
    )
    d_merge_in = d_resid.astype(BF16)
    grad_merge = lax.dot_general(d_merge_in, gated, rows_to_rows, preferred_element_type=F32)
    shard_merge = scatter_rows(grad_merge).T
    d_gated = jnp.dot(d_merge_in, whole_merge, preferred_element_type=F32)
    d_states = d_gated * gelu_out
    d_gelu_pre = (d_gated * states * gelu_slope).astype(BF16)
    local_grad, grad_run, first = recur_adjoint(rate, d_states, masks, softer)
    grad_in = shifted(first, "ctx", -1)[0:1]
    back, tail, head, gate_grads, sums = recur_backward(
        local_grad, grad_run, grad_in, rate, entry, conv, states, masks, branch, halo, taps, gates, softer
    )
    returned = shifted(head, "ctx", -1)
    d_branch = lax.dynamic_update_slice_in_dim(back, (tail + returned).astype(BF16), piece - 8, 0)

    part_one = lax.dot_general(
        d_gelu_pre, whole_gelu, (((1,), (1,)), ((), ())), preferred_element_type=F32
    ) + lax.dot_general(d_branch, whole_recur, (((1,), (1,)), ((), ())), preferred_element_type=F32)
    stat_one = jnp.sum(part_one * inputs * gain_one, axis=-1)
    grad_mix = jnp.sum(part_one * inputs * scale_one, axis=0)
    d_normed = lax.psum_scatter(
        part_one.astype(BF16), "tp", scatter_dimension=1, tiled=True
    ).astype(F32)
    stat_one = lax.psum(stat_one, "tp")[:, None] / features
    grad_recur = lax.dot_general(normed, d_branch, rows_to_rows, preferred_element_type=F32)
    grad_gelu = lax.dot_general(normed, d_gelu_pre, rows_to_rows, preferred_element_type=F32)
    shard_recur = scatter_rows(grad_recur)
    shard_gelu = scatter_rows(grad_gelu)

    def own(block):
        return lax.dynamic_slice_in_dim(block, feat_start, feat_local, 1)

    own_inputs = own(inputs)
    grad_tokens = (
        own(d_resid)
        + scale_one * d_normed * own(gain_one)
        - own_inputs * scale_one**3 * stat_one
    ).astype(BF16)

    both_norms = lax.psum(
        jnp.stack([grad_mix, grad_feed / lax.axis_size("tp")]), ("fsdp", "ctx", "tp")
    )
    norm_local = norm_mix.shape[0]
    own_norms = lax.dynamic_slice_in_dim(both_norms, lax.axis_index("fsdp") * norm_local, norm_local, 1)

    diagonal = [
        gate_grads[i * block : (i + 1) * block, part * chans + i * block : part * chans + (i + 1) * block]
        for part in range(2)
        for i in range(heads)
    ]
    gate_sums = lax.psum(jnp.stack(diagonal).astype(BF16), ("fsdp", "ctx")).astype(F32)
    row_sums = lax.psum(sums, ("fsdp", "ctx"))
    return (
        output,
        grad_tokens,
        shard_recur,
        shard_gelu,
        shard_merge,
        shard_gate,
        shard_up,
        shard_down,
        own_norms[0],
        own_norms[1],
        row_sums[4 : 4 + width],
        row_sums[3],
        gate_sums[:heads],
        gate_sums[heads:],
        row_sums[1],
        row_sums[2],
        CGAIN * row_sums[0] * jax.nn.sigmoid(-decay_logit),
    )


def solution(mesh):
    placed = (
        P(("fsdp", "ctx"), None),
        P("fsdp"),
        P(("fsdp", "ctx"), None),
        P("fsdp", "tp"),
        P("fsdp", "tp"),
        P("tp", "fsdp"),
        P("fsdp", "tp"),
        P("fsdp", "tp"),
        P("tp", "fsdp"),
        P("fsdp"),
        P("fsdp"),
        P(None, "tp"),
        P("tp"),
        P("tp", None, None),
        P("tp", None, None),
        P("tp"),
        P("tp"),
        P("tp"),
    )
    return jax.shard_map(
        shards,
        mesh=mesh,
        in_specs=placed,
        out_specs=(
            P(("fsdp", "ctx"), "tp"),
            P(("fsdp", "ctx"), "tp"),
            P("fsdp", "tp"),
            P("fsdp", "tp"),
            P("tp", "fsdp"),
            P("fsdp", "tp"),
            P("fsdp", "tp"),
            P("tp", "fsdp"),
            P("fsdp"),
            P("fsdp"),
            P(None, "tp"),
            P("tp"),
            P("tp", None, None),
            P("tp", None, None),
            P("tp"),
            P("tp"),
            P("tp"),
        ),
        check_vma=False,
    )
```

time: 2120 us -> 1160 us (0.55)
  waiting for transfers between devices: 1050 us -> 609 us
  local copies, waits for them, and re-layouts: 551 us -> 141 us
  other arithmetic: 222 us -> 101 us
  Pallas kernels: 0 us -> 41 us
  matrix products: 193 us -> 153 us
  blocking collectives: 60.2 us -> 81.6 us
    slice x144 -> x8, local copies, waits for them, and re-layouts: 331 us -> 4.85 us  [the longest x1 2.25 us: shards(): gate_sums[heads:]]
    psum x5 -> x3, waiting for transfers between devices: 568 us -> 311 us  [the longest x1 157 us: shards(): merged = lax.psum(part_merge.astype(BF16), 'tp').astype(F32)]
    pad x72 -> x0, local copies, waits for them, and re-layouts: 155 us -> none  [the longest x36 77.8 us: shards(): lax.associative_scan(combine, (following, d_states), reverse=True)]
    reduce_scatter x7 -> x8, waiting for transfers between devices: 270 us -> 132 us  [the longest x6 69.1 us: scatter_rows(): lax.psum_scatter(pair.reshape(-1, grad.shape[1]), 'fsdp', scatter_dimensi...]
    add x58 -> x0, other arithmetic: 73.7 us -> none  [the longest x20 25.9 us: shards(): lax.associative_scan(combine, (following, d_states), reverse=True)]
    all_gather x6, waiting for transfers between devices: 207 us -> 148 us  [gather_rows(): mine = lax.all_gather(mine, 'fsdp', axis=0)]
    psum x2 -> x3, blocking collectives: 25.4 us -> 73.5 us  [the longest x1 39 us: shards(): lax.psum(jnp.stack([grad_mix, grad_feed / lax.axis_size('tp')]), ('fsdp',...]
    dynamic_slice x1 -> x10, local copies, waits for them, and re-layouts: 0.03 us -> 43.6 us  [the longest x2 25.7 us: scatter_rows(): mine = lax.dynamic_index_in_dim(halves, core, 1, False)]
  transfers between devices with their start and end apart: 20 -> 39, of which waited for: 15 -> 15; matrix products, arithmetic and copies ran while one was open for 33% -> 26% of each run, Pallas kernels for 0% -> 4%
where the time goes in v1:
time: 1160 us; the launch traced here: 1150 us
  waiting for transfers between devices  609 us (52%)
  matrix products  153 us (13%)
  local copies, waits for them, and re-layouts  141 us (12%)
  other arithmetic  101 us (9%)
  blocking collectives  81.6 us (7%)
  Pallas kernels  41 us (4%)
  between operations  15.3 us (1%)
  starting transfers between devices  12.9 us (1%)
    psum x1, waiting for transfers between devices, shards(): merged = lax.psum(part_merge.astype(BF16), 'tp').astype(F32)  157 us
    psum x1, waiting for transfers between devices, shards(): d_normed_two = lax.psum(part_two.astype(BF16), 'tp').astype(F32)  154 us
    all_gather x6, waiting for transfers between devices, gather_rows(): mine = lax.all_gather(mine, 'fsdp', axis=0)  148 us
    reduce_scatter x6, waiting for transfers between devices, scatter_rows(): lax.psum_scatter(pair.reshape(-1, grad.shape[1]), 'fsdp', scatter_dimensi...  69.1 us
    reduce_scatter x1, waiting for transfers between devices, shards(): lax.psum_scatter(part_one.astype(BF16), 'tp', scatter_dimension=1, tiled=...  62.8 us
    unnamed x138, local copies, waits for them, and re-layouts  42.5 us
    psum x1, blocking collectives, shards(): lax.psum(jnp.stack([grad_mix, grad_feed / lax.axis_size('tp')]), ('fsdp',...  39 us
    dynamic_slice x2, local copies, waits for them, and re-layouts, scatter_rows(): mine = lax.dynamic_index_in_dim(halves, core, 1, False)  25.7 us
  transfers between devices with their start and end apart: 39, of which 15 were waited for; matrix products, arithmetic and copies ran while one was open for 26% of the time, Pallas kernels for 4%

profile of v1, /device:TPU:0, one launch (start us, length us, event | category | flops | bytes accessed | tf_op | source)
XLA Modules:
  0.0 1154.4 jit_solution(1006709520142682619)
XLA Ops:
  25.7 16.2 %all-gather.13.cloned.1.call-done = bf16[1024,640]{1,0:T(8,128)(2,1)} async-done(((bf16[256,640]{1,0:T(8,128)(2,1)}), bf16[1024,640]{1,0:T(8,128)(2,1)}) %all-gather.13.cloned.1.call-update) | async-done | bytes 1310736 | tf_op jit(solution)/shard_map/all_gather | solution.py:33
  54.0 19.0 %all-gather.15.cloned.1.call-done = bf16[1024,640]{1,0:T(8,128)(2,1)} async-done(((bf16[256,640]{1,0:T(8,128)(2,1)}), bf16[1024,640]{1,0:T(8,128)(2,1)}) %all-gather.15.cloned.1.call-update) | async-done | bytes 1310736 | tf_op jit(solution)/shard_map/all_gather | solution.py:33
  75.9 28.0 %all-gather.17.cloned.1.call-done = bf16[1024,640]{0,1:T(8,128)(2,1)} async-done(((bf16[256,640]{0,1:T(8,128)(2,1)}), bf16[1024,640]{0,1:T(8,128)(2,1)}) %all-gather.17.cloned.1.call-update) | async-done | bytes 1310736 | tf_op jit(solution)/shard_map/all_gather | solution.py:33
  124.9 13.4 %recur_forward.1 = (bf16[1024,640]{1,0:T(8,128)(2,1)}, f32[1024,640]{1,0:T(8,128)}, f32[1024,640]{1,0:T(8,128)}, f32[1024,640]{1,0:T(8,128)}, f32[1024,640]{1,0:T(8,128)}) custom-call(bf16[1024,640]{1,0:T(8,128)(2,1)} %copy-done.26, bf16[8,640]{1,0:T(8,128)(2,1)} %copy-done.47, f32[1024,4]{1,0:T(8,128)} %convert_element_type.192.mask_ref, ...), custom_call_target="tpu_custom_call" | custom-call | flops 1677721600 | bytes 15728640 | tf_op jit(solution)/shard_map/recur_forward/pallas_call | solution.py:176
  152.8 43.3 %all-gather.23.cloned.1.call-done = bf16[1024,1536]{0,1:T(8,128)(2,1)} async-done(((bf16[256,1536]{0,1:T(8,128)(2,1)}), bf16[1024,1536]{0,1:T(8,128)(2,1)}) %all-gather.23.cloned.1.call-update) | async-done | bytes 3145744 | tf_op jit(solution)/shard_map/all_gather | solution.py:33
  200.7 41.5 %all-gather.19.cloned.1.call-done = bf16[1024,1536]{1,0:T(8,128)(2,1)} async-done(((bf16[256,1536]{1,0:T(8,128)(2,1)}), bf16[1024,1536]{1,0:T(8,128)(2,1)}) %all-gather.19.cloned.1.call-update) | async-done | bytes 3145744 | tf_op jit(solution)/shard_map/all_gather | solution.py:33
  242.3 157.4 %all-reduce.13.cloned.1.call-done = bf16[1024,2048]{1,0:T(8,128)(2,1)} async-done(((bf16[1024,2048]{1,0:T(8,128)(2,1)}), bf16[1024,2048]{1,0:T(8,128)(2,1)}) %all-reduce.13.cloned.1.call-update) | async-done | bytes 4194320 | tf_op jit(solution)/shard_map/psum | solution.py:457
  423.0 10.6 fusion.90
  445.5 16.2 %fusion.13 = (bf16[1024,1536]{1,0:T(8,128)(2,1)}, bf16[1024,1536]{1,0:T(8,128)(2,1)S(1)}, bf16[1024,1536]{1,0:T(8,128)(2,1)}) fusion(f32[1024,1536]{1,0:T(8,128)} %fusion.90, f32[1536,1024]{0,1:T(8,128)} %fusion.95, bf16[1024,2048]{1,0:T(8,128)(2,1)} %multiply_convert_fusion, bf16[2048,1536]{1,0:T(8,128)(2,1)S(1)} %bitcast.207), kind=kOutput, calls=%fused_computation.27 | convolution fusion | flops 6481772544 | bytes 32505856 | tf_op jit(solution)/shard_map/dot_general | solution.py:463
  470.8 10.5 add_convert_fusion
  481.4 154.1 %all-reduce.15.cloned.1.call-done = bf16[1024,2048]{1,0:T(8,128)(2,1)} async-done(((bf16[1024,2048]{1,0:T(8,128)(2,1)}), bf16[1024,2048]{1,0:T(8,128)(2,1)}) %all-reduce.15.cloned.1.call-update) | async-done | bytes 4194320 | tf_op jit(solution)/shard_map/psum | solution.py:472
  651.0 11.4 fusion.70
  698.8 18.8 %recur_backward.1 = (bf16[1024,640]{1,0:T(8,128)(2,1)}, f32[8,640]{1,0:T(8,128)}, f32[8,640]{1,0:T(8,128)}, f32[640,1280]{1,0:T(8,128)}, f32[16,640]{1,0:T(8,128)}) custom-call(f32[1024,640]{1,0:T(8,128)} %get-tuple-element.33.grad_ref, f32[1024,640]{1,0:T(8,128)} %get-tuple-element.34.run_ref, f32[1,640]{1,0:T(1,128)} %slice.153.enter_ref, ...), custom_call_target="tpu_custom_call" | custom-call | flops 3355443200 | bytes 18350080 | tf_op jit(solution)/shard_map/recur_backward/pallas_call | solution.py:348
  738.4 11.1 convolution_convert_fusion
  772.8 12.4 %convolution_bitcast_fusion = f32[2048,1536]{0,1:T(8,128)} fusion(bf16[1024,1536]{1,0:T(8,128)(2,1)} %get-tuple-element.106, bf16[1024,2048]{1,0:T(8,128)(2,1)} %param.20), kind=kOutput, calls=%fused_computation.6 | convolution fusion | flops 6442450944 | bytes 19922944 | tf_op jit(solution)/shard_map/dot_general | solution.py:484
  785.2 17.0 %reshape.184 = f32[4,2,256,1536]{2,1,0,3:T(2,128)} reshape(f32[2048,1536]{0,1:T(8,128)} %convolution_bitcast_fusion) | data formatting | bytes 25165824 | tf_op jit(solution)/shard_map/reshape | solution.py:43
  802.2 9.8 constant_dynamic-slice_fusion
  812.0 15.3 %copy.110 = bf16[4,1,256,1536]{3,2,0,1:T(8,128)(2,1)} copy(bf16[4,1,256,1536]{2,1,0,3:T(2,128)(2,1)} %constant_dynamic-slice_fusion) | data formatting | bytes 6291456
  837.3 16.0 %copy.97 = f32[4,1,256,1536]{3,2,0,1:T(8,128)} copy(f32[4,1,256,1536]{2,1,0,3:T(1,128)} %constant_dynamic-slice_fusion.1) | data formatting | bytes 12582912 | tf_op jit(solution)/shard_map/jit(dynamic_index_in_dim)/dynamic_slice | solution.py:44
  906.8 25.2 %psum.46 = f32[16,640]{1,0:T(8,128)S(1)} all-reduce(f32[16,640]{1,0:T(8,128)S(1)} %copy-done.41), channel_id=1, replica_groups=mesh['fsdp'=4,'ctx'=2,'tp'=4] {'fsdp','ctx'}, use_global_device_ids=true, to_apply=%region_18.19 | all-reduce | flops 10240 | bytes 81920 | tf_op jit(solution)/shard_map/psum | solution.py:548
  943.2 39.0 %psum.45 = f32[2,2048]{1,0:T(2,128)S(1)} all-reduce(f32[2,2048]{1,0:T(2,128)S(1)} %pad_maximum_fusion.6), channel_id=1, replica_groups=mesh['fsdp'=4,'ctx'=2,'tp'=4] {'fsdp','ctx','tp'}, use_global_device_ids=true, to_apply=%region_17.18 | all-reduce | flops 4096 | bytes 32768 | tf_op jit(solution)/shard_map/psum | solution.py:536
  995.4 21.7 %reduce-scatter.23.cloned.1.call-done = bf16[256,1536]{0,1:T(8,128)(2,1)} async-done(((bf16[1024,1536]{0,1:T(8,128)(2,1)}), bf16[256,1536]{0,1:T(8,128)(2,1)}) %reduce-scatter.23.cloned.1.call-update) | async-done | bytes 786448 | tf_op jit(solution)/shard_map/reduce_scatter | solution.py:47
  1017.1 47.3 %reduce-scatter.19.cloned.1.call-done = bf16[256,1536]{0,1:T(8,128)(2,1)} async-done(((bf16[1024,1536]{0,1:T(8,128)(2,1)}), bf16[256,1536]{0,1:T(8,128)(2,1)}) %reduce-scatter.19.cloned.1.call-update) | async-done | bytes 786448 | tf_op jit(solution)/shard_map/reduce_scatter | solution.py:47
  1080.7 62.8 %reduce-scatter.11.cloned.1.call-done = bf16[1024,512]{1,0:T(8,128)(2,1)} async-done(((bf16[1024,2048]{1,0:T(8,128)(2,1)}), bf16[1024,512]{1,0:T(8,128)(2,1)}) %reduce-scatter.11.cloned.1.call-update) | async-done | bytes 1048592 | tf_op jit(solution)/shard_map/reduce_scatter | solution.py:517
  (340 shorter events, 321.0 us)
Async XLA Ops:
  7.2 34.6 %all-gather.13.cloned.1.call-start = ((), (), s32[]{:S(2)}) async-start(), calls=%async_computation.19 | async-start | bytes 1638400 | tf_op jit(solution)/shard_map/all_gather | solution.py:33
  9.2 63.8 %all-gather.15.cloned.1.call-start = ((), (), s32[]{:S(2)}) async-start(), calls=%async_computation.20 | async-start | bytes 1638400 | tf_op jit(solution)/shard_map/all_gather | solution.py:33
  11.0 93.0 %all-gather.17.cloned.1.call-start = ((), (), s32[]{:S(2)}) async-start(), calls=%async_computation.21 | async-start | bytes 1638400 | tf_op jit(solution)/shard_map/all_gather | solution.py:33
  12.8 139.9 %all-gather.21.cloned.1.call-start = ((), (), s32[]{:S(2)}) async-start(), calls=%async_computation.23 | async-start | bytes 3932160 | tf_op jit(solution)/shard_map/all_gather | solution.py:33
  13.8 182.3 %all-gather.23.cloned.1.call-start = ((), (), s32[]{:S(2)}) async-start(), calls=%async_computation.24 | async-start | bytes 3932160 | tf_op jit(solution)/shard_map/all_gather | solution.py:33
  14.9 227.4 %all-gather.19.cloned.1.call-start = ((), (), s32[]{:S(2)}) async-start(), calls=%async_computation.22 | async-start | bytes 3932160 | tf_op jit(solution)/shard_map/all_gather | solution.py:33
  16.4 383.2 %all-reduce.13.cloned.1.call-start = ((), (), s32[]{:S(2)}) async-start(), calls=%async_computation.8 | async-start | bytes 8388608 | tf_op jit(solution)/shard_map/psum | solution.py:457
  41.9 63.9 %collective-permute-start = (bf16[4,256,640]{2,1,0:T(8,128)(2,1)}, bf16[4,256,640]{2,1,0:T(8,128)(2,1)}, u32[]{:S(2)}, u32[]{:S(2)}) collective-permute-start(bf16[4,256,640]{2,1,0:T(8,128)(2,1)} %bitcast.233), channel_id=1, source_target_pairs={{0,4},{4,0},{1,5},{5,1},{2,6},{6,2},{3,7},{7,3},{8,12},{12,8},{9,1... | collective-permute-start | bytes 3932168 | tf_op jit(solution)/shard_map/ppermute | solution.py:20
  73.0 44.0 %collective-permute-start.3 = (bf16[4,256,640]{2,1,0:T(8,128)(2,1)}, bf16[4,256,640]{2,1,0:T(8,128)(2,1)}, u32[]{:S(2)}, u32[]{:S(2)}) collective-permute-start(bf16[4,256,640]{2,1,0:T(8,128)(2,1)} %bitcast.231), channel_id=1, source_target_pairs={{0,4},{4,0},{1,5},{5,1},{2,6},{6,2},{3,7},{7,3},{8,12},{12,8},{9,1... | collective-permute-start | bytes 3932168 | tf_op jit(solution)/shard_map/ppermute | solution.py:20
  152.4 483.0 %all-reduce.15.cloned.1.call-start = ((), (), s32[]{:S(2)}) async-start(), calls=%async_computation.10 | async-start | bytes 8388608 | tf_op jit(solution)/shard_map/psum | solution.py:472
  152.7 256.9 %collective-permute-start.6 = (bf16[4,256,1536]{2,1,0:T(8,128)(2,1)}, bf16[4,256,1536]{2,1,0:T(8,128)(2,1)}, u32[]{:S(2)}, u32[]{:S(2)}) collective-permute-start(bf16[4,256,1536]{2,1,0:T(8,128)(2,1)} %bitcast.216), channel_id=1, source_target_pairs={{0,4},{4,0},{1,5},{5,1},{2,6},{6,2},{3,7},{7,3},{8,12},{12,8},{9,1... | collective-permute-start | bytes 9437192 | tf_op jit(solution)/shard_map/ppermute | solution.py:20
  200.7 215.1 %collective-permute-start.7 = (bf16[4,256,1536]{2,1,0:T(8,128)(2,1)}, bf16[4,256,1536]{2,1,0:T(8,128)(2,1)}, u32[]{:S(2)}, u32[]{:S(2)}) collective-permute-start(bf16[4,256,1536]{2,1,0:T(8,128)(2,1)} %bitcast.192), channel_id=1, source_target_pairs={{0,4},{4,0},{1,5},{5,1},{2,6},{6,2},{3,7},{7,3},{8,12},{12,8},{9,1... | collective-permute-start | bytes 9437192 | tf_op jit(solution)/shard_map/ppermute | solution.py:20
  242.3 200.4 %collective-permute-start.5 = (bf16[4,256,1536]{2,1,0:T(8,128)(2,1)}, bf16[4,256,1536]{2,1,0:T(8,128)(2,1)}, u32[]{:S(2)}, u32[]{:S(2)}) collective-permute-start(bf16[4,256,1536]{2,1,0:T(8,128)(2,1)} %bitcast.214), channel_id=1, source_target_pairs={{0,4},{4,0},{1,5},{5,1},{2,6},{6,2},{3,7},{7,3},{8,12},{12,8},{9,1... | collective-permute-start | bytes 9437192 | tf_op jit(solution)/shard_map/ppermute | solution.py:20
  481.3 501.6 %reduce-scatter.15.cloned.1.call-start = ((), (), s32[]{:S(2)}) async-start(), calls=%async_computation.13 | async-start | bytes 1638400 | tf_op jit(solution)/shard_map/reduce_scatter | solution.py:47
  675.5 307.5 %all-reduce.17.cloned.1.call-start = ((), (), s32[]{:S(2)}) async-start(), calls=%async_computation.18 | async-start | bytes 1310720 | tf_op jit(solution)/shard_map/psum | solution.py:547
  722.5 262.7 %reduce-scatter.17.cloned.1.call-start = ((), (), s32[]{:S(2)}) async-start(), calls=%async_computation.14 | async-start | bytes 1638400 | tf_op jit(solution)/shard_map/reduce_scatter | solution.py:47
  726.1 259.6 %reduce-scatter.13.cloned.1.call-start = ((), (), s32[]{:S(2)}) async-start(), calls=%async_computation.12 | async-start | bytes 1638400 | tf_op jit(solution)/shard_map/reduce_scatter | solution.py:47
  738.0 247.9 %reduce-scatter.9.cloned.1.call-start = ((), (), s32[]{:S(2)}) async-start(), calls=%async_computation.9 | async-start | bytes 5242880 | tf_op jit(solution)/shard_map/reduce_scatter | solution.py:473
  749.6 241.2 %reduce-scatter.21.cloned.1.call-start = ((), (), s32[]{:S(2)}) async-start(), calls=%async_computation.16 | async-start | bytes 3932160 | tf_op jit(solution)/shard_map/reduce_scatter | solution.py:47
  772.6 244.5 %reduce-scatter.23.cloned.1.call-start = ((), (), s32[]{:S(2)}) async-start(), calls=%async_computation.17 | async-start | bytes 3932160 | tf_op jit(solution)/shard_map/reduce_scatter | solution.py:47
  864.4 200.1 %reduce-scatter.19.cloned.1.call-start = ((), (), s32[]{:S(2)}) async-start(), calls=%async_computation.15 | async-start | bytes 3932160 | tf_op jit(solution)/shard_map/reduce_scatter | solution.py:47
  887.5 256.0 %reduce-scatter.11.cloned.1.call-start = ((), (), s32[]{:S(2)}) async-start(), calls=%async_computation.11 | async-start | bytes 5242880 | tf_op jit(solution)/shard_map/reduce_scatter | solution.py:517
  990.7 73.7 %collective-permute-start.19 = (bf16[256,1536]{0,1:T(8,128)(2,1)}, bf16[256,1536]{0,1:T(8,128)(2,1)S(1)}, u32[]{:S(2)}, u32[]{:S(2)}) collective-permute-start(bf16[256,1536]{0,1:T(8,128)(2,1)} %reduce-scatter.21.cloned.1.call-done), channel_id=1, source_target_pairs={{0,4},{4,0},{1,5},{5,1},{2,6},{6,2},{3,7},{7,3},{8,12},{12,8},{9,1... | collective-permute-start | bytes 2359304 | tf_op jit(solution)/shard_map/ppermute | solution.py:20
  1017.1 60.2 %collective-permute-start.21 = (bf16[256,1536]{0,1:T(8,128)(2,1)}, bf16[256,1536]{0,1:T(8,128)(2,1)}, u32[]{:S(2)}, u32[]{:S(2)}) collective-permute-start(bf16[256,1536]{0,1:T(8,128)(2,1)} %reduce-scatter.23.cloned.1.call-done), channel_id=1, source_target_pairs={{0,4},{4,0},{1,5},{5,1},{2,6},{6,2},{3,7},{7,3},{8,12},{12,8},{9,1... | collective-permute-start | bytes 2359304 | tf_op jit(solution)/shard_map/ppermute | solution.py:20
  (78 other events, 741.5 us)
Sparse Core Ops, SparseCore 0:
  10.4 31.3 all-gather.12
  44.3 28.6 all-gather.14
  75.4 28.5 all-gather.16
  106.2 43.8 all-gather.20
  152.4 43.6 all-gather.22
  198.4 43.8 all-gather.18
  244.6 154.9 all-reduce.12
  481.4 153.9 all-reduce.14
  675.6 28.4 reduce-scatter.14
  722.6 54.8 all-reduce.16
  781.0 28.7 reduce-scatter.16
  813.2 29.4 reduce-scatter.12
  845.0 76.7 reduce-scatter.8
  924.7 44.9 reduce-scatter.20
  973.1 43.9 reduce-scatter.22
  1020.5 43.8 reduce-scatter.18
  1066.6 76.7 reduce-scatter.10

commit v2 on v1

--- a/solution.py
+++ b/solution.py
@@ -26,29 +26,460 @@
     return lax.ppermute(block, axis, route)
 
 
-def gather_rows(shard):
-    half = shard.shape[0] // 2
+def gather_halves(shard, dim):
+    half = shard.shape[dim] // 2
     core = lax.axis_index("ctx")
-    mine = lax.dynamic_slice_in_dim(shard, core * half, half, 0)
-    mine = lax.all_gather(mine, "fsdp", axis=0)
+    mine = lax.dynamic_slice_in_dim(shard, core * half, half, dim)
+    mine = lax.all_gather(mine, "fsdp", axis=dim)
     other = swap_cores(mine)
     first = jnp.where(core == 0, mine, other)
     second = jnp.where(core == 0, other, mine)
-    return jnp.stack([first, second], axis=1).reshape(-1, shard.shape[1])
-
-
-def scatter_rows(grad):
+    both = jnp.stack([first, second], axis=dim + 1)
+    return both.reshape(shard.shape[:dim] + (-1,) + shard.shape[dim + 1 :])
+
+
+def split_features(block):
     shards = lax.axis_size("fsdp")
     core = lax.axis_index("ctx")
-    halves = grad.reshape(shards, 2, grad.shape[0] // shards // 2, grad.shape[1])
-    mine = lax.dynamic_index_in_dim(halves, core, 1, False)
-    send = lax.dynamic_index_in_dim(halves, 1 - core, 1, False).astype(BF16)
-    pair = (mine + swap_cores(send).astype(F32)).astype(BF16)
-    total = lax.psum_scatter(pair.reshape(-1, grad.shape[1]), "fsdp", scatter_dimension=0, tiled=True)
+    parts = block.reshape(block.shape[0], shards, 2, -1)
+    return [
+        lax.dynamic_index_in_dim(parts, index, 2, False).reshape(block.shape[0], -1)
+        for index in (core, 1 - core)
+    ]
+
+
+def pair_sums(left, right, dim):
+    rows_to_rows = (((0,), (0,)), ((), ()))
+
+    def product(index):
+        pair = (left[index], right) if dim == 0 else (right, left[index])
+        return lax.dot_general(*pair, rows_to_rows, preferred_element_type=F32)
+
+    arrived = swap_cores(product(1).astype(BF16))
+    return (product(0) + arrived.astype(F32)).astype(BF16)
+
+
+def to_owners(mine, dim):
+    total = lax.psum_scatter(mine, "fsdp", scatter_dimension=dim, tiled=True)
     other = swap_cores(total)
+    core = lax.axis_index("ctx")
     first = jnp.where(core == 0, total, other)
     second = jnp.where(core == 0, other, total)
-    return jnp.concatenate([first, second], axis=0).astype(F32)
+    return jnp.concatenate([first, second], axis=dim).astype(F32)
+
+
+def after(value, *others):
+    return lax.optimization_barrier((value, *others))[0]
+
+
+class Square:
+    def __init__(self):
+        me = lax.axis_index("fsdp")
+        row, col = me // 2, me % 2
+        self.me = me
+        self.core = lax.axis_index("ctx")
+        self.near = (row * 2 + 1 - col, (1 - row) * 2 + col)
+        self.far = (1 - row) * 2 + 1 - col
+
+
+def remote(source, target, send, arrive, **device):
+    return pltpu.make_async_remote_copy(
+        source, target, send, arrive, device_id=device, device_id_type=pl.DeviceIdType.MESH
+    )
+
+
+class Gather:
+    def __init__(self, items, stages, send, arrive, local):
+        self.items, self.stages = items, stages
+        self.send, self.arrive, self.local = send, arrive, local
+        self.square = Square()
+
+    def piece(self, w, owner, low, size):
+        shard, whole, dim, offset = self.items[w]
+        low = pl.multiple_of(owner * shard.shape[dim] + low, 128)
+        if dim == 0:
+            return whole.at[pl.ds(low, size), pl.ds(offset, shard.shape[1])]
+        return whole.at[:, pl.ds(low, size)]
+
+    def copy(self, w, k):
+        shard, _, dim, _ = self.items[w]
+        square = self.square
+        half = shard.shape[dim] // 2
+        low = pl.multiple_of(square.core * half, 128)
+        first, second = square.near
+        if k < 2:
+            source = shard.at[pl.ds(low, half), :] if dim == 0 else shard.at[:, pl.ds(low, half)]
+            target = self.piece(w, square.me, low, half)
+            device = {"fsdp": square.near[k]}
+        elif k < 4:
+            source = target = self.piece(w, square.near[k - 2], low + (k - 2) * (half // 2), half // 2)
+            device = {"fsdp": square.near[3 - k]}
+        else:
+            source = target = self.piece(w, (first, second, square.far)[k - 4], low, half)
+            device = {"ctx": 1 - square.core}
+        return remote(source, target, self.send.at[w, k], self.arrive.at[w, k], **device)
+
+    def stage(self, w, out):
+        shard = self.items[w][0]
+        if out:
+            target = self.piece(w, self.square.me, 0, shard.shape[self.items[w][2]])
+            return pltpu.make_async_copy(self.stages[w], target, self.local.at[w, 1])
+        return pltpu.make_async_copy(shard, self.stages[w], self.local.at[w, 0])
+
+    def start(self, w):
+        self.copy(w, 0).start()
+        self.copy(w, 1).start()
+        self.stage(w, False).start()
+
+    def forward(self, w):
+        self.copy(w, 0).wait_recv()
+        self.copy(w, 2).start()
+        self.copy(w, 1).wait_recv()
+        self.copy(w, 3).start()
+        self.copy(w, 4).start()
+        self.copy(w, 5).start()
+        self.stage(w, False).wait()
+        self.stage(w, True).start()
+
+    def hand_over(self, w):
+        self.copy(w, 2).wait_recv()
+        self.copy(w, 3).wait_recv()
+        self.copy(w, 6).start()
+
+    def finish(self, w):
+        for k in (4, 5, 6):
+            self.copy(w, k).wait_recv()
+        for k in range(7):
+            self.copy(w, k).wait_send()
+        self.stage(w, True).wait()
+
+
+def greet(line, square):
+    barrier = pltpu.get_barrier_semaphore()
+
+    def call(**device):
+        pl.semaphore_signal(barrier, inc=1, device_id=device, device_id_type=pl.DeviceIdType.MESH)
+
+    peers = 0
+    if line:
+        count, me = lax.axis_size("tp"), lax.axis_index("tp")
+
+        @pl.when(me > 0)
+        def _():
+            call(tp=me - 1)
+
+        @pl.when(me < count - 1)
+        def _():
+            call(tp=me + 1)
+
+        peers = jnp.where((me > 0) & (me < count - 1), 2, 1)
+    if square:
+        place = Square()
+        call(fsdp=place.near[0])
+        call(fsdp=place.near[1])
+        call(fsdp=place.far)
+        call(ctx=1 - place.core)
+        peers = peers + 4
+    pl.semaphore_wait(barrier, peers)
+
+
+def line_sum(part, whole, inbox, sems, finish, between):
+    count, me = lax.axis_size("tp"), lax.axis_index("tp")
+    half = part.shape[0] // 2
+    chunks = inbox.shape[1]
+    rows = half // chunks
+    sum_send, sum_arrive, share_send, share_arrive = sems
+
+    def spot(side, c):
+        return pl.ds(pl.multiple_of(side * half + c * rows, rows), rows)
+
+    def place(side):
+        return count - 1 - me if side else me
+
+    def onward(side, c, source):
+        target = me - 1 if side else me + 1
+        return remote(source, inbox.at[side, c], sum_send.at[side, c], sum_arrive.at[side, c], tp=target)
+
+    def share(side, c):
+        target = me + 1 if side else me - 1
+        block = whole.at[spot(side, c), :]
+        return remote(block, block, share_send.at[side, c], share_arrive.at[side, c], tp=target)
+
+    for side in (0, 1):
+        @pl.when(place(side) == 0)
+        def _():
+            onward(side, 0, part.at[spot(side, 0), :]).start()
+
+    def step(t, carry):
+        for side in (0, 1):
+            here = place(side)
+            c = t - here
+
+            @pl.when((here == 0) & (t + 1 < chunks))
+            def _():
+                onward(side, t + 1, part.at[spot(side, t + 1), :]).start()
+
+            @pl.when((c >= 0) & (c < chunks) & (here > 0))
+            def _():
+                onward(side, c, inbox.at[side, c]).wait_recv()
+                total = (inbox[side, c].astype(F32) + part[spot(side, c), :].astype(F32)).astype(BF16)
+
+                @pl.when(here < count - 1)
+                def _():
+                    inbox[side, c] = total
+                    onward(side, c, inbox.at[side, c]).start()
+
+                @pl.when(here == count - 1)
+                def _():
+                    whole[spot(side, c), :] = total
+                    share(side, c).start()
+                    finish(spot(side, c))
+
+        for side in (0, 1):
+            here = place(side)
+            c = t - 2 * (count - 1) + here
+
+            @pl.when((c >= 0) & (c < chunks) & (here < count - 1))
+            def _():
+                share(side, c).wait_recv()
+
+                @pl.when(here > 0)
+                def _():
+                    share(side, c).start()
+
+                finish(spot(side, c))
+
+        between(t)
+        return carry
+
+    lax.fori_loop(0, chunks + 2 * (count - 1), step, 0)
+
+    def drain(c, carry):
+        for side in (0, 1):
+            here = place(side)
+
+            @pl.when(here < count - 1)
+            def _():
+                onward(side, c, inbox.at[side, c]).wait_send()
+
+            @pl.when(here > 0)
+            def _():
+                share(side, c).wait_send()
+
+        return carry
+
+    lax.fori_loop(0, chunks, drain, 0)
+
+
+def put_split(ref, rows, block):
+    core = lax.axis_index("ctx")
+    size = block.shape[1] // 8
+    for owner in range(4):
+        for index in range(2):
+            low = (2 * owner + index) * size
+            ref[(index + core) % 2, rows, owner * size : (owner + 1) * size] = block[:, low : low + size]
+
+
+CHUNK = 32
+
+
+def enter_kernel(
+    tokens, gain_shard, recur, gelu, merge,
+    normed, halves, gains, whole_in, whole_merge,
+    stage_recur, stage_gelu, stage_merge, send, arrive, local, gain_send, gain_arrive,
+):
+    square = Square()
+    greet(False, True)
+    width = gain_shard.shape[1]
+
+    def gain_copy(k, owner, target):
+        spot = gains.at[:, pl.ds(pl.multiple_of(owner * width, 128), width)]
+        return remote(gain_shard, spot, gain_send.at[k], gain_arrive.at[k], fsdp=target)
+
+    others = (*square.near, square.far)
+    for k, target in enumerate(others):
+        gain_copy(k, square.me, target).start()
+    gather = Gather(
+        [(recur, whole_in, 0, 0), (gelu, whole_in, 0, recur.shape[1]), (merge, whole_merge, 1, 0)],
+        (stage_recur, stage_gelu, stage_merge), send, arrive, local,
+    )
+    for w in range(3):
+        gather.start(w)
+    gains[:, pl.ds(pl.multiple_of(square.me * width, 128), width)] = gain_shard[...]
+    for k, owner in enumerate(others):
+        gain_copy(k, owner, owner).wait_recv()
+
+    def norm(t, carry):
+        rows = pl.ds(pl.multiple_of(t * CHUNK, CHUNK), CHUNK)
+        block = tokens[rows, :].astype(F32)
+        block = (block * rms_scale(block) * gains[0:1, :]).astype(BF16)
+        normed[rows, :] = block
+        put_split(halves, rows, block)
+        return carry
+
+    lax.fori_loop(0, tokens.shape[0] // CHUNK, norm, 0)
+    for w in range(3):
+        gather.forward(w)
+    for w in range(3):
+        gather.hand_over(w)
+    for w in range(3):
+        gather.finish(w)
+    for k, target in enumerate(others):
+        gain_copy(k, square.me, target).wait_send()
+
+
+ANY = pl.BlockSpec(memory_space=pl.ANY)
+NEAR = pl.BlockSpec(memory_space=pltpu.VMEM)
+
+
+def gather_scratch(shards):
+    count = len(shards)
+    dma = pltpu.SemaphoreType.DMA
+    return [pltpu.VMEM(w.shape, w.dtype) for w in shards] + [dma((count, 7)), dma((count, 7)), dma((count, 2))]
+
+
+def enter(tokens, gain_shard, recur, gelu, merge):
+    rows, features = tokens.shape
+    shape = jax.ShapeDtypeStruct
+    inner = recur.shape[1]
+    dma = pltpu.SemaphoreType.DMA
+    return pl.pallas_call(
+        enter_kernel,
+        out_shape=(
+            shape((rows, features), BF16),
+            shape((2, rows, features // 2), BF16),
+            shape((8, features), F32),
+            shape((features, 2 * inner), BF16),
+            shape((inner, features), BF16),
+        ),
+        in_specs=[NEAR, NEAR, ANY, ANY, ANY],
+        out_specs=[NEAR, NEAR, NEAR, ANY, ANY],
+        scratch_shapes=gather_scratch([recur, gelu, merge]) + [dma((3,)), dma((3,))],
+        compiler_params=pltpu.CompilerParams(collective_id=1, has_side_effects=True),
+        name="enter",
+    )(tokens, gain_shard, recur, gelu, merge)
+
+
+def line_scratch(rows, features):
+    chunks = rows // 2 // CHUNK
+    dma = pltpu.SemaphoreType.DMA((2, chunks))
+    return [pltpu.VMEM((2, chunks, CHUNK, features), BF16), dma, dma, dma, dma]
+
+
+def middle_kernel(gathers, part, tokens, gains, *refs):
+    if gathers:
+        gate, up, down, merged, normed, halves, whole_in, whole_down = refs[:8]
+        inbox, *rest = refs[8:]
+        sems, (stage_gate, stage_up, stage_down, send, arrive, local) = rest[:4], rest[4:]
+        gather = Gather(
+            [(gate, whole_in, 0, 0), (up, whole_in, 0, gate.shape[1]), (down, whole_down, 1, 0)],
+            (stage_gate, stage_up, stage_down), send, arrive, local,
+        )
+        greet(True, True)
+        for w in range(3):
+            gather.start(w)
+    else:
+        merged, normed, inbox, *sems = refs
+        greet(True, False)
+
+    def finish(rows):
+        block = tokens[rows, :].astype(F32) + merged[rows, :].astype(F32)
+        block = (block * rms_scale(block) * gains[1:2, :]).astype(BF16)
+        normed[rows, :] = block
+        if gathers:
+            put_split(halves, rows, block)
+
+    def between(t):
+        if gathers:
+            for w in range(3):
+                @pl.when(t == 5 + 4 * w)
+                def _():
+                    gather.forward(w)
+
+                @pl.when(t == 17 + w)
+                def _():
+                    gather.hand_over(w)
+
+    line_sum(part, merged, inbox, sems, finish, between)
+    if gathers:
+        for w in range(3):
+            gather.finish(w)
+
+
+def middle(part, tokens, gains, shards):
+    rows, features = tokens.shape
+    shape = jax.ShapeDtypeStruct
+    whole = shape((rows, features), BF16)
+    outs, specs = [whole, whole], [NEAR, NEAR]
+    scratch = line_scratch(rows, features)
+    if shards:
+        gate, up, down = shards
+        outs += [
+            shape((2, rows, features // 2), BF16),
+            shape((features, 2 * gate.shape[1]), BF16),
+            shape((down.shape[0], features), BF16),
+        ]
+        specs += [NEAR, ANY, ANY]
+        scratch += gather_scratch(shards)
+    return pl.pallas_call(
+        lambda *refs: middle_kernel(bool(shards), *refs),
+        out_shape=tuple(outs),
+        in_specs=[NEAR, NEAR, NEAR] + [ANY] * len(shards),
+        out_specs=specs,
+        scratch_shapes=scratch,
+        compiler_params=pltpu.CompilerParams(collective_id=2, has_side_effects=True),
+        name="middle",
+    )(part, tokens, gains, *shards)
+
+
+def turn_kernel(split, part, tokens, merged, upstream, gains, own, grad_in, gain_sum, *refs):
+    if split:
+        halves, whole, wide, inbox, *sems = refs
+    else:
+        whole, wide, inbox, *sems = refs
+    greet(True, False)
+    gain_sum[...] = jnp.zeros_like(gain_sum)
+    width = own.shape[1]
+    start = pl.multiple_of(lax.axis_index("tp") * width, 128)
+
+    def finish(rows):
+        block = tokens[rows, :].astype(F32) + merged[rows, :].astype(F32)
+        scale = rms_scale(block)
+        grad = whole[rows, :].astype(F32)
+        gain_sum[0:1, :] += jnp.sum(grad * (block * scale), axis=0, keepdims=True)
+        grad = grad * gains[1:2, :]
+        mean = jnp.mean(block * grad, axis=-1, keepdims=True)
+        grad = upstream[rows, :].astype(F32) + scale * grad - block * (scale * scale * scale * mean)
+        wide[...] = grad
+        own[rows, :] = wide[:, pl.ds(start, width)]
+        grad = grad.astype(BF16)
+        grad_in[rows, :] = grad
+        if split:
+            put_split(halves, rows, grad)
+
+    line_sum(part, whole, inbox, sems, finish, lambda t: None)
+
+
+def turn(part, tokens, merged, upstream, gains, split):
+    rows, features = tokens.shape
+    shape = jax.ShapeDtypeStruct
+    outs = [
+        shape((rows, features // lax.axis_size("tp")), F32),
+        shape((rows, features), BF16),
+        shape((8, features), F32),
+    ]
+    if split:
+        outs.append(shape((2, rows, features // 2), BF16))
+    return pl.pallas_call(
+        lambda *refs: turn_kernel(split, *refs),
+        out_shape=tuple(outs),
+        in_specs=[NEAR] * 5,
+        out_specs=[NEAR] * len(outs),
+        scratch_shapes=[pltpu.VMEM((rows, features), BF16), pltpu.VMEM((CHUNK, features), F32)]
+        + line_scratch(rows, features),
+        compiler_params=pltpu.CompilerParams(collective_id=3, has_side_effects=True),
+        name="turn",
+    )(part, tokens, merged, upstream, gains)
 
 
 def gelu_pair(q):
@@ -123,9 +554,26 @@
         carry_ref[8:9, lanes] = product[last : last + 1, :]
 
 
+def spread_blocks(blocks_ref, out_ref):
+    chans, size = blocks_ref.shape[1:]
+    row = lax.broadcasted_iota(jnp.int32, (chans, chans), 0)
+    col = lax.broadcasted_iota(jnp.int32, (chans, chans), 1)
+    inner = lax.broadcasted_iota(jnp.int32, (size, chans), 0)
+    outer = lax.broadcasted_iota(jnp.int32, (size, chans), 1)
+    inside = row < 0
+    repeat = outer < 0
+    for low in range(0, chans, size):
+        inside |= (row >= low) & (row < low + size) & (col >= low) & (col < low + size)
+        repeat |= outer - low == inner
+    repeat = repeat.astype(F32).astype(BF16)
+    for gate in range(2):
+        wide = jnp.dot(blocks_ref[gate], repeat, preferred_element_type=F32)
+        out_ref[:, gate * chans : (gate + 1) * chans] = jnp.where(inside, wide, 0.0).astype(BF16)
+
+
 def forward_kernel(
-    branch_ref, halo_ref, mask_ref, taps_ref, bias_ref, gates_ref, gate_bias_ref, softer_ref,
-    conv_ref, rate_ref, entry_ref, state_ref, run_ref,
+    branch_ref, halo_ref, mask_ref, taps_ref, bias_ref, blocks_ref, gate_bias_ref, softer_ref,
+    conv_ref, rate_ref, entry_ref, state_ref, run_ref, gates_ref,
     window, decay, value, inner, product, carry,
 ):
     rows, chans = conv_ref.shape
@@ -133,6 +581,7 @@
 
     @pl.when(spot == 0)
     def _():
+        spread_blocks(blocks_ref, gates_ref)
         window[0:8, :] = halo_ref[...].astype(F32)
         carry[0:8, :] = jnp.zeros((8, chans), F32)
         carry[8:16, :] = jnp.ones((8, chans), F32)
@@ -170,24 +619,27 @@
     return pl.BlockSpec(shape, lambda i: (0, 0))
 
 
-def recur_forward(branch, halo, masks, taps, bias, gates, gate_bias, softer):
-    rows, chans = branch.shape
+def recur_forward(branch, halo, masks, taps, bias, blocks, gate_bias, softer):
+    rows, chans = branch.shape[0], halo.shape[1]
     wide = jax.ShapeDtypeStruct((rows, chans), F32)
     return pl.pallas_call(
         forward_kernel,
         grid=(rows // TILE,),
-        out_shape=(jax.ShapeDtypeStruct((rows, chans), BF16), wide, wide, wide, wide),
+        out_shape=(
+            jax.ShapeDtypeStruct((rows, chans), BF16), wide, wide, wide, wide,
+            jax.ShapeDtypeStruct((chans, 2 * chans), BF16),
+        ),
         in_specs=[
             tile_spec(chans),
             fixed_spec((8, chans)),
             tile_spec(masks.shape[1]),
             fixed_spec(taps.shape),
             fixed_spec((1, chans)),
-            fixed_spec(gates.shape),
+            pl.BlockSpec(blocks.shape, lambda i: (0, 0, 0)),
             fixed_spec((1, 2 * chans)),
             fixed_spec((1, chans)),
         ],
-        out_specs=[tile_spec(chans)] * 5,
+        out_specs=[tile_spec(chans)] * 5 + [fixed_spec((chans, 2 * chans))],
         scratch_shapes=[
             pltpu.VMEM((TILE + 8, chans), F32),
             pltpu.VMEM((chans // LANES, TILE, LANES), F32),
@@ -200,11 +652,43 @@
             flops=2 * rows * chans * 2 * chans, bytes_accessed=24 * rows * chans, transcendentals=5 * rows * chans
         ),
         name="recur_forward",
-    )(branch, halo, masks, taps, bias, gates, gate_bias, softer)
+    )(branch, halo, masks, taps, bias, blocks, gate_bias, softer)
+
+
+def merge_kernel(local_ref, run_ref, enter_ref, pre_ref, weight_ref, state_ref, gated_ref, part_ref):
+    state = local_ref[...] + run_ref[...] * enter_ref[0:1, :]
+    state_ref[...] = state
+    pre = pre_ref[...].astype(F32)
+    gated = (state * gelu_pair(pre)[0]).astype(BF16)
+    gated_ref[...] = gated
+    part_ref[...] = jnp.dot(gated, weight_ref[...], preferred_element_type=F32).astype(BF16)
+
+
+def merge_states(local, run, enter, branches, weight):
+    rows, chans = local.shape
+    features = weight.shape[1]
+    shape = jax.ShapeDtypeStruct
+    return pl.pallas_call(
+        merge_kernel,
+        grid=(rows // TILE,),
+        out_shape=(shape((rows, chans), F32), shape((rows, chans), BF16), shape((rows, features), BF16)),
+        in_specs=[
+            tile_spec(chans), tile_spec(chans), fixed_spec((1, chans)),
+            pl.BlockSpec((TILE, chans), lambda i: (i, 1)),
+            fixed_spec(weight.shape),
+        ],
+        out_specs=[tile_spec(chans), tile_spec(chans), tile_spec(features)],
+        cost_estimate=pl.CostEstimate(
+            flops=2 * rows * chans * features, bytes_accessed=16 * rows * chans, transcendentals=rows * chans
+        ),
+        name="merge_states",
+    )(local, run, enter, branches, weight)
 
 
 def adjoint_kernel(
-    rate_ref, up_ref, mask_ref, softer_ref, grad_ref, run_ref, head_ref, decay, value, inner, product, carry
+    rate_ref, up_ref, pre_ref, state_ref, mask_ref, softer_ref,
+    grad_ref, run_ref, head_ref, pre_grad_ref,
+    decay, value, inner, product, carry,
 ):
     rows, chans = rate_ref.shape
     groups = chans // LANES
@@ -226,26 +710,33 @@
     gap = CGAIN * rate_ref[...] * softer_ref[...]
     step = jnp.where(keep, jnp.exp(-gap), 0.0)
     put_lanes(decay, step, rows)
-    put_lanes(value, up_ref[...], rows)
+    gate, slope = gelu_pair(pre_ref[...].astype(F32))
+    up = up_ref[...]
+    pre_grad_ref[...] = (up * state_ref[...] * slope).astype(BF16)
+    put_lanes(value, up * gate, rows)
     sweep(decay, value, inner, product, grad_ref, run_ref, carry, True, 1)
     head_ref[...] = jnp.broadcast_to(step[0:1, :] * carry[0:1, :], (8, chans))
 
 
-def recur_adjoint(rate, up, masks, softer):
+def recur_adjoint(rate, up, branches, state, masks, softer):
     rows, chans = rate.shape
     count = rows // TILE
     wide = jax.ShapeDtypeStruct((rows, chans), F32)
     return pl.pallas_call(
         adjoint_kernel,
         grid=(count,),
-        out_shape=(wide, wide, jax.ShapeDtypeStruct((8, chans), F32)),
+        out_shape=(
+            wide, wide, jax.ShapeDtypeStruct((8, chans), F32), jax.ShapeDtypeStruct((rows, chans), BF16)
+        ),
         in_specs=[
             tile_spec(chans, count),
+            tile_spec(chans, count),
+            pl.BlockSpec((TILE, chans), lambda i: (count - 1 - i, 1)),
             tile_spec(chans, count),
             tile_spec(masks.shape[1], count),
             fixed_spec((1, chans)),
         ],
-        out_specs=[tile_spec(chans, count), tile_spec(chans, count), fixed_spec((8, chans))],
+        out_specs=[tile_spec(chans, count), tile_spec(chans, count), fixed_spec((8, chans)), tile_spec(chans, count)],
         scratch_shapes=[
             pltpu.VMEM((chans // LANES, TILE + 8, LANES), F32),
             pltpu.VMEM((chans // LANES, TILE, LANES), F32),
@@ -257,12 +748,12 @@
             flops=8 * rows * chans, bytes_accessed=16 * rows * chans, transcendentals=rows * chans
         ),
         name="recur_adjoint",
-    )(rate, up, masks, softer)
+    )(rate, up, branches, state, masks, softer)
 
 
 def backward_kernel(
     grad_ref, run_ref, enter_ref, rate_ref, entry_ref, conv_ref, state_ref, mask_ref,
-    branch_ref, halo_ref, taps_ref, gates_ref, softer_ref,
+    branch_ref, pre_grad_ref, halo_ref, taps_ref, gates_ref, softer_ref,
     back_ref, tail_ref, head_ref, gate_grad_ref, sums_ref,
     shifts, edge,
 ):
@@ -321,7 +812,8 @@
         moved = shifts[shift - 1, shift : shift + rows, :]
         add_row(4 + shift, moved * branch)
         back = back + taps_ref[shift : shift + 1, :] * moved
-    back_ref[...] = back.astype(BF16)
+    back_ref[:, 0:chans] = back.astype(BF16)
+    back_ref[:, chans:] = pre_grad_ref[...]
 
     @pl.when(spot == 0)
     def _():
@@ -340,7 +832,7 @@
         head_ref[...] = head
 
 
-def recur_backward(grad, run, enter, rate, entry, conv, state, masks, branch, halo, taps, gates, softer):
+def recur_backward(grad, run, enter, rate, entry, conv, state, masks, branch, pre_grad, halo, taps, gates, softer):
     rows, chans = rate.shape
     count = rows // TILE
     edge = jax.ShapeDtypeStruct((8, chans), F32)
@@ -349,7 +841,7 @@
         backward_kernel,
         grid=(count,),
         out_shape=(
-            jax.ShapeDtypeStruct((rows, chans), BF16),
+            jax.ShapeDtypeStruct((rows, 2 * chans), BF16),
             edge,
             edge,
             jax.ShapeDtypeStruct((chans, 2 * chans), F32),
@@ -359,13 +851,14 @@
             wide, wide, fixed_spec((1, chans)), wide, wide, wide, wide,
             tile_spec(masks.shape[1], count),
             wide,
+            wide,
             fixed_spec((8, chans)),
             fixed_spec(taps.shape),
             fixed_spec(gates.shape),
             fixed_spec((1, chans)),
         ],
         out_specs=[
-            wide,
+            tile_spec(2 * chans, count),
             fixed_spec((8, chans)),
             fixed_spec((8, chans)),
             fixed_spec((chans, 2 * chans)),
@@ -379,15 +872,7 @@
             flops=8 * rows * chans * chans, bytes_accessed=28 * rows * chans, transcendentals=2 * rows * chans
         ),
         name="recur_backward",
-    )(grad, run, enter, rate, entry, conv, state, masks, branch, halo, taps, gates, softer)
-
-
-def spread_blocks(blocks):
-    count, size = blocks.shape[0], blocks.shape[1]
-    rows = [
-        jnp.pad(blocks[i], ((0, 0), (i * size, (count - 1 - i) * size))) for i in range(count)
-    ]
-    return jnp.concatenate(rows, axis=0)
+    )(grad, run, enter, rate, entry, conv, state, masks, branch, pre_grad, halo, taps, gates, softer)
 
 
 def shards(
@@ -419,14 +904,20 @@
     feat_local = features // lax.axis_size("tp")
     feat_start = lax.axis_index("tp") * feat_local
 
-    whole_recur = gather_rows(w_recur)
-    whole_gelu = gather_rows(w_gelu)
-    gains = lax.all_gather(jnp.stack([norm_mix, norm_feed]), "fsdp", axis=1, tiled=True).astype(F32)
-    gain_one, gain_two = gains[0:1], gains[1:2]
-    whole_merge = gather_rows(w_merge.T)
-    whole_gate = gather_rows(w_gate)
-    whole_up = gather_rows(w_up)
-    whole_down = gather_rows(w_down.T)
+    square = lax.axis_size("fsdp") == 4
+    gain_shard = jnp.concatenate(
+        [jnp.stack([norm_mix, norm_feed]).astype(F32), jnp.zeros((6, norm_mix.shape[0]), F32)], axis=0
+    )
+    if square:
+        normed, normed_split, gains, whole_in, whole_merge = enter(tokens, gain_shard, w_recur, w_gelu, w_merge)
+    else:
+        whole_in = gather_halves(jnp.concatenate([w_recur, w_gelu], axis=1), 0)
+        whole_merge = gather_halves(w_merge, 1)
+        gains = lax.all_gather(gain_shard, "fsdp", axis=1, tiled=True)
+        inputs = tokens.astype(F32)
+        normed = (inputs * rms_scale(inputs) * gains[0:1]).astype(BF16)
+        normed_split = split_features(normed)
+    gain_one = gains[0:1]
 
     padded_ids = jnp.concatenate([jnp.full((edge,), -1, jnp.int32), segments])
     local_ids = lax.dynamic_slice_in_dim(padded_ids, lax.axis_index("ctx") * piece, piece + edge)
@@ -436,99 +927,87 @@
         axis=1,
     ).astype(F32)
     taps = conv_taps.astype(F32)
-    gates = jnp.concatenate([spread_blocks(rate_gate), spread_blocks(entry_gate)], axis=1)
+    blocks = jnp.stack([rate_gate.reshape(chans, block), entry_gate.reshape(chans, block)])
     gate_bias = jnp.concatenate([rate_bias, entry_bias]).astype(F32)[None, :]
     softer = jax.nn.softplus(-decay_logit)[None, :]
 
-    inputs = tokens.astype(F32)
-    scale_one = rms_scale(inputs)
-    normed = (inputs * scale_one * gain_one).astype(BF16)
-    branch = jnp.dot(normed, whole_recur, preferred_element_type=F32).astype(BF16)
-    halo = shifted(branch[piece - 8 :], "ctx", 1)
-    pre_gelu = jnp.dot(normed, whole_gelu, preferred_element_type=F32)
-    conv, rate, entry, local_state, run = recur_forward(
-        branch, halo, masks, taps, conv_bias.astype(F32)[None, :], gates, gate_bias, softer
+    rows_to_features = (((1,), (1,)), ((), ()))
+    branches = jnp.dot(normed, whole_in, preferred_element_type=F32).astype(BF16)
+    halo = shifted(branches[piece - 8 :, :chans], "ctx", 1)
+    conv, rate, entry, local_state, run, gates = recur_forward(
+        branches, halo, masks, taps, conv_bias.astype(F32)[None, :], blocks, gate_bias, softer
     )
     state_in = shifted(local_state[piece - 8 :], "ctx", 1)[7:8]
-    states = local_state + run * state_in
-    gelu_out, gelu_slope = gelu_pair(pre_gelu)
-    gated = (states * gelu_out).astype(BF16)
-    part_merge = lax.dot_general(gated, whole_merge, (((1,), (1,)), ((), ())), preferred_element_type=F32)
-    merged = lax.psum(part_merge.astype(BF16), "tp").astype(F32)
-
-    d_hidden = lax.dot_general(cotangent, whole_down, (((1,), (0,)), ((), ())), preferred_element_type=F32)
-    resid = inputs + merged
-    scale_two = rms_scale(resid)
-    normed_two = (resid * scale_two * gain_two).astype(BF16)
-    gate_pre = jnp.dot(normed_two, whole_gate, preferred_element_type=F32)
-    up_vals = jnp.dot(normed_two, whole_up, preferred_element_type=F32)
-    gate_act, gate_slope = gelu_pair(gate_pre)
+    states, gated, part_merge = merge_states(local_state, run, state_in, branches, whole_merge)
+
+    if square:
+        merged, normed_two, normed_two_split, whole_mid, whole_down = middle(
+            part_merge, tokens, gains, (w_gate, w_up, w_down)
+        )
+    else:
+        merged, normed_two = middle(part_merge, tokens, gains, ())
+        normed_two_split = split_features(normed_two)
+        whole_mid = gather_halves(jnp.concatenate([w_gate, w_up], axis=1), 0)
+        whole_down = gather_halves(w_down, 1)
+    cotangent_split = split_features(cotangent)
+
+    units = w_gate.shape[1]
+    pre_mid = jnp.dot(normed_two, whole_mid, preferred_element_type=F32).astype(BF16)
+    d_hidden = lax.dot_general(cotangent, whole_down, rows_to_features, preferred_element_type=F32).astype(BF16)
+    gate_act, gate_slope = gelu_pair(pre_mid[:, :units].astype(F32))
+    up_vals = pre_mid[:, units:].astype(F32)
+    wide_hidden = d_hidden.astype(F32)
     hidden = (gate_act * up_vals).astype(BF16)
-    d_gate = (d_hidden * up_vals * gate_slope).astype(BF16)
-    d_up = (d_hidden * gate_act).astype(BF16)
-    part_two = lax.dot_general(
-        d_gate, whole_gate, (((1,), (1,)), ((), ())), preferred_element_type=F32
-    ) + lax.dot_general(d_up, whole_up, (((1,), (1,)), ((), ())), preferred_element_type=F32)
-    d_normed_two = lax.psum(part_two.astype(BF16), "tp").astype(F32)
+    d_mid = jnp.concatenate(
+        [(wide_hidden * up_vals * gate_slope).astype(BF16), (wide_hidden * gate_act).astype(BF16)], axis=1
+    )
+    part_two = lax.dot_general(d_mid, whole_mid, rows_to_features, preferred_element_type=F32).astype(BF16)
+    pair_down = pair_sums(cotangent_split, hidden, 1)
+    pair_mid = pair_sums(normed_two_split, d_mid, 0)
+    part_two = after(part_two, pair_down, pair_mid)
+    turned = turn(part_two, tokens, merged, cotangent, gains, square)
+    own_resid_grad, d_merge_in, feed_sums = turned[:3]
+    d_merge_split = turned[3] if square else split_features(d_merge_in)
+    grad_feed = feed_sums[0]
+
     feed = lax.psum_scatter(
-        lax.dot_general(
-            hidden, whole_down, (((1,), (1,)), ((), ())), preferred_element_type=F32
-        ).astype(BF16),
+        jnp.dot(after(hidden, d_merge_in), whole_down, preferred_element_type=F32).astype(BF16),
         "tp",
         scatter_dimension=1,
         tiled=True,
     ).astype(F32)
-    output = (lax.dynamic_slice_in_dim(resid, feat_start, feat_local, 1) + feed).astype(BF16)
-
-    rows_to_rows = (((0,), (0,)), ((), ()))
-    grad_down = lax.dot_general(cotangent, hidden, rows_to_rows, preferred_element_type=F32)
-    grad_gate = lax.dot_general(normed_two, d_gate, rows_to_rows, preferred_element_type=F32)
-    grad_up = lax.dot_general(normed_two, d_up, rows_to_rows, preferred_element_type=F32)
-    shard_down = scatter_rows(grad_down).T
-    shard_gate = scatter_rows(grad_gate)
-    shard_up = scatter_rows(grad_up)
-
-    grad_feed = jnp.sum(d_normed_two * resid * scale_two, axis=0)
-    weighted = d_normed_two * gain_two
-    d_resid = (
-        cotangent.astype(F32)
-        + scale_two * weighted
-        - resid * scale_two**3 * jnp.mean(resid * weighted, axis=-1, keepdims=True)
-    )
-    d_merge_in = d_resid.astype(BF16)
-    grad_merge = lax.dot_general(d_merge_in, gated, rows_to_rows, preferred_element_type=F32)
-    shard_merge = scatter_rows(grad_merge).T
-    d_gated = jnp.dot(d_merge_in, whole_merge, preferred_element_type=F32)
-    d_states = d_gated * gelu_out
-    d_gelu_pre = (d_gated * states * gelu_slope).astype(BF16)
-    local_grad, grad_run, first = recur_adjoint(rate, d_states, masks, softer)
+    shard_down = to_owners(pair_down, 1)
+    shard_mid = to_owners(pair_mid, 0)
+
+    d_gated = lax.dot_general(d_merge_in, whole_merge, rows_to_features, preferred_element_type=F32)
+    local_grad, grad_run, first, d_gelu_pre = recur_adjoint(rate, d_gated, branches, states, masks, softer)
     grad_in = shifted(first, "ctx", -1)[0:1]
     back, tail, head, gate_grads, sums = recur_backward(
-        local_grad, grad_run, grad_in, rate, entry, conv, states, masks, branch, halo, taps, gates, softer
+        local_grad, grad_run, grad_in, rate, entry, conv, states, masks, branches, d_gelu_pre,
+        halo, taps, gates, softer
     )
     returned = shifted(head, "ctx", -1)
-    d_branch = lax.dynamic_update_slice_in_dim(back, (tail + returned).astype(BF16), piece - 8, 0)
-
-    part_one = lax.dot_general(
-        d_gelu_pre, whole_gelu, (((1,), (1,)), ((), ())), preferred_element_type=F32
-    ) + lax.dot_general(d_branch, whole_recur, (((1,), (1,)), ((), ())), preferred_element_type=F32)
+    shard_merge = to_owners(pair_sums(d_merge_split, after(gated, back), 1), 1)
+    d_in = lax.dynamic_update_slice(back, (tail + returned).astype(BF16), (piece - 8, 0))
+
+    inputs = tokens.astype(F32)
+    scale_one = rms_scale(inputs)
+    part_one = lax.dot_general(d_in, whole_in, rows_to_features, preferred_element_type=F32)
     stat_one = jnp.sum(part_one * inputs * gain_one, axis=-1)
     grad_mix = jnp.sum(part_one * inputs * scale_one, axis=0)
     d_normed = lax.psum_scatter(
         part_one.astype(BF16), "tp", scatter_dimension=1, tiled=True
     ).astype(F32)
     stat_one = lax.psum(stat_one, "tp")[:, None] / features
-    grad_recur = lax.dot_general(normed, d_branch, rows_to_rows, preferred_element_type=F32)
-    grad_gelu = lax.dot_general(normed, d_gelu_pre, rows_to_rows, preferred_element_type=F32)
-    shard_recur = scatter_rows(grad_recur)
-    shard_gelu = scatter_rows(grad_gelu)
+    shard_in = to_owners(pair_sums(normed_split, d_in, 0), 0)
 
     def own(block):
         return lax.dynamic_slice_in_dim(block, feat_start, feat_local, 1)
 
     own_inputs = own(inputs)
+    output = (own_inputs + own(merged).astype(F32) + feed).astype(BF16)
     grad_tokens = (
-        own(d_resid)
+        own_resid_grad
         + scale_one * d_normed * own(gain_one)
         - own_inputs * scale_one**3 * stat_one
     ).astype(BF16)
@@ -549,11 +1028,11 @@
     return (
         output,
         grad_tokens,
-        shard_recur,
-        shard_gelu,
+        shard_in[:, :chans],
+        shard_in[:, chans:],
         shard_merge,
-        shard_gate,
-        shard_up,
+        shard_mid[:, :units],
+        shard_mid[:, units:],
         shard_down,
         own_norms[0],
         own_norms[1],

time: 1160 us -> 830 us (0.72)
  waiting for transfers between devices: 609 us -> 183 us
  Pallas kernels: 41 us -> 338 us
  local copies, waits for them, and re-layouts: 141 us -> 28.9 us
  other arithmetic: 101 us -> 26.6 us
    psum x2 -> x0, waiting for transfers between devices: 311 us -> none  [the longest x1 157 us: shards(): merged = lax.psum(part_merge.astype(BF16), 'tp').astype(F32)]
    pallas_call x0 -> x4, Pallas kernels: none -> 293 us  [the longest x1 119 us: middle(): pl.pallas_call(lambda *refs: middle_kernel(bool(shards), *refs), out_shap...]
    all_gather x6 -> x0, waiting for transfers between devices: 148 us -> none  [gather_rows(): mine = lax.all_gather(mine, 'fsdp', axis=0)]
    dynamic_slice x9 -> x1, local copies, waits for them, and re-layouts: 43.6 us -> 4.16 us  [split_features(): lax.dynamic_index_in_dim(parts, index, 2, False).reshape(block.shape[0], -1)]
    reshape x7 -> x0, local copies, waits for them, and re-layouts: 35.4 us -> none  [the longest x6 18.5 us: scatter_rows(): pair.reshape(-1, grad.shape[1])]
    unnamed x138 -> x78, local copies, waits for them, and re-layouts: 42.5 us -> 10.6 us
    reduce_scatter x7 -> x5, waiting for transfers between devices: 69.1 us -> 101 us  [the longest x1 79 us: shards(): lax.psum_scatter(jnp.dot(after(hidden, d_merge_in), whole_down, preferred...]
    convert_element_type x14 -> x5, other arithmetic: 34.8 us -> 8.31 us  [the longest x4 4.31 us: to_owners(): return jnp.concatenate([first, second], axis=dim).astype(F32)]
  transfers between devices with their start and end apart: 39 -> 19, of which waited for: 15 -> 4; matrix products, arithmetic and copies ran while one was open for 26% -> 17% of each run, Pallas kernels for 4% -> 18%
where the time goes in v2:
time: 830 us; the launch traced here: 824 us
  Pallas kernels  338 us (41%)
  waiting for transfers between devices  183 us (22%)
  matrix products  146 us (18%)
  blocking collectives  74.4 us (9%)
  local copies, waits for them, and re-layouts  28.9 us (3%)
  other arithmetic  26.6 us (3%)
  between operations  16.5 us (2%)
  starting transfers between devices  11.3 us (1%)
    pallas_call x1, Pallas kernels, middle(): pl.pallas_call(lambda *refs: middle_kernel(bool(shards), *refs), out_shap...  119 us
    pallas_call x1, Pallas kernels, turn(): pl.pallas_call(lambda *refs: turn_kernel(split, *refs), out_shape=tuple(o...  118 us
    reduce_scatter x1, waiting for transfers between devices, shards(): lax.psum_scatter(part_one.astype(BF16), 'tp', scatter_dimension=1, tiled=...  79.5 us
    reduce_scatter x1, waiting for transfers between devices, shards(): lax.psum_scatter(jnp.dot(after(hidden, d_merge_in), whole_down, preferred...  79 us
    dot_general x8, matrix products, product(): return lax.dot_general(*pair, rows_to_rows, preferred_element_type=F32)  55.5 us
    pallas_call x1, Pallas kernels, enter(): pl.pallas_call(enter_kernel, out_shape=(shape((rows, features), BF16), sh...  44.9 us
    psum x1, blocking collectives, shards(): lax.psum(jnp.stack([grad_mix, grad_feed / lax.axis_size('tp')]), ('fsdp',...  39 us
    psum x1, blocking collectives, shards(): row_sums = lax.psum(sums, ('fsdp', 'ctx'))  25.2 us
  transfers between devices with their start and end apart: 19, of which 4 were waited for; matrix products, arithmetic and copies ran while one was open for 17% of the time, Pallas kernels for 18%

profile of v2, /device:TPU:0, one launch (start us, length us, event | category | flops | bytes accessed | tf_op | source)
XLA Modules:
  0.0 823.8 jit_solution(18363268852116902512)
XLA Ops:
  10.0 44.9 %enter.1 = (bf16[1024,2048]{1,0:T(8,128)(2,1)}, bf16[2,1024,1024]{2,1,0:T(8,128)(2,1)}, f32[8,2048]{1,0:T(8,128)}, bf16[2048,1280]{1,0:T(8,128)(2,1)}, bf16[640,2048]{1,0:T(8,128)(2,1)}) custom-call(bf16[1024,2048]{1,0:T(8,128)(2,1)} %refs_1_.3, f32[8,512]{1,0:T(8,128)} %fusion.46.gain_shard, bf16[512,640]{1,0:T(8,128)(2,1)} %recur.1, ...), custom_call_target="tpu_custom_call" | custom-call | tf_op jit(solution)/shard_map/enter/pallas_call | solution.py:346
  55.1 8.9 %convolution_convert_fusion.5.branch_ref.pre_ref = bf16[1024,1280]{1,0:T(8,128)(2,1)S(1)} fusion(bf16[1024,2048]{1,0:T(8,128)(2,1)} %get-tuple-element.52, bf16[2048,1280]{1,0:T(8,128)(2,1)} %get-tuple-element.53), kind=kOutput, calls=%fused_computation.35 | convolution fusion | flops 5370019840 | bytes 12058624 | tf_op jit(solution)/shard_map/dot_general | solution.py:935
  78.1 14.3 %recur_forward.1 = (bf16[1024,640]{1,0:T(8,128)(2,1)}, f32[1024,640]{1,0:T(8,128)}, f32[1024,640]{1,0:T(8,128)}, f32[1024,640]{1,0:T(8,128)}, f32[1024,640]{1,0:T(8,128)}, /*index=5*/bf16[640,1280]{1,0:T(8,128)(2,1)}) custom-call(bf16[1024,1280]{1,0:T(8,128)(2,1)} %copy-done.1, bf16[8,640]{1,0:T(8,128)(2,1)} %copy-done.18, ...), custom_call_target="tpu_custom_call" | custom-call | flops 1677721600 | bytes 15728640 | tf_op jit(solution)/shard_map/recur_forward/pallas_call | solution.py:625
  99.2 10.7 %merge_states.1 = (f32[1024,640]{1,0:T(8,128)}, bf16[1024,640]{1,0:T(8,128)(2,1)}, bf16[1024,2048]{1,0:T(8,128)(2,1)}) custom-call(f32[1024,640]{1,0:T(8,128)} %get-tuple-element.54.local_ref, f32[1024,640]{1,0:T(8,128)} %get-tuple-element.55.run_ref, f32[1,640]{1,0:T(1,128)} %slice.166.enter_ref, bf16[1024,1280]{1,0:T(8,128)(2,1)} %copy-done.1, ...), custom_call_target="tpu_custom_call" | custom-call | flops 2684354560 | bytes 10485760 | tf_op jit(solution)/shard_map/merge_states/pallas_call | solution.py:671
  109.8 118.9 %middle.1 = (bf16[1024,2048]{1,0:T(8,128)(2,1)}, bf16[1024,2048]{1,0:T(8,128)(2,1)}, bf16[2,1024,1024]{2,1,0:T(8,128)(2,1)}, bf16[2048,3072]{1,0:T(8,128)(2,1)}, bf16[1536,2048]{1,0:T(8,128)(2,1)}) custom-call(bf16[1024,2048]{1,0:T(8,128)(2,1)} %get-tuple-element.57.refs_0_, bf16[1024,2048]{1,0:T(8,128)(2,1)} %refs_1_.3, ...), custom_call_target="tpu_custom_call" | custom-call | tf_op jit(solution)/shard_map/middle/pallas_call | solution.py:424
  228.8 18.6 %convolution_convert_fusion.1 = bf16[1024,3072]{1,0:T(8,128)(2,1)} fusion(bf16[1024,2048]{1,0:T(8,128)(2,1)} %get-tuple-element.60, bf16[2048,3072]{1,0:T(8,128)(2,1)} %get-tuple-element.61), kind=kOutput, calls=%fused_computation.29 | convolution fusion | flops 12888047616 | bytes 23068672 | tf_op jit(solution)/shard_map/dot_general | solution.py:955
  247.4 14.2 %fusion.6 = (bf16[1024,1536]{1,0:T(8,128)(2,1)S(1)}, bf16[1024,1536]{1,0:T(8,128)(2,1)S(1)}, bf16[1024,1536]{1,0:T(8,128)(2,1)}) fusion(bf16[1024,3072]{1,0:T(8,128)(2,1)} %convolution_convert_fusion.1, bf16[1536,2048]{1,0:T(8,128)(2,1)S(1)} %copy-done.24, bf16[1024,2048]{1,0:T(8,128)(2,1)S(1)} %copy-done.2), kind=kOutput, calls=%fused_computation.19 | convolution fusion | flops 6488064000 | bytes 26214400 | tf_op jit(solution)/shard_map/dot_general | solution.py:956
  261.7 7.9 convolution_convert_fusion.7
  269.8 9.2 %convolution_convert_fusion = bf16[1024,3072]{1,0:T(8,128)(2,1)} fusion(bf16[2,1024,1024]{2,1,0:T(8,128)(2,1)S(1)} %copy-done.26, bf16[1024,1536]{1,0:T(8,128)(2,1)S(1)} %get-tuple-element.94, bf16[1024,1536]{1,0:T(8,128)(2,1)S(1)} %get-tuple-element.93), kind=kOutput, calls=%fused_computation.28 | convolution fusion | flops 6458179584 | bytes 14680064 | tf_op jit(solution)/shard_map/dot_general | solution.py:56
  284.6 19.8 %convolution_convert_fusion.2.refs_0_ = bf16[1024,2048]{1,0:T(8,128)(2,1)} fusion(bf16[2048,3072]{1,0:T(8,128)(2,1)} %get-tuple-element.61, bf16[1024,1536]{1,0:T(8,128)(2,1)} %copy-done.32, bf16[1024,1536]{1,0:T(8,128)(2,1)} %copy-done.31), kind=kOutput, calls=%fused_computation.32 | convolution fusion | flops 12899581952 | bytes 23068672 | tf_op jit(solution)/shard_map/dot_general | solution.py:964
  304.3 12.6 %add_convert_fusion = bf16[1024,3072]{1,0:T(8,128)(2,1)} fusion(bf16[1024,3072]{1,0:T(8,128)(2,1)} %collective-permute-done.3, bf16[2,1024,1024]{2,1,0:T(8,128)(2,1)S(1)} %copy-done.27, bf16[1024,1536]{1,0:T(8,128)(2,1)} %copy-done.32, bf16[1024,1536]{1,0:T(8,128)(2,1)} %copy-done.31), kind=kOutput, calls=%fused_computation.7 | convolution fusion | flops 6464471040 | bytes 20971520 | tf_op jit(solution)/shard_map/dot_general | solution.py:56
  316.9 118.4 %turn.1 = (f32[1024,512]{1,0:T(8,128)}, bf16[1024,2048]{1,0:T(8,128)(2,1)}, f32[8,2048]{1,0:T(8,128)}, bf16[2,1024,1024]{2,1,0:T(8,128)(2,1)}) custom-call(bf16[1024,2048]{1,0:T(8,128)(2,1)} %convolution_convert_fusion.2.refs_0_, bf16[1024,2048]{1,0:T(8,128)(2,1)} %refs_1_.3, bf16[1024,2048]{1,0:T(8,128)(2,1)} %get-tuple-element.59.refs_2_, ...), custom_call_target="tpu_custom_call" | custom-call | tf_op jit(solution)/shard_map/turn/pallas_call | solution.py:473
  435.4 7.1 fusion.58.up_ref
  442.5 11.5 %recur_adjoint.1 = (f32[1024,640]{1,0:T(8,128)}, f32[1024,640]{1,0:T(8,128)}, f32[8,640]{1,0:T(8,128)}, bf16[1024,640]{1,0:T(8,128)(2,1)}) custom-call(f32[1024,640]{1,0:T(8,128)} %get-tuple-element.68.rate_ref, f32[1024,640]{1,0:T(8,128)} %fusion.58.up_ref, bf16[1024,1280]{1,0:T(8,128)(2,1)} %copy-done.1, f32[1024,640]{1,0:T(8,128)} %get-tuple-element.69.state_ref, ...), custom_call_target="tpu_custom_call" | custom-call | flops 5242880 | bytes 10485760 | tf_op jit(solution)/shard_map/recur_adjoint/pallas_call | solution.py:725
  457.9 18.9 %recur_backward.1 = (bf16[1024,1280]{1,0:T(8,128)(2,1)}, f32[8,640]{1,0:T(8,128)}, f32[8,640]{1,0:T(8,128)}, f32[640,1280]{1,0:T(8,128)}, f32[16,640]{1,0:T(8,128)}) custom-call(f32[1024,640]{1,0:T(8,128)} %get-tuple-element.70.grad_ref, f32[1024,640]{1,0:T(8,128)} %get-tuple-element.71.run_ref, f32[1,640]{1,0:T(1,128)} %slice.169.enter_ref, ...), custom_call_target="tpu_custom_call" | custom-call | flops 3355443200 | bytes 18350080 | tf_op jit(solution)/shard_map/recur_backward/pallas_call | solution.py:840
  498.0 6.8 add_convert_fusion.2
  506.7 11.2 %convolution_convert_fusion.3 = bf16[1024,2048]{1,0:T(8,128)(2,1)} fusion(bf16[1024,1536]{1,0:T(8,128)(2,1)S(1)} %copy-done.34, bf16[1536,2048]{1,0:T(8,128)(2,1)} %get-tuple-element.62), kind=kOutput, calls=%fused_computation.33 | convolution fusion | flops 6444548096 | bytes 13631488 | tf_op jit(solution)/shard_map/dot_general | solution.py:974
  522.9 10.4 %multiply_reduce_fusion = (f32[2048]{0:T(1024)S(1)}, f32[1024]{0:T(1024)S(1)}, bf16[1024,2048]{1,0:T(8,128)(2,1)}) fusion(f32[1024]{0:T(1024)S(1)} %get-tuple-element.121, bf16[1024,2048]{1,0:T(8,128)(2,1)S(1)} %copy-done, f32[2048]{0:T(1024)S(1)} %bitcast.97, bf16[1024,1280]{1,0:T(8,128)(2,1)S(1)} %copy-done.30, bf16[2048,1280]{1,0:T(8,128)(2,1)} %get-tuple-element.53), kind=kOutput, calls=%fused_computation.8 | convolution fusion | flops 5383386112 | bytes 16277504 | tf_op jit(solution)/shard_map/dot_general | solution.py:995
  540.8 25.2 %psum.30 = f32[16,640]{1,0:T(8,128)S(1)} all-reduce(f32[16,640]{1,0:T(8,128)S(1)} %copy-done.14), channel_id=1, replica_groups=mesh['fsdp'=4,'ctx'=2,'tp'=4] {'fsdp','ctx'}, use_global_device_ids=true, to_apply=%region_11.12 | all-reduce | flops 10240 | bytes 81920 | tf_op jit(solution)/shard_map/psum | solution.py:1027
  567.8 10.3 %psum.28 = f32[1024]{0:T(1024)S(1)} all-reduce(f32[1024]{0:T(1024)S(1)} %get-tuple-element.88), channel_id=1, replica_groups=mesh['fsdp'=4,'ctx'=2,'tp'=4] {'tp'}, use_global_device_ids=true, to_apply=%region_4.5 | all-reduce | flops 1024 | bytes 8192 | tf_op jit(solution)/shard_map/psum | solution.py:1001
  578.2 39.0 %psum.29 = f32[2,2048]{1,0:T(2,128)S(1)} all-reduce(f32[2,2048]{1,0:T(2,128)S(1)} %pad_maximum_fusion.5), channel_id=1, replica_groups=mesh['fsdp'=4,'ctx'=2,'tp'=4] {'fsdp','ctx','tp'}, use_global_device_ids=true, to_apply=%region_10.11 | all-reduce | flops 4096 | bytes 32768 | tf_op jit(solution)/shard_map/psum | solution.py:1015
  624.2 21.5 %reduce-scatter.15.cloned.1.call-done = bf16[256,3072]{1,0:T(8,128)(2,1)} async-done(((bf16[1024,3072]{1,0:T(8,128)(2,1)}), bf16[256,3072]{1,0:T(8,128)(2,1)}) %reduce-scatter.15.cloned.1.call-update) | async-done | bytes 1572880 | tf_op jit(solution)/shard_map/reduce_scatter | solution.py:63
  645.7 79.0 %reduce-scatter.7.cloned.1.call-done = bf16[1024,512]{1,0:T(8,128)(2,1)} async-done(((bf16[1024,2048]{1,0:T(8,128)(2,1)}), bf16[1024,512]{1,0:T(8,128)(2,1)}) %reduce-scatter.7.cloned.1.call-update) | async-done | bytes 1048592 | tf_op jit(solution)/shard_map/reduce_scatter | solution.py:973
  724.7 79.5 %reduce-scatter.9.cloned.1.call-done = bf16[1024,512]{1,0:T(8,128)(2,1)} async-done(((bf16[1024,2048]{1,0:T(8,128)(2,1)}), bf16[1024,512]{1,0:T(8,128)(2,1)}) %reduce-scatter.9.cloned.1.call-update) | async-done | bytes 1048592 | tf_op jit(solution)/shard_map/reduce_scatter | solution.py:998
  (174 shorter events, 88.4 us)
Async XLA Ops:
  8.0 570.1 %reduce-scatter.17.cloned.1.call-start = ((), (), s32[]{:S(2)}) async-start(), calls=%async_computation.11 | async-start | bytes 3932160 | tf_op jit(solution)/shard_map/reduce_scatter | solution.py:63
  64.0 13.4 %collective-permute-start = (bf16[8,640]{1,0:T(8,128)(2,1)S(1)}, bf16[8,640]{1,0:T(8,128)(2,1)S(1)}, u32[]{:S(2)}, u32[]{:S(2)}) collective-permute-start(bf16[8,640]{1,0:T(8,128)(2,1)S(1)} %slice.165), channel_id=1, source_target_pairs={{0,4},{1,5},{2,6},{3,7},{8,12},{9,13},{10,14},{11,15},{16,20},{17,... | collective-permute-start | bytes 30728 | tf_op jit(solution)/shard_map/ppermute | solution.py:26
  93.1 5.5 collective-permute-start.1
  269.6 9.8 %collective-permute-start.2 = (bf16[1536,1024]{1,0:T(8,128)(2,1)S(1)}, bf16[1536,1024]{1,0:T(8,128)(2,1)S(1)}, u32[]{:S(2)}, u32[]{:S(2)}) collective-permute-start(bf16[1536,1024]{1,0:T(8,128)(2,1)S(1)} %convolution_convert_fusion.7), channel_id=1, source_target_pairs={{0,4},{4,0},{1,5},{5,1},{2,6},{6,2},{3,7},{7,3},{8,12},{12,8},{9,1... | collective-permute-start | bytes 9437192 | tf_op jit(solution)/shard_map/ppermute | solution.py:20
  279.0 25.4 %collective-permute-start.3 = (bf16[1024,3072]{1,0:T(8,128)(2,1)}, bf16[1024,3072]{1,0:T(8,128)(2,1)}, u32[]{:S(2)}, u32[]{:S(2)}) collective-permute-start(bf16[1024,3072]{1,0:T(8,128)(2,1)} %convolution_convert_fusion), channel_id=1, source_target_pairs={{0,4},{4,0},{1,5},{5,1},{2,6},{6,2},{3,7},{7,3},{8,12},{12,8},{9,1... | collective-permute-start | bytes 18874376 | tf_op jit(solution)/shard_map/ppermute | solution.py:20
  284.5 333.3 %all-reduce.4.cloned.1.call-start = ((), (), s32[]{:S(2)}) async-start(), calls=%async_computation.12 | async-start | bytes 1310720 | tf_op jit(solution)/shard_map/psum | solution.py:1026
  284.6 19.8 %copy-start.27 = (bf16[2,1024,1024]{2,1,0:T(8,128)(2,1)S(1)}, bf16[2,1024,1024]{2,1,0:T(8,128)(2,1)}, u32[]{:S(2)}) copy-start(bf16[2,1024,1024]{2,1,0:T(8,128)(2,1)} %get-tuple-element.63) | copy-start | bytes 12582916
  316.9 118.5 %copy-start.4 = (bf16[640,2048]{1,0:T(8,128)(2,1)S(1)}, bf16[640,2048]{1,0:T(8,128)(2,1)}, u32[]{:S(2)}) copy-start(bf16[640,2048]{1,0:T(8,128)(2,1)} %get-tuple-element.56.weight_ref) | copy-start | bytes 7864324
  454.0 3.3 collective-permute-start.4
  476.8 7.8 collective-permute-start.5
  482.9 9.6 %collective-permute-start.8 = (bf16[640,1024]{1,0:T(8,128)(2,1)}, bf16[640,1024]{1,0:T(8,128)(2,1)}, u32[]{:S(2)}, u32[]{:S(2)}) collective-permute-start(bf16[640,1024]{1,0:T(8,128)(2,1)} %fusion.29), channel_id=1, source_target_pairs={{0,4},{4,0},{1,5},{5,1},{2,6},{6,2},{3,7},{7,3},{8,12},{12,8},{9,1... | collective-permute-start | bytes 3932168 | tf_op jit(solution)/shard_map/ppermute | solution.py:20
  489.3 8.7 %collective-permute-start.6 = (bf16[1024,1280]{1,0:T(8,128)(2,1)}, bf16[1024,1280]{1,0:T(8,128)(2,1)}, u32[]{:S(2)}, u32[]{:S(2)}) collective-permute-start(bf16[1024,1280]{1,0:T(8,128)(2,1)} %convolution_convert_fusion.6), channel_id=1, source_target_pairs={{0,4},{4,0},{1,5},{5,1},{2,6},{6,2},{3,7},{7,3},{8,12},{12,8},{9,1... | collective-permute-start | bytes 7864328 | tf_op jit(solution)/shard_map/ppermute | solution.py:20
  492.4 127.8 %reduce-scatter.13.cloned.1.call-start = ((), (), s32[]{:S(2)}) async-start(), calls=%async_computation.9 | async-start | bytes 1638400 | tf_op jit(solution)/shard_map/reduce_scatter | solution.py:63
  497.5 125.0 %reduce-scatter.11.cloned.1.call-start = ((), (), s32[]{:S(2)}) async-start(), calls=%async_computation.8 | async-start | bytes 3276800 | tf_op jit(solution)/shard_map/reduce_scatter | solution.py:63
  504.8 140.9 %reduce-scatter.15.cloned.1.call-start = ((), (), s32[]{:S(2)}) async-start(), calls=%async_computation.10 | async-start | bytes 7864320 | tf_op jit(solution)/shard_map/reduce_scatter | solution.py:63
  505.4 219.3 %reduce-scatter.7.cloned.1.call-start = ((), (), s32[]{:S(2)}) async-start(), calls=%async_computation.6 | async-start | bytes 5242880 | tf_op jit(solution)/shard_map/reduce_scatter | solution.py:973
  518.0 286.2 %reduce-scatter.9.cloned.1.call-start = ((), (), s32[]{:S(2)}) async-start(), calls=%async_computation.7 | async-start | bytes 5242880 | tf_op jit(solution)/shard_map/reduce_scatter | solution.py:998
  533.4 33.8 %copy-start.17 = (f32[640]{0:T(1024)S(1)}, f32[640]{0:T(1024)}, u32[]{:S(2)}) copy-start(f32[640]{0:T(1024)} %param.35) | copy-start | bytes 7684
  578.1 42.0 %copy-start.9 = (bf16[1536,256]{1,0:T(8,128)(2,1)S(1)}, bf16[1536,256]{1,0:T(8,128)(2,1)}, u32[]{:S(2)}) copy-start(bf16[1536,256]{1,0:T(8,128)(2,1)} %reduce-scatter.17.cloned.1.call-done) | copy-start | bytes 2359300
  578.1 42.0 %collective-permute-start.11 = (bf16[1536,256]{1,0:T(8,128)(2,1)}, bf16[1536,256]{1,0:T(8,128)(2,1)S(1)}, u32[]{:S(2)}, u32[]{:S(2)}) collective-permute-start(bf16[1536,256]{1,0:T(8,128)(2,1)} %reduce-scatter.17.cloned.1.call-done), channel_id=1, source_target_pairs={{0,4},{4,0},{1,5},{5,1},{2,6},{6,2},{3,7},{7,3},{8,12},{12,8},{9,1... | collective-permute-start | bytes 2359304 | tf_op jit(solution)/shard_map/ppermute | solution.py:20
  620.2 2.7 collective-permute-start.9
  622.4 181.7 %copy-start.6 = (f32[1024,512]{1,0:T(8,128)S(1)}, f32[1024,512]{1,0:T(8,128)}, u32[]{:S(2)}) copy-start(f32[1024,512]{1,0:T(8,128)} %get-tuple-element.67) | copy-start | bytes 6291460
  622.5 185.7 %collective-permute-start.7 = (bf16[256,1280]{1,0:T(8,128)(2,1)}, bf16[256,1280]{1,0:T(8,128)(2,1)S(1)}, u32[]{:S(2)}, u32[]{:S(2)}) collective-permute-start(bf16[256,1280]{1,0:T(8,128)(2,1)} %reduce-scatter.11.cloned.1.call-done), channel_id=1, source_target_pairs={{0,4},{4,0},{1,5},{5,1},{2,6},{6,2},{3,7},{7,3},{8,12},{12,8},{9,1... | collective-permute-start | bytes 1966088 | tf_op jit(solution)/shard_map/ppermute | solution.py:20
  645.7 164.4 %collective-permute-start.10 = (bf16[256,3072]{1,0:T(8,128)(2,1)}, bf16[256,3072]{1,0:T(8,128)(2,1)}, u32[]{:S(2)}, u32[]{:S(2)}) collective-permute-start(bf16[256,3072]{1,0:T(8,128)(2,1)} %reduce-scatter.15.cloned.1.call-done), channel_id=1, source_target_pairs={{0,4},{4,0},{1,5},{5,1},{2,6},{6,2},{3,7},{7,3},{8,12},{12,8},{9,1... | collective-permute-start | bytes 4718600 | tf_op jit(solution)/shard_map/ppermute | solution.py:20
  (30 other events, 256.2 us)
Sparse Core Ops, SparseCore 0:
  284.6 42.2 reduce-scatter.16
  497.6 28.5 reduce-scatter.12
  529.8 41.9 reduce-scatter.10
  574.6 71.0 reduce-scatter.14
  647.9 76.7 reduce-scatter.6
  726.8 77.2 reduce-scatter.8
Sparse Core Ops, SparseCore 1:
  492.5 66.3 all-reduce.3

commit v3 on v2

--- a/solution.py
+++ b/solution.py
@@ -59,8 +59,11 @@
     return (product(0) + arrived.astype(F32)).astype(BF16)
 
 
-def to_owners(mine, dim):
-    total = lax.psum_scatter(mine, "fsdp", scatter_dimension=dim, tiled=True)
+def half_to_owners(mine, dim):
+    return lax.psum_scatter(mine, "fsdp", scatter_dimension=dim, tiled=True)
+
+
+def both_halves(total, dim):
     other = swap_cores(total)
     core = lax.axis_index("ctx")
     first = jnp.where(core == 0, total, other)
@@ -281,11 +284,12 @@
 
 
 CHUNK = 32
+LINE_COST = pl.CostEstimate(flops=0, bytes_accessed=400_000_000, transcendentals=0)
 
 
 def enter_kernel(
-    tokens, gain_shard, recur, gelu, merge,
-    normed, halves, gains, whole_in, whole_merge,
+    tokens, upstream, gain_shard, recur, gelu, merge,
+    normed, halves, upstream_halves, gains, whole_in, whole_merge,
     stage_recur, stage_gelu, stage_merge, send, arrive, local, gain_send, gain_arrive,
 ):
     square = Square()
@@ -315,6 +319,7 @@
         block = (block * rms_scale(block) * gains[0:1, :]).astype(BF16)
         normed[rows, :] = block
         put_split(halves, rows, block)
+        put_split(upstream_halves, rows, upstream[rows, :])
         return carry
 
     lax.fori_loop(0, tokens.shape[0] // CHUNK, norm, 0)
@@ -338,7 +343,7 @@
     return [pltpu.VMEM(w.shape, w.dtype) for w in shards] + [dma((count, 7)), dma((count, 7)), dma((count, 2))]
 
 
-def enter(tokens, gain_shard, recur, gelu, merge):
+def enter(tokens, upstream, gain_shard, recur, gelu, merge):
     rows, features = tokens.shape
     shape = jax.ShapeDtypeStruct
     inner = recur.shape[1]
@@ -348,16 +353,17 @@
         out_shape=(
             shape((rows, features), BF16),
             shape((2, rows, features // 2), BF16),
+            shape((2, rows, features // 2), BF16),
             shape((8, features), F32),
             shape((features, 2 * inner), BF16),
             shape((inner, features), BF16),
         ),
-        in_specs=[NEAR, NEAR, ANY, ANY, ANY],
-        out_specs=[NEAR, NEAR, NEAR, ANY, ANY],
+        in_specs=[NEAR, NEAR, NEAR, ANY, ANY, ANY],
+        out_specs=[NEAR, NEAR, NEAR, NEAR, ANY, ANY],
         scratch_shapes=gather_scratch([recur, gelu, merge]) + [dma((3,)), dma((3,))],
         compiler_params=pltpu.CompilerParams(collective_id=1, has_side_effects=True),
         name="enter",
-    )(tokens, gain_shard, recur, gelu, merge)
+    )(tokens, upstream, gain_shard, recur, gelu, merge)
 
 
 def line_scratch(rows, features):
@@ -428,6 +434,7 @@
         out_specs=specs,
         scratch_shapes=scratch,
         compiler_params=pltpu.CompilerParams(collective_id=2, has_side_effects=True),
+        cost_estimate=LINE_COST,
         name="middle",
     )(part, tokens, gains, *shards)
 
@@ -478,6 +485,7 @@
         scratch_shapes=[pltpu.VMEM((rows, features), BF16), pltpu.VMEM((CHUNK, features), F32)]
         + line_scratch(rows, features),
         compiler_params=pltpu.CompilerParams(collective_id=3, has_side_effects=True),
+        cost_estimate=LINE_COST,
         name="turn",
     )(part, tokens, merged, upstream, gains)
 
@@ -909,7 +917,9 @@
         [jnp.stack([norm_mix, norm_feed]).astype(F32), jnp.zeros((6, norm_mix.shape[0]), F32)], axis=0
     )
     if square:
-        normed, normed_split, gains, whole_in, whole_merge = enter(tokens, gain_shard, w_recur, w_gelu, w_merge)
+        normed, normed_split, cotangent_split, gains, whole_in, whole_merge = enter(
+            tokens, cotangent, gain_shard, w_recur, w_gelu, w_merge
+        )
     else:
         whole_in = gather_halves(jnp.concatenate([w_recur, w_gelu], axis=1), 0)
         whole_merge = gather_halves(w_merge, 1)
@@ -917,6 +927,7 @@
         inputs = tokens.astype(F32)
         normed = (inputs * rms_scale(inputs) * gains[0:1]).astype(BF16)
         normed_split = split_features(normed)
+        cotangent_split = split_features(cotangent)
     gain_one = gains[0:1]
 
     padded_ids = jnp.concatenate([jnp.full((edge,), -1, jnp.int32), segments])
@@ -949,7 +960,6 @@
         normed_two_split = split_features(normed_two)
         whole_mid = gather_halves(jnp.concatenate([w_gate, w_up], axis=1), 0)
         whole_down = gather_halves(w_down, 1)
-    cotangent_split = split_features(cotangent)
 
     units = w_gate.shape[1]
     pre_mid = jnp.dot(normed_two, whole_mid, preferred_element_type=F32).astype(BF16)
@@ -968,17 +978,13 @@
     turned = turn(part_two, tokens, merged, cotangent, gains, square)
     own_resid_grad, d_merge_in, feed_sums = turned[:3]
     d_merge_split = turned[3] if square else split_features(d_merge_in)
-    grad_feed = feed_sums[0]
-
-    feed = lax.psum_scatter(
-        jnp.dot(after(hidden, d_merge_in), whole_down, preferred_element_type=F32).astype(BF16),
-        "tp",
-        scatter_dimension=1,
-        tiled=True,
-    ).astype(F32)
-    shard_down = to_owners(pair_down, 1)
-    shard_mid = to_owners(pair_mid, 0)
-
+    half_down = half_to_owners(pair_down, 1)
+    half_mid = half_to_owners(pair_mid, 0)
+    d_merge_in = after(d_merge_in, half_down, half_mid)
+
+    part_feed = jnp.dot(after(hidden, d_merge_in), whole_down, preferred_element_type=F32).astype(BF16)
+    feed = lax.psum_scatter(part_feed, "tp", scatter_dimension=1, tiled=True)
+    d_merge_in = after(d_merge_in, part_feed)
     d_gated = lax.dot_general(d_merge_in, whole_merge, rows_to_features, preferred_element_type=F32)
     local_grad, grad_run, first, d_gelu_pre = recur_adjoint(rate, d_gated, branches, states, masks, softer)
     grad_in = shifted(first, "ctx", -1)[0:1]
@@ -987,34 +993,45 @@
         halo, taps, gates, softer
     )
     returned = shifted(head, "ctx", -1)
-    shard_merge = to_owners(pair_sums(d_merge_split, after(gated, back), 1), 1)
     d_in = lax.dynamic_update_slice(back, (tail + returned).astype(BF16), (piece - 8, 0))
-
+    part_one = lax.dot_general(d_in, whole_in, rows_to_features, preferred_element_type=F32).astype(BF16)
+    part_one = after(part_one, feed)
+    d_normed = lax.psum_scatter(part_one, "tp", scatter_dimension=1, tiled=True)
+
+    pair_merge = pair_sums(d_merge_split, after(gated, part_one), 1)
+    pair_in = pair_sums(normed_split, after(d_in, part_one), 0)
+    half_in = half_to_owners(after(pair_in, d_normed), 0)
+    half_merge = half_to_owners(after(pair_merge, d_normed), 1)
     inputs = tokens.astype(F32)
     scale_one = rms_scale(inputs)
-    part_one = lax.dot_general(d_in, whole_in, rows_to_features, preferred_element_type=F32)
-    stat_one = jnp.sum(part_one * inputs * gain_one, axis=-1)
-    grad_mix = jnp.sum(part_one * inputs * scale_one, axis=0)
-    d_normed = lax.psum_scatter(
-        part_one.astype(BF16), "tp", scatter_dimension=1, tiled=True
-    ).astype(F32)
-    stat_one = lax.psum(stat_one, "tp")[:, None] / features
-    shard_in = to_owners(pair_sums(normed_split, d_in, 0), 0)
+    wide_part = part_one.astype(F32)
+    stat_one = jnp.sum(wide_part * inputs * gain_one, axis=-1)
+    grad_mix = jnp.sum(wide_part * inputs * scale_one, axis=0)
+    norm_sums = jnp.stack([grad_mix, feed_sums[0] / lax.axis_size("tp")])
+    lines = -(-norm_sums.size // chans)
+    flat = jnp.pad(norm_sums.reshape(-1), (0, lines * chans - norm_sums.size)).reshape(lines, chans)
+    row_sums = lax.psum(jnp.concatenate([sums, flat], axis=0), ("fsdp", "ctx"))
+    norm_sums = row_sums[sums.shape[0] :].reshape(-1)[: norm_sums.size]
+    line_sums = lax.psum(jnp.concatenate([stat_one, norm_sums]), "tp")
+    stat_one = line_sums[:piece][:, None] / features
+    both_norms = line_sums[piece:].reshape(2, features)
+
+    shard_down = both_halves(half_down, 1)
+    shard_mid = both_halves(half_mid, 0)
+    shard_merge = both_halves(half_merge, 1)
+    shard_in = both_halves(half_in, 0)
 
     def own(block):
         return lax.dynamic_slice_in_dim(block, feat_start, feat_local, 1)
 
     own_inputs = own(inputs)
-    output = (own_inputs + own(merged).astype(F32) + feed).astype(BF16)
+    output = (own_inputs + own(merged).astype(F32) + feed.astype(F32)).astype(BF16)
     grad_tokens = (
         own_resid_grad
-        + scale_one * d_normed * own(gain_one)
+        + scale_one * d_normed.astype(F32) * own(gain_one)
         - own_inputs * scale_one**3 * stat_one
     ).astype(BF16)
 
-    both_norms = lax.psum(
-        jnp.stack([grad_mix, grad_feed / lax.axis_size("tp")]), ("fsdp", "ctx", "tp")
-    )
     norm_local = norm_mix.shape[0]
     own_norms = lax.dynamic_slice_in_dim(both_norms, lax.axis_index("fsdp") * norm_local, norm_local, 1)
 
@@ -1024,7 +1041,6 @@
         for i in range(heads)
     ]
     gate_sums = lax.psum(jnp.stack(diagonal).astype(BF16), ("fsdp", "ctx")).astype(F32)
-    row_sums = lax.psum(sums, ("fsdp", "ctx"))
     return (
         output,
         grad_tokens,

time: 830 us -> 751 us (0.905)
  waiting for transfers between devices: 183 us -> 144 us
  blocking collectives: 74.4 us -> 42.2 us
    reduce_scatter x6, waiting for transfers between devices: 180 us -> 99.7 us  [the longest x1 63.7 us: shards(): d_normed = lax.psum_scatter(part_one, 'tp', scatter_dimension=1, tiled=True)]
    psum x1, waiting for transfers between devices: 0.01 us -> 36.3 us  [shards(): lax.psum(jnp.stack(diagonal).astype(BF16), ('fsdp', 'ctx')).astype(F32)]
    psum x3 -> x2, blocking collectives: 74.4 us -> 42.2 us  [the longest x1 23.2 us: shards(): row_sums = lax.psum(jnp.concatenate([sums, flat], axis=0), ('fsdp', 'ctx'))]
  transfers between devices with their start and end apart: 19 -> 19, of which waited for: 4 -> 8; matrix products, arithmetic and copies ran while one was open for 17% -> 16% of each run, Pallas kernels for 18% -> 20%
where the time goes in v3:
time: 751 us; the launch traced here: 745 us
  Pallas kernels  341 us (45%)
  waiting for transfers between devices  144 us (19%)
  matrix products  142 us (19%)
  blocking collectives  42.2 us (6%)
  other arithmetic  29.7 us (4%)
  local copies, waits for them, and re-layouts  23.3 us (3%)
  between operations  15.3 us (2%)
  starting transfers between devices  7.78 us (1%)
    pallas_call x1, Pallas kernels, middle(): pl.pallas_call(lambda *refs: middle_kernel(bool(shards), *refs), out_shap...  120 us
    pallas_call x1, Pallas kernels, turn(): pl.pallas_call(lambda *refs: turn_kernel(split, *refs), out_shape=tuple(o...  118 us
    reduce_scatter x1, waiting for transfers between devices, shards(): d_normed = lax.psum_scatter(part_one, 'tp', scatter_dimension=1, tiled=True)  63.7 us
    dot_general x8, matrix products, product(): return lax.dot_general(*pair, rows_to_rows, preferred_element_type=F32)  53 us
    pallas_call x1, Pallas kernels, enter(): pl.pallas_call(enter_kernel, out_shape=(shape((rows, features), BF16), sh...  47.5 us
    psum x1, waiting for transfers between devices, shards(): lax.psum(jnp.stack(diagonal).astype(BF16), ('fsdp', 'ctx')).astype(F32)  36.3 us
    psum x1, blocking collectives, shards(): row_sums = lax.psum(jnp.concatenate([sums, flat], axis=0), ('fsdp', 'ctx'))  23.2 us
    pallas_call x1, Pallas kernels, recur_backward(): pl.pallas_call(backward_kernel, grid=(count,), out_shape=(jax.ShapeDtypeS...  19 us
  transfers between devices with their start and end apart: 19, of which 8 were waited for; matrix products, arithmetic and copies ran while one was open for 16% of the time, Pallas kernels for 20%

profile of v3, /device:TPU:0, one launch (start us, length us, event | category | flops | bytes accessed | tf_op | source)
XLA Modules:
  0.0 745.2 jit_solution(15655230431271178153)
XLA Ops:
  9.2 47.5 %enter.1 = (bf16[1024,2048]{1,0:T(8,128)(2,1)}, bf16[2,1024,1024]{2,1,0:T(8,128)(2,1)}, bf16[2,1024,1024]{2,1,0:T(8,128)(2,1)}, f32[8,2048]{1,0:T(8,128)}, bf16[...) custom-call(bf16[1024,2048]{1,0:T(8,128)(2,1)} %refs_1_.3, bf16[1024,2048]{1,0:T(8,128)(2,1)} %refs_3_.3, ...), custom_call_target="tpu_custom_call" | custom-call | tf_op jit(solution)/shard_map/enter/pallas_call | solution.py:351
  56.8 9.0 %convolution_convert_fusion.5.branch_ref.pre_ref = bf16[1024,1280]{1,0:T(8,128)(2,1)S(1)} fusion(bf16[1024,2048]{1,0:T(8,128)(2,1)} %get-tuple-element.59, bf16[2048,1280]{1,0:T(8,128)(2,1)} %get-tuple-element.60), kind=kOutput, calls=%fused_computation.35 | convolution fusion | flops 5370019840 | bytes 12058624 | tf_op jit(solution)/shard_map/dot_general | solution.py:946
  73.4 14.3 %recur_forward.1 = (bf16[1024,640]{1,0:T(8,128)(2,1)}, f32[1024,640]{1,0:T(8,128)}, f32[1024,640]{1,0:T(8,128)}, f32[1024,640]{1,0:T(8,128)}, f32[1024,640]{1,0:T(8,128)}, /*index=5*/bf16[640,1280]{1,0:T(8,128)(2,1)}) custom-call(bf16[1024,1280]{1,0:T(8,128)(2,1)} %copy-done.1, bf16[8,640]{1,0:T(8,128)(2,1)} %copy-done.17, ...), custom_call_target="tpu_custom_call" | custom-call | flops 1677721600 | bytes 15728640 | tf_op jit(solution)/shard_map/recur_forward/pallas_call | solution.py:633
  91.1 10.7 %merge_states.1 = (f32[1024,640]{1,0:T(8,128)}, bf16[1024,640]{1,0:T(8,128)(2,1)}, bf16[1024,2048]{1,0:T(8,128)(2,1)}) custom-call(f32[1024,640]{1,0:T(8,128)} %get-tuple-element.61.local_ref, f32[1024,640]{1,0:T(8,128)} %get-tuple-element.62.run_ref, f32[1,640]{1,0:T(1,128)} %slice.190.enter_ref, bf16[1024,1280]{1,0:T(8,128)(2,1)} %copy-done.1, ...), custom_call_target="tpu_custom_call" | custom-call | flops 2684354560 | bytes 10485760 | tf_op jit(solution)/shard_map/merge_states/pallas_call | solution.py:679
  101.8 119.9 %middle.1 = (bf16[1024,2048]{1,0:T(8,128)(2,1)}, bf16[1024,2048]{1,0:T(8,128)(2,1)}, bf16[2,1024,1024]{2,1,0:T(8,128)(2,1)}, bf16[2048,3072]{1,0:T(8,128)(2,1)}, bf16[1536,2048]{1,0:T(8,128)(2,1)}) custom-call(bf16[1024,2048]{1,0:T(8,128)(2,1)} %get-tuple-element.64.refs_0_, bf16[1024,2048]{1,0:T(8,128)(2,1)} %refs_1_.3, ...), custom_call_target="tpu_custom_call" | custom-call | bytes 400000000 | tf_op jit(solution)/shard_map/middle/pallas_call | solution.py:430
  221.7 18.5 %convolution_convert_fusion.1 = bf16[1024,3072]{1,0:T(8,128)(2,1)} fusion(bf16[1024,2048]{1,0:T(8,128)(2,1)} %get-tuple-element.67, bf16[2048,3072]{1,0:T(8,128)(2,1)} %get-tuple-element.68), kind=kOutput, calls=%fused_computation.30 | convolution fusion | flops 12888047616 | bytes 23068672 | tf_op jit(solution)/shard_map/dot_general | solution.py:965
  240.2 14.3 %fusion.6 = (bf16[1024,1536]{1,0:T(8,128)(2,1)S(1)}, bf16[1024,1536]{1,0:T(8,128)(2,1)S(1)}, bf16[1024,1536]{1,0:T(8,128)(2,1)}) fusion(bf16[1024,3072]{1,0:T(8,128)(2,1)} %convolution_convert_fusion.1, bf16[1536,2048]{1,0:T(8,128)(2,1)S(1)} %copy-done.23, bf16[1024,2048]{1,0:T(8,128)(2,1)S(1)} %copy-done.3), kind=kOutput, calls=%fused_computation.20 | convolution fusion | flops 6488064000 | bytes 26214400 | tf_op jit(solution)/shard_map/dot_general | solution.py:966
  254.5 6.8 convolution_convert_fusion.8
  261.4 9.4 %convolution_convert_fusion = bf16[1024,3072]{1,0:T(8,128)(2,1)} fusion(bf16[2,1024,1024]{2,1,0:T(8,128)(2,1)S(1)} %copy-done.27, bf16[1024,1536]{1,0:T(8,128)(2,1)S(1)} %get-tuple-element.108, bf16[1024,1536]{1,0:T(8,128)(2,1)S(1)} %get-tuple-element.107), kind=kOutput, calls=%fused_computation.29 | convolution fusion | flops 6458179584 | bytes 14680064 | tf_op jit(solution)/shard_map/dot_general | solution.py:56
  281.4 12.2 %add_convert_fusion = bf16[1024,3072]{1,0:T(8,128)(2,1)} fusion(bf16[1024,3072]{1,0:T(8,128)(2,1)} %collective-permute-done.3, bf16[2,1024,1024]{2,1,0:T(8,128)(2,1)} %get-tuple-element.71, bf16[1024,1536]{1,0:T(8,128)(2,1)} %copy-done.32, bf16[1024,1536]{1,0:T(8,128)(2,1)S(1)} %get-tuple-element.107), kind=kOutput, calls=%fused_computation.7 | convolution fusion | flops 6464471040 | bytes 20971520 | tf_op jit(solution)/shard_map/dot_general | solution.py:56
  293.6 18.9 %convolution_convert_fusion.2.refs_0_ = bf16[1024,2048]{1,0:T(8,128)(2,1)} fusion(bf16[2048,3072]{1,0:T(8,128)(2,1)} %get-tuple-element.68, bf16[1024,1536]{1,0:T(8,128)(2,1)} %copy-done.32, bf16[1024,1536]{1,0:T(8,128)(2,1)S(1)} %get-tuple-element.107), kind=kOutput, calls=%fused_computation.32 | convolution fusion | flops 12899581952 | bytes 23068672 | tf_op jit(solution)/shard_map/dot_general | solution.py:974
  312.5 117.9 %turn.1 = (f32[1024,512]{1,0:T(8,128)}, bf16[1024,2048]{1,0:T(8,128)(2,1)}, f32[8,2048]{1,0:T(8,128)}, bf16[2,1024,1024]{2,1,0:T(8,128)(2,1)}) custom-call(bf16[1024,2048]{1,0:T(8,128)(2,1)} %convolution_convert_fusion.2.refs_0_, bf16[1024,2048]{1,0:T(8,128)(2,1)} %refs_1_.3, bf16[1024,2048]{1,0:T(8,128)(2,1)} %get-tuple-element.66.refs_2_, ...), custom_call_target="tpu_custom_call" | custom-call | bytes 400000000 | tf_op jit(solution)/shard_map/turn/pallas_call | solution.py:480
  430.5 11.0 %convolution_convert_fusion.3 = bf16[1024,2048]{1,0:T(8,128)(2,1)} fusion(bf16[1024,1536]{1,0:T(8,128)(2,1)S(1)} %copy-done.33, bf16[1536,2048]{1,0:T(8,128)(2,1)} %get-tuple-element.69), kind=kOutput, calls=%fused_computation.33 | convolution fusion | flops 6444548096 | bytes 13631488 | tf_op jit(solution)/shard_map/dot_general | solution.py:985
  443.3 7.1 fusion.68.up_ref
  450.4 11.7 %recur_adjoint.1 = (f32[1024,640]{1,0:T(8,128)}, f32[1024,640]{1,0:T(8,128)}, f32[8,640]{1,0:T(8,128)}, bf16[1024,640]{1,0:T(8,128)(2,1)}) custom-call(f32[1024,640]{1,0:T(8,128)} %get-tuple-element.77.rate_ref, f32[1024,640]{1,0:T(8,128)} %fusion.68.up_ref, bf16[1024,1280]{1,0:T(8,128)(2,1)} %copy-done.1, f32[1024,640]{1,0:T(8,128)} %get-tuple-element.79.state_ref, ...), custom_call_target="tpu_custom_call" | custom-call | flops 5242880 | bytes 10485760 | tf_op jit(solution)/shard_map/recur_adjoint/pallas_call | solution.py:733
  466.0 19.0 %recur_backward.1 = (bf16[1024,1280]{1,0:T(8,128)(2,1)}, f32[8,640]{1,0:T(8,128)}, f32[8,640]{1,0:T(8,128)}, f32[640,1280]{1,0:T(8,128)}, f32[16,640]{1,0:T(8,128)}) custom-call(f32[1024,640]{1,0:T(8,128)} %get-tuple-element.80.grad_ref, f32[1024,640]{1,0:T(8,128)} %get-tuple-element.81.run_ref, f32[1,640]{1,0:T(1,128)} %slice.193.enter_ref, ...), custom_call_target="tpu_custom_call" | custom-call | flops 3355443200 | bytes 18350080 | tf_op jit(solution)/shard_map/recur_backward/pallas_call | solution.py:848
  489.6 10.1 %convolution_convert_fusion.6 = bf16[1024,2048]{1,0:T(8,128)(2,1)} fusion(bf16[1024,1280]{1,0:T(8,128)(2,1)} %fusion.54, bf16[2048,1280]{1,0:T(8,128)(2,1)} %get-tuple-element.60), kind=kOutput, calls=%fused_computation.36 | convolution fusion | flops 5370806272 | bytes 12058624 | tf_op jit(solution)/shard_map/dot_general | solution.py:997
  499.7 17.2 %reduce-scatter.11.cloned.1.call-done = bf16[1024,512]{1,0:T(8,128)(2,1)} async-done(((bf16[1024,2048]{1,0:T(8,128)(2,1)}), bf16[1024,512]{1,0:T(8,128)(2,1)}) %reduce-scatter.11.cloned.1.call-update) | async-done | bytes 1048592 | tf_op jit(solution)/shard_map/reduce_scatter | solution.py:986
  532.7 63.7 %reduce-scatter.13.cloned.1.call-done = bf16[1024,512]{1,0:T(8,128)(2,1)} async-done(((bf16[1024,2048]{1,0:T(8,128)(2,1)}), bf16[1024,512]{1,0:T(8,128)(2,1)}) %reduce-scatter.13.cloned.1.call-update) | async-done | bytes 1048592 | tf_op jit(solution)/shard_map/reduce_scatter | solution.py:999
  608.2 6.8 add_convert_fusion.2
  619.5 36.3 %all-reduce.5.cloned.1.call-done = bf16[8,160,160]{2,1,0:T(8,128)(2,1)} async-done(((bf16[8,160,160]{2,1,0:T(8,128)(2,1)}), bf16[8,160,160]{2,1,0:T(8,128)(2,1)}) %all-reduce.5.cloned.1.call-update) | async-done | bytes 409616 | tf_op jit(solution)/shard_map/psum | solution.py:1043
  667.5 23.2 %psum.21 = f32[23,640]{1,0:T(8,128)S(1)} all-reduce(f32[23,640]{1,0:T(8,128)S(1)} %pad_maximum_fusion.5), channel_id=1, replica_groups=mesh['fsdp'=4,'ctx'=2,'tp'=4] {'fsdp','ctx'}, use_global_device_ids=true, to_apply=%region_7.8 | all-reduce | flops 14720 | bytes 117760 | tf_op jit(solution)/shard_map/psum | solution.py:1013
  691.3 19.0 %psum.22 = f32[5120]{0:T(1024)S(1)} all-reduce(f32[5120]{0:T(1024)S(1)} %pad_maximum_fusion.6), channel_id=1, replica_groups=mesh['fsdp'=4,'ctx'=2,'tp'=4] {'tp'}, use_global_device_ids=true, to_apply=%region_8.9 | all-reduce | flops 5120 | bytes 40960 | tf_op jit(solution)/shard_map/psum | solution.py:1015
  712.2 18.7 %reduce-scatter.15.cloned.1.call-done = bf16[256,1280]{1,0:T(8,128)(2,1)} async-done(((bf16[1024,1280]{1,0:T(8,128)(2,1)}), bf16[256,1280]{1,0:T(8,128)(2,1)}) %reduce-scatter.15.cloned.1.call-update) | async-done | bytes 655376 | tf_op jit(solution)/shard_map/reduce_scatter | solution.py:63
  (180 shorter events, 86.8 us)
Async XLA Ops:
  7.2 423.3 %reduce-scatter.7.cloned.1.call-start = ((), (), s32[]{:S(2)}) async-start(), calls=%async_computation.6 | async-start | bytes 3932160 | tf_op jit(solution)/shard_map/reduce_scatter | solution.py:63
  65.8 7.0 collective-permute-start
  88.5 2.1 collective-permute-start.1
  221.7 18.5 %copy-start.3 = (bf16[1024,2048]{1,0:T(8,128)(2,1)S(1)}, bf16[1024,2048]{1,0:T(8,128)(2,1)}, u32[]{:S(2)}) copy-start(bf16[1024,2048]{1,0:T(8,128)(2,1)} %refs_3_.3) | copy-start | bytes 12582916
  261.3 10.0 %collective-permute-start.2 = (bf16[1536,1024]{1,0:T(8,128)(2,1)S(1)}, bf16[1536,1024]{1,0:T(8,128)(2,1)S(1)}, u32[]{:S(2)}, u32[]{:S(2)}) collective-permute-start(bf16[1536,1024]{1,0:T(8,128)(2,1)S(1)} %convolution_convert_fusion.8), channel_id=1, source_target_pairs={{0,4},{4,0},{1,5},{5,1},{2,6},{6,2},{3,7},{7,3},{8,12},{12,8},{9,1... | collective-permute-start | bytes 9437192 | tf_op jit(solution)/shard_map/ppermute | solution.py:20
  270.8 10.6 %collective-permute-start.3 = (bf16[1024,3072]{1,0:T(8,128)(2,1)}, bf16[1024,3072]{1,0:T(8,128)(2,1)}, u32[]{:S(2)}, u32[]{:S(2)}) collective-permute-start(bf16[1024,3072]{1,0:T(8,128)(2,1)} %convolution_convert_fusion), channel_id=1, source_target_pairs={{0,4},{4,0},{1,5},{5,1},{2,6},{6,2},{3,7},{7,3},{8,12},{12,8},{9,1... | collective-permute-start | bytes 18874376 | tf_op jit(solution)/shard_map/ppermute | solution.py:20
  278.0 152.5 %reduce-scatter.9.cloned.1.call-start = ((), (), s32[]{:S(2)}) async-start(), calls=%async_computation.7 | async-start | bytes 7864320 | tf_op jit(solution)/shard_map/reduce_scatter | solution.py:63
  293.6 223.4 %reduce-scatter.11.cloned.1.call-start = ((), (), s32[]{:S(2)}) async-start(), calls=%async_computation.8 | async-start | bytes 5242880 | tf_op jit(solution)/shard_map/reduce_scatter | solution.py:986
  312.5 118.0 %copy-start.33 = (bf16[1024,1536]{1,0:T(8,128)(2,1)S(1)}, bf16[1024,1536]{1,0:T(8,128)(2,1)}, u32[]{:S(2)}) copy-start(bf16[1024,1536]{1,0:T(8,128)(2,1)} %get-tuple-element.75) | copy-start | bytes 9437188
  441.6 154.8 %reduce-scatter.13.cloned.1.call-start = ((), (), s32[]{:S(2)}) async-start(), calls=%async_computation.9 | async-start | bytes 5242880 | tf_op jit(solution)/shard_map/reduce_scatter | solution.py:999
  462.1 3.3 collective-permute-start.4
  485.0 3.3 collective-permute-start.5
  517.0 138.8 %all-reduce.5.cloned.1.call-start = ((), (), s32[]{:S(2)}) async-start(), calls=%async_computation.12 | async-start | bytes 1310720 | tf_op jit(solution)/shard_map/psum | solution.py:1043
  522.2 6.3 collective-permute-start.8
  527.4 80.8 %collective-permute-start.6 = (bf16[1024,1280]{1,0:T(8,128)(2,1)}, bf16[1024,1280]{1,0:T(8,128)(2,1)}, u32[]{:S(2)}, u32[]{:S(2)}) collective-permute-start(bf16[1024,1280]{1,0:T(8,128)(2,1)} %convolution_convert_fusion.7), channel_id=1, source_target_pairs={{0,4},{4,0},{1,5},{5,1},{2,6},{6,2},{3,7},{7,3},{8,12},{12,8},{9,1... | collective-permute-start | bytes 7864328 | tf_op jit(solution)/shard_map/ppermute | solution.py:20
  528.4 183.8 %reduce-scatter.17.cloned.1.call-start = ((), (), s32[]{:S(2)}) async-start(), calls=%async_computation.11 | async-start | bytes 1638400 | tf_op jit(solution)/shard_map/reduce_scatter | solution.py:63
  596.5 134.4 %reduce-scatter.15.cloned.1.call-start = ((), (), s32[]{:S(2)}) async-start(), calls=%async_computation.10 | async-start | bytes 3276800 | tf_op jit(solution)/shard_map/reduce_scatter | solution.py:63
  607.6 8.3 %collective-permute-start.11 = (bf16[1536,256]{1,0:T(8,128)(2,1)}, bf16[1536,256]{1,0:T(8,128)(2,1)}, u32[]{:S(2)}, u32[]{:S(2)}) collective-permute-start(bf16[1536,256]{1,0:T(8,128)(2,1)} %reduce-scatter.7.cloned.1.call-done), channel_id=1, source_target_pairs={{0,4},{4,0},{1,5},{5,1},{2,6},{6,2},{3,7},{7,3},{8,12},{12,8},{9,1... | collective-permute-start | bytes 2359304 | tf_op jit(solution)/shard_map/ppermute | solution.py:20
  607.7 50.3 %collective-permute-start.10 = (bf16[256,3072]{1,0:T(8,128)(2,1)S(1)}, bf16[256,3072]{1,0:T(8,128)(2,1)S(1)}, u32[]{:S(2)}, u32[]{:S(2)}) collective-permute-start(bf16[256,3072]{1,0:T(8,128)(2,1)S(1)} %copy-done.7), channel_id=1, source_target_pairs={{0,4},{4,0},{1,5},{5,1},{2,6},{6,2},{3,7},{7,3},{8,12},{12,8},{9,1... | collective-permute-start | bytes 4718600 | tf_op jit(solution)/shard_map/ppermute | solution.py:20
  664.8 46.8 %copy-start.16 = (f32[640]{0:T(1024)S(1)}, f32[640]{0:T(1024)}, u32[]{:S(2)}) copy-start(f32[640]{0:T(1024)} %param.35) | copy-start | bytes 7684
  664.8 66.1 %copy-start.6 = (f32[1024,512]{1,0:T(8,128)S(1)}, f32[1024,512]{1,0:T(8,128)}, u32[]{:S(2)}) copy-start(f32[1024,512]{1,0:T(8,128)} %get-tuple-element.76) | copy-start | bytes 6291460
  664.8 66.1 %copy-start.8 = (bf16[1024,512]{1,0:T(8,128)(2,1)S(1)}, bf16[1024,512]{1,0:T(8,128)(2,1)}, u32[]{:S(2)}) copy-start(bf16[1024,512]{1,0:T(8,128)(2,1)} %reduce-scatter.11.cloned.1.call-done) | copy-start | bytes 3145732
  712.2 22.4 %collective-permute-start.9 = (bf16[640,256]{1,0:T(8,128)(2,1)}, bf16[640,256]{1,0:T(8,128)(2,1)S(1)}, u32[]{:S(2)}, u32[]{:S(2)}) collective-permute-start(bf16[640,256]{1,0:T(8,128)(2,1)} %reduce-scatter.17.cloned.1.call-done), channel_id=1, source_target_pairs={{0,4},{4,0},{1,5},{5,1},{2,6},{6,2},{3,7},{7,3},{8,12},{12,8},{9,1... | collective-permute-start | bytes 983048 | tf_op jit(solution)/shard_map/ppermute | solution.py:20
  730.9 5.0 collective-permute-start.7
  (29 other events, 214.7 us)
Sparse Core Ops, SparseCore 0:
  278.1 41.9 reduce-scatter.6
  323.2 70.0 reduce-scatter.8
  441.7 75.1 reduce-scatter.10
  519.1 77.2 reduce-scatter.12
  600.0 55.7 all-reduce.4
  659.1 29.2 reduce-scatter.16
  691.4 39.4 reduce-scatter.14

commit v4 on v3

--- a/solution.py
+++ b/solution.py
@@ -157,7 +157,7 @@
         self.stage(w, True).wait()
 
 
-def greet(line, square):
+def greet(line, square, whole_line=False):
     barrier = pltpu.get_barrier_semaphore()
 
     def call(**device):
@@ -176,6 +176,14 @@
             call(tp=me + 1)
 
         peers = jnp.where((me > 0) & (me < count - 1), 2, 1)
+    if whole_line:
+        count, me = lax.axis_size("tp"), lax.axis_index("tp")
+        for other in range(count):
+            @pl.when(me != other)
+            def _():
+                call(tp=other)
+
+        peers = peers + (count - 1)
     if square:
         place = Square()
         call(fsdp=place.near[0])
@@ -488,6 +496,247 @@
         cost_estimate=LINE_COST,
         name="turn",
     )(part, tokens, merged, upstream, gains)
+
+
+def rounded_sum(*blocks):
+    total = blocks[0].astype(F32)
+    for block in blocks[1:]:
+        total = total + block.astype(F32)
+    return total.astype(BF16)
+
+
+class Scatter:
+    def __init__(self, items, boxes, lasts, send, arrive):
+        self.items, self.boxes, self.lasts = items, boxes, lasts
+        self.send, self.arrive = send, arrive
+        self.square = Square()
+
+    def block(self, w, owner, k):
+        part, _, dim = self.items[w]
+        size = part.shape[dim] // 4
+        if dim == 0:
+            low = pl.multiple_of(owner * size + k * (size // 2), 128)
+            return part.at[pl.ds(low, size // 2), :]
+        half = part.shape[0] // 2
+        return part.at[pl.ds(k * half, half), pl.ds(pl.multiple_of(owner * size, 128), size)]
+
+    def spot(self, w, k):
+        part, out, dim = self.items[w]
+        size = part.shape[dim] // 4
+        low = pl.multiple_of(self.square.core * size, 128)
+        if dim == 0:
+            return out.at[pl.ds(low + k * (size // 2), size // 2), :]
+        half = part.shape[0] // 2
+        return out.at[pl.ds(k * half, half), pl.ds(low, size)]
+
+    def copy(self, w, k, j):
+        square = self.square
+        first, second = square.near[k], square.near[1 - k]
+        send, arrive = self.send.at[w, 4 * k + j], self.arrive.at[w, 4 * k + j]
+        if j < 2:
+            owner = square.far if j == 0 else first
+            return remote(self.block(w, owner, k), self.boxes[w].at[k, j], send, arrive, fsdp=first)
+        if j == 2:
+            return remote(self.boxes[w].at[k, 0], self.lasts[w].at[k], send, arrive, fsdp=second)
+        return remote(self.spot(w, k), self.spot(w, k), send, arrive, ctx=1 - square.core)
+
+    def start(self, w):
+        for j in (0, 1):
+            for k in (0, 1):
+                self.copy(w, k, j).start()
+
+    def relay(self, w):
+        for k in (0, 1):
+            self.copy(w, k, 0).wait_recv()
+            mine = self.block(w, self.square.near[1 - k], k)
+            self.boxes[w][k, 0] = rounded_sum(mine[...], self.boxes[w][k, 0])
+            self.copy(w, k, 2).start()
+
+    def finish(self, w):
+        for k in (0, 1):
+            self.copy(w, k, 1).wait_recv()
+            self.copy(w, k, 2).wait_recv()
+            mine = self.block(w, self.square.me, k)
+            self.spot(w, k)[...] = rounded_sum(mine[...], self.boxes[w][k, 1], self.lasts[w][k])
+            self.copy(w, k, 3).start()
+
+    def drain(self, w):
+        for k in (0, 1):
+            self.copy(w, k, 3).wait_recv()
+            for j in range(4):
+                self.copy(w, k, j).wait_send()
+
+
+def scatter_scratch(items):
+    blocks = []
+    for shape, dim in items:
+        rows, cols = (shape[0] // 8, shape[1]) if dim == 0 else (shape[0] // 2, shape[1] // 4)
+        blocks.append((rows, cols))
+    dma = pltpu.SemaphoreType.DMA((len(items), 8))
+    return (
+        [pltpu.VMEM((2, 2, *block), BF16) for block in blocks]
+        + [pltpu.VMEM((2, *block), BF16) for block in blocks]
+        + [dma, dma]
+    )
+
+
+def leave_kernel(
+    part_in, part_merge, gates, sums, norms, stats,
+    own_in, own_merge, gate_sums, row_sums, norm_sums, stat_sums,
+    box_in, box_merge, last_in, last_merge, send, arrive,
+    gate_core, gate_half, gate_near, gate_pair, gate_far, gate_send, gate_arrive,
+    core_sums, core_norms, box_sums, box_norms, sum_send, sum_arrive,
+    line_norms, line_stats, norm_send, norm_arrive, stat_send, stat_arrive,
+):
+    square = Square()
+    count, place = lax.axis_size("tp"), lax.axis_index("tp")
+    core = square.core
+    others = (*square.near, square.far)
+    greet(False, True, True)
+
+    def norm_copy(k, source):
+        box = line_norms.at[source]
+        return remote(box, box, norm_send.at[k], norm_arrive.at[source], tp=k)
+
+    def stat_copy(k, source):
+        return remote(stats, line_stats.at[source], stat_send.at[k], stat_arrive.at[source], tp=k)
+
+    def core_copy(k):
+        source, target = ((sums, core_sums), (norms, core_norms))[k]
+        return remote(source, target, sum_send.at[k], sum_arrive.at[k], ctx=1 - core)
+
+    def square_copy(k, j):
+        box = (box_sums, box_norms)[k].at[square.me]
+        at = 2 + 3 * k + j
+        return remote(box, box, sum_send.at[at], sum_arrive.at[at], fsdp=others[j])
+
+    gate_rows = gates.shape[0] // 2
+    gate_cols = gates.shape[1] // 2
+    my_rows = pl.ds(pl.multiple_of(core * gate_rows, 16), gate_rows)
+    your_rows = pl.ds(pl.multiple_of((1 - core) * gate_rows, 16), gate_rows)
+
+    def gate_copy(j):
+        send, arrive = gate_send.at[j], gate_arrive.at[j]
+        if j == 0:
+            return remote(gates.at[your_rows, :], gate_core, send, arrive, ctx=1 - core)
+        if j == 5:
+            spot = gate_sums.at[my_rows, :]
+            return remote(spot, spot, send, arrive, ctx=1 - core)
+        k = (j - 1) % 2
+        if j < 3:
+            return remote(gate_half.at[k], gate_near.at[k], send, arrive, fsdp=square.near[k])
+        return remote(gate_pair.at[k], gate_far.at[k], send, arrive, fsdp=square.near[1 - k])
+
+    scatter = Scatter(
+        [(part_merge, own_merge, 1), (part_in, own_in, 0)], (box_merge, box_in), (last_merge, last_in), send, arrive
+    )
+    gate_copy(0).start()
+    core_copy(0).start()
+    core_copy(1).start()
+    for k in range(count):
+        @pl.when(place != k)
+        def _():
+            stat_copy(k, place).start()
+
+    line_stats[place] = stats[...]
+    core_copy(0).wait_recv()
+    core_copy(1).wait_recv()
+    box_sums[square.me] = sums[...] + core_sums[...]
+    box_norms[square.me] = norms[...] + core_norms[...]
+    for k in (0, 1):
+        for j in range(3):
+            square_copy(k, j).start()
+    gate_copy(0).wait_recv()
+    for k in (0, 1):
+        cols = slice(k * gate_cols, (k + 1) * gate_cols)
+        gate_half[k] = rounded_sum(gates[my_rows, cols], gate_core[:, cols])
+        gate_copy(1 + k).start()
+    scatter.start(0)
+    scatter.start(1)
+    for k in (0, 1):
+        for j in range(3):
+            square_copy(k, j).wait_recv()
+    row_sums[...] = box_sums[0] + box_sums[1] + box_sums[2] + box_sums[3]
+    line_norms[place] = box_norms[0] + box_norms[1] + box_norms[2] + box_norms[3]
+    for k in range(count):
+        @pl.when(place != k)
+        def _():
+            norm_copy(k, place).start()
+
+    for k in (0, 1):
+        gate_copy(1 + k).wait_recv()
+        gate_pair[k] = rounded_sum(gate_half[k], gate_near[k])
+        gate_copy(3 + k).start()
+    scatter.relay(0)
+    scatter.relay(1)
+    for k in (0, 1):
+        cols = slice(k * gate_cols, (k + 1) * gate_cols)
+        gate_copy(3 + k).wait_recv()
+        gate_sums[my_rows, cols] = rounded_sum(gate_pair[k], gate_far[k])
+    gate_copy(5).start()
+    for k in range(count):
+        @pl.when(place != k)
+        def _():
+            norm_copy(k, k).wait_recv()
+            stat_copy(k, k).wait_recv()
+
+    total = line_norms[0]
+    stat = line_stats[0]
+    for k in range(1, count):
+        total = total + line_norms[k]
+        stat = stat + line_stats[k]
+    norm_sums[...] = total
+    stat_sums[...] = stat
+    scatter.finish(0)
+    scatter.finish(1)
+    for w in (0, 1):
+        scatter.drain(w)
+    gate_copy(5).wait_recv()
+    for j in range(6):
+        gate_copy(j).wait_send()
+    for k in (0, 1):
+        core_copy(k).wait_send()
+        for j in range(3):
+            square_copy(k, j).wait_send()
+    for k in range(count):
+        @pl.when(place != k)
+        def _():
+            norm_copy(k, place).wait_send()
+            stat_copy(k, place).wait_send()
+
+
+def leave(part_in, part_merge, gates, sums, norms, stats):
+    shape = jax.ShapeDtypeStruct
+    count = lax.axis_size("tp")
+    dma = pltpu.SemaphoreType.DMA
+    height, width = gates.shape[0] // 2, gates.shape[1] // 2
+    quarter = pltpu.VMEM((2, height, width), BF16)
+    return pl.pallas_call(
+        leave_kernel,
+        out_shape=(
+            shape((part_in.shape[0] // 2, part_in.shape[1]), BF16),
+            shape((part_merge.shape[0], part_merge.shape[1] // 2), BF16),
+            shape(gates.shape, BF16),
+            shape(sums.shape, F32),
+            shape(norms.shape, F32),
+            shape(stats.shape, F32),
+        ),
+        in_specs=[NEAR] * 6,
+        out_specs=[NEAR] * 6,
+        scratch_shapes=(
+            (lambda boxes: [boxes[1], boxes[0], boxes[3], boxes[2], boxes[4], boxes[5]])(
+                scatter_scratch([(part_merge.shape, 1), (part_in.shape, 0)])
+            )
+            + [pltpu.VMEM((height, 2 * width), BF16), quarter, quarter, quarter, quarter, dma((6,)), dma((6,))]
+            + [pltpu.VMEM(sums.shape, F32), pltpu.VMEM(norms.shape, F32)]
+            + [pltpu.VMEM((4, *sums.shape), F32), pltpu.VMEM((4, *norms.shape), F32), dma((8,)), dma((8,))]
+            + [pltpu.VMEM((count, *norms.shape), F32), pltpu.VMEM((count, *stats.shape), F32)]
+            + [dma((count,))] * 4
+        ),
+        compiler_params=pltpu.CompilerParams(collective_id=4, has_side_effects=True),
+        cost_estimate=pl.CostEstimate(flops=0, bytes_accessed=160_000_000, transcendentals=0),
+        name="leave",
+    )(part_in, part_merge, gates, sums, norms, stats)
 
 
 def gelu_pair(q):
@@ -971,22 +1220,22 @@
     d_mid = jnp.concatenate(
         [(wide_hidden * up_vals * gate_slope).astype(BF16), (wide_hidden * gate_act).astype(BF16)], axis=1
     )
-    part_two = lax.dot_general(d_mid, whole_mid, rows_to_features, preferred_element_type=F32).astype(BF16)
+    part_feed = jnp.dot(hidden, whole_down, preferred_element_type=F32).astype(BF16)
+    feed = lax.psum_scatter(part_feed, "tp", scatter_dimension=1, tiled=True)
+    hidden = after(hidden, part_feed)
+    part_two = lax.dot_general(d_mid, after(whole_mid, part_feed), rows_to_features, preferred_element_type=F32).astype(BF16)
     pair_down = pair_sums(cotangent_split, hidden, 1)
-    pair_mid = pair_sums(normed_two_split, d_mid, 0)
+    pair_mid = pair_sums(after(normed_two_split, part_feed), d_mid, 0)
     part_two = after(part_two, pair_down, pair_mid)
     turned = turn(part_two, tokens, merged, cotangent, gains, square)
     own_resid_grad, d_merge_in, feed_sums = turned[:3]
     d_merge_split = turned[3] if square else split_features(d_merge_in)
     half_down = half_to_owners(pair_down, 1)
     half_mid = half_to_owners(pair_mid, 0)
-    d_merge_in = after(d_merge_in, half_down, half_mid)
-
-    part_feed = jnp.dot(after(hidden, d_merge_in), whole_down, preferred_element_type=F32).astype(BF16)
-    feed = lax.psum_scatter(part_feed, "tp", scatter_dimension=1, tiled=True)
-    d_merge_in = after(d_merge_in, part_feed)
+    d_merge_in = after(d_merge_in, half_down, feed)
+
     d_gated = lax.dot_general(d_merge_in, whole_merge, rows_to_features, preferred_element_type=F32)
-    local_grad, grad_run, first, d_gelu_pre = recur_adjoint(rate, d_gated, branches, states, masks, softer)
+    local_grad, grad_run, first, d_gelu_pre = recur_adjoint(after(rate, half_mid), d_gated, branches, states, masks, softer)
     grad_in = shifted(first, "ctx", -1)[0:1]
     back, tail, head, gate_grads, sums = recur_backward(
         local_grad, grad_run, grad_in, rate, entry, conv, states, masks, branches, d_gelu_pre,
@@ -995,36 +1244,42 @@
     returned = shifted(head, "ctx", -1)
     d_in = lax.dynamic_update_slice(back, (tail + returned).astype(BF16), (piece - 8, 0))
     part_one = lax.dot_general(d_in, whole_in, rows_to_features, preferred_element_type=F32).astype(BF16)
-    part_one = after(part_one, feed)
     d_normed = lax.psum_scatter(part_one, "tp", scatter_dimension=1, tiled=True)
 
     pair_merge = pair_sums(d_merge_split, after(gated, part_one), 1)
     pair_in = pair_sums(normed_split, after(d_in, part_one), 0)
-    half_in = half_to_owners(after(pair_in, d_normed), 0)
-    half_merge = half_to_owners(after(pair_merge, d_normed), 1)
     inputs = tokens.astype(F32)
     scale_one = rms_scale(inputs)
     wide_part = part_one.astype(F32)
     stat_one = jnp.sum(wide_part * inputs * gain_one, axis=-1)
     grad_mix = jnp.sum(wide_part * inputs * scale_one, axis=0)
     norm_sums = jnp.stack([grad_mix, feed_sums[0] / lax.axis_size("tp")])
-    lines = -(-norm_sums.size // chans)
-    flat = jnp.pad(norm_sums.reshape(-1), (0, lines * chans - norm_sums.size)).reshape(lines, chans)
-    row_sums = lax.psum(jnp.concatenate([sums, flat], axis=0), ("fsdp", "ctx"))
-    norm_sums = row_sums[sums.shape[0] :].reshape(-1)[: norm_sums.size]
-    line_sums = lax.psum(jnp.concatenate([stat_one, norm_sums]), "tp")
-    stat_one = line_sums[:piece][:, None] / features
-    both_norms = line_sums[piece:].reshape(2, features)
-
+    spread = jnp.arange(2 * chans)[None, :] % chans // block
+    diagonal = sum(jnp.where(spread == i, gate_grads[i * block : (i + 1) * block], 0.0) for i in range(heads))
+    diagonal = diagonal.astype(BF16)
+    if square:
+        norm_sums = jnp.pad(norm_sums, ((0, 6), (0, 0)))
+        own_in, own_merge, gate_sums, row_sums, both_norms, line_stats = leave(
+            pair_in, pair_merge, diagonal, sums, norm_sums, stat_one.reshape(-1, 128)
+        )
+        shard_in, shard_merge = own_in.astype(F32), own_merge.astype(F32)
+        stat_one = line_stats.reshape(-1)
+    else:
+        shard_in = both_halves(half_to_owners(pair_in, 0), 0)
+        shard_merge = both_halves(half_to_owners(pair_merge, 1), 1)
+        gate_sums = lax.psum(diagonal, ("fsdp", "ctx"))
+        row_sums = lax.psum(sums, ("fsdp", "ctx"))
+        both_norms = lax.psum(norm_sums, ("fsdp", "ctx", "tp"))
+        stat_one = lax.psum(stat_one, "tp")
+    stat_one = stat_one[:, None] / features
     shard_down = both_halves(half_down, 1)
     shard_mid = both_halves(half_mid, 0)
-    shard_merge = both_halves(half_merge, 1)
-    shard_in = both_halves(half_in, 0)
+    gate_sums = gate_sums.astype(F32).reshape(block, 2, heads, block).transpose(1, 2, 0, 3)
 
     def own(block):
         return lax.dynamic_slice_in_dim(block, feat_start, feat_local, 1)
 
-    own_inputs = own(inputs)
+    own_inputs = own(tokens).astype(F32)
     output = (own_inputs + own(merged).astype(F32) + feed.astype(F32)).astype(BF16)
     grad_tokens = (
         own_resid_grad
@@ -1035,12 +1290,6 @@
     norm_local = norm_mix.shape[0]
     own_norms = lax.dynamic_slice_in_dim(both_norms, lax.axis_index("fsdp") * norm_local, norm_local, 1)
 
-    diagonal = [
-        gate_grads[i * block : (i + 1) * block, part * chans + i * block : part * chans + (i + 1) * block]
-        for part in range(2)
-        for i in range(heads)
-    ]
-    gate_sums = lax.psum(jnp.stack(diagonal).astype(BF16), ("fsdp", "ctx")).astype(F32)
     return (
         output,
         grad_tokens,
@@ -1054,8 +1303,8 @@
         own_norms[1],
         row_sums[4 : 4 + width],
         row_sums[3],
-        gate_sums[:heads],
-        gate_sums[heads:],
+        gate_sums[0],
+        gate_sums[1],
         row_sums[1],
         row_sums[2],
         CGAIN * row_sums[0] * jax.nn.sigmoid(-decay_logit),

time: 751 us -> 630 us (0.84)
  waiting for transfers between devices: 144 us -> 25.8 us
  Pallas kernels: 341 us -> 403 us
  blocking collectives: 42.2 us -> 0 us
  matrix products: 142 us -> 128 us
    reduce_scatter x1, waiting for transfers between devices: 63.7 us -> 0.01 us  [shards(): d_normed = lax.psum_scatter(part_one, 'tp', scatter_dimension=1, tiled=True)]
    pallas_call x0 -> x1, Pallas kernels: none -> 54.1 us  [leave(): pl.pallas_call(leave_kernel, out_shape=(shape((part_in.shape[0] // 2, par...]
    psum x2 -> x0, blocking collectives: 42.2 us -> none  [the longest x1 23.2 us: shards(): row_sums = lax.psum(jnp.concatenate([sums, flat], axis=0), ('fsdp', 'ctx'))]
    psum x1 -> x0, waiting for transfers between devices: 36.3 us -> none  [shards(): lax.psum(jnp.stack(diagonal).astype(BF16), ('fsdp', 'ctx')).astype(F32)]
    reduce_scatter x1, waiting for transfers between devices: 17.2 us -> 0.02 us  [shards(): feed = lax.psum_scatter(part_feed, 'tp', scatter_dimension=1, tiled=True)]
    dot_general x8, matrix products: 53 us -> 43.3 us  [product(): return lax.dot_general(*pair, rows_to_rows, preferred_element_type=F32)]
    pallas_call x1, Pallas kernels: 118 us -> 126 us  [turn(): pl.pallas_call(lambda *refs: turn_kernel(split, *refs), out_shape=tuple(o...]
    reduce_scatter x4 -> x2, waiting for transfers between devices: 18.7 us -> 18.4 us  [half_to_owners(): return lax.psum_scatter(mine, 'fsdp', scatter_dimension=dim, tiled=True)]
  transfers between devices with their start and end apart: 19 -> 14, of which waited for: 8 -> 5; matrix products, arithmetic and copies ran while one was open for 16% -> 16% of each run, Pallas kernels for 20% -> 29%
where the time goes in v4:
time: 630 us; the launch traced here: 625 us
  Pallas kernels  403 us (64%)
  matrix products  128 us (20%)
  waiting for transfers between devices  25.8 us (4%)
  other arithmetic  22.4 us (4%)
  local copies, waits for them, and re-layouts  22.2 us (4%)
  between operations  14.5 us (2%)
  starting transfers between devices  9.04 us (1%)
    pallas_call x1, Pallas kernels, turn(): pl.pallas_call(lambda *refs: turn_kernel(split, *refs), out_shape=tuple(o...  126 us
    pallas_call x1, Pallas kernels, middle(): pl.pallas_call(lambda *refs: middle_kernel(bool(shards), *refs), out_shap...  120 us
    pallas_call x1, Pallas kernels, leave(): pl.pallas_call(leave_kernel, out_shape=(shape((part_in.shape[0] // 2, par...  54.1 us
    pallas_call x1, Pallas kernels, enter(): pl.pallas_call(enter_kernel, out_shape=(shape((rows, features), BF16), sh...  47.4 us
    dot_general x8, matrix products, product(): return lax.dot_general(*pair, rows_to_rows, preferred_element_type=F32)  43.3 us
    pallas_call x1, Pallas kernels, recur_backward(): pl.pallas_call(backward_kernel, grid=(count,), out_shape=(jax.ShapeDtypeS...  19 us
    dot_general x1, matrix products, shards(): lax.dot_general(d_mid, after(whole_mid, part_feed), rows_to_features, pre...  18.5 us
    reduce_scatter x2, waiting for transfers between devices, half_to_owners(): return lax.psum_scatter(mine, 'fsdp', scatter_dimension=dim, tiled=True)  18.4 us
  transfers between devices with their start and end apart: 14, of which 5 were waited for; matrix products, arithmetic and copies ran while one was open for 16% of the time, Pallas kernels for 29%

profile of v4, /device:TPU:0, one launch (start us, length us, event | category | flops | bytes accessed | tf_op | source)
XLA Modules:
  0.0 624.7 jit_solution(7052465141880846595)
XLA Ops:
  9.2 47.4 %enter.1 = (bf16[1024,2048]{1,0:T(8,128)(2,1)}, bf16[2,1024,1024]{2,1,0:T(8,128)(2,1)}, bf16[2,1024,1024]{2,1,0:T(8,128)(2,1)}, f32[8,2048]{1,0:T(8,128)}, bf16[...) custom-call(bf16[1024,2048]{1,0:T(8,128)(2,1)} %refs_1_.3, bf16[1024,2048]{1,0:T(8,128)(2,1)} %refs_3_.3, ...), custom_call_target="tpu_custom_call" | custom-call | tf_op jit(solution)/shard_map/enter/pallas_call | solution.py:359
  56.7 9.0 %convolution_convert_fusion.5.branch_ref.pre_ref = bf16[1024,1280]{1,0:T(8,128)(2,1)S(1)} fusion(bf16[1024,2048]{1,0:T(8,128)(2,1)} %get-tuple-element.64, bf16[2048,1280]{1,0:T(8,128)(2,1)} %get-tuple-element.65), kind=kOutput, calls=%fused_computation.36 | convolution fusion | flops 5370019840 | bytes 12058624 | tf_op jit(solution)/shard_map/dot_general | solution.py:1195
  73.4 14.3 %recur_forward.1 = (bf16[1024,640]{1,0:T(8,128)(2,1)}, f32[1024,640]{1,0:T(8,128)}, f32[1024,640]{1,0:T(8,128)}, f32[1024,640]{1,0:T(8,128)}, f32[1024,640]{1,0:T(8,128)}, /*index=5*/bf16[640,1280]{1,0:T(8,128)(2,1)}) custom-call(bf16[1024,1280]{1,0:T(8,128)(2,1)} %copy-done, bf16[8,640]{1,0:T(8,128)(2,1)} %copy-done.12, ...), custom_call_target="tpu_custom_call" | custom-call | flops 1677721600 | bytes 15728640 | tf_op jit(solution)/shard_map/recur_forward/pallas_call | solution.py:882
  91.1 10.7 %merge_states.1 = (f32[1024,640]{1,0:T(8,128)}, bf16[1024,640]{1,0:T(8,128)(2,1)}, bf16[1024,2048]{1,0:T(8,128)(2,1)}) custom-call(f32[1024,640]{1,0:T(8,128)} %get-tuple-element.66.local_ref, f32[1024,640]{1,0:T(8,128)} %get-tuple-element.67.run_ref, f32[1,640]{1,0:T(1,128)} %slice.150.enter_ref, bf16[1024,1280]{1,0:T(8,128)(2,1)} %copy-done, ...), custom_call_target="tpu_custom_call" | custom-call | flops 2684354560 | bytes 10485760 | tf_op jit(solution)/shard_map/merge_states/pallas_call | solution.py:928
  101.8 120.2 %middle.1 = (bf16[1024,2048]{1,0:T(8,128)(2,1)}, bf16[1024,2048]{1,0:T(8,128)(2,1)}, bf16[2,1024,1024]{2,1,0:T(8,128)(2,1)}, bf16[2048,3072]{1,0:T(8,128)(2,1)}, bf16[1536,2048]{1,0:T(8,128)(2,1)}) custom-call(bf16[1024,2048]{1,0:T(8,128)(2,1)} %get-tuple-element.69.refs_0_, bf16[1024,2048]{1,0:T(8,128)(2,1)} %refs_1_.3, ...), custom_call_target="tpu_custom_call" | custom-call | bytes 400000000 | tf_op jit(solution)/shard_map/middle/pallas_call | solution.py:438
  222.0 17.1 %convolution_convert_fusion.1 = bf16[1024,3072]{1,0:T(8,128)(2,1)S(1)} fusion(bf16[1024,2048]{1,0:T(8,128)(2,1)} %get-tuple-element.72, bf16[2048,3072]{1,0:T(8,128)(2,1)} %get-tuple-element.75), kind=kOutput, calls=%fused_computation.31 | convolution fusion | flops 12888047616 | bytes 23068672 | tf_op jit(solution)/shard_map/dot_general | solution.py:1214
  239.1 12.6 %fusion.7 = (bf16[1024,1536]{1,0:T(8,128)(2,1)S(1)}, bf16[1024,1536]{1,0:T(8,128)(2,1)}, bf16[1024,1536]{1,0:T(8,128)(2,1)S(1)}) fusion(bf16[1024,3072]{1,0:T(8,128)(2,1)S(1)} %convolution_convert_fusion.1, bf16[1536,2048]{1,0:T(8,128)(2,1)S(1)} %copy-done.19, bf16[1024,2048]{1,0:T(8,128)(2,1)S(1)} %copy-done.1), kind=kOutput, calls=%fused_computation.21 | convolution fusion | flops 6488064000 | bytes 26214400 | tf_op jit(solution)/shard_map/dot_general | solution.py:1215
  253.4 8.2 %convolution_convert_fusion.4 = bf16[1024,2048]{1,0:T(8,128)(2,1)} fusion(bf16[1024,1536]{1,0:T(8,128)(2,1)S(1)} %get-tuple-element.76, bf16[1536,2048]{1,0:T(8,128)(2,1)S(1)} %copy-done.19), kind=kOutput, calls=%fused_computation.35 | convolution fusion | flops 6444548096 | bytes 13631488 | tf_op jit(solution)/shard_map/dot_general | solution.py:1223
  261.9 6.2 convolution_convert_fusion.8
  268.1 8.9 %convolution_convert_fusion = bf16[1024,3072]{1,0:T(8,128)(2,1)} fusion(bf16[2,1024,1024]{2,1,0:T(8,128)(2,1)S(1)} %copy-done.23, bf16[1024,1536]{1,0:T(8,128)(2,1)S(1)} %copy-done.26, bf16[1024,1536]{1,0:T(8,128)(2,1)S(1)} %get-tuple-element.117), kind=kOutput, calls=%fused_computation.30 | convolution fusion | flops 6458179584 | bytes 14680064 | tf_op jit(solution)/shard_map/dot_general | solution.py:56
  277.5 4.9 add_convert_fusion.1
  282.6 5.0 collective-permute-done.3
  287.6 11.6 %add_convert_fusion = bf16[1024,3072]{1,0:T(8,128)(2,1)} fusion(bf16[1024,3072]{1,0:T(8,128)(2,1)} %collective-permute-done.3, bf16[2,1024,1024]{2,1,0:T(8,128)(2,1)} %get-tuple-element.79, bf16[1024,1536]{1,0:T(8,128)(2,1)} %get-tuple-element.118, bf16[1024,1536]{1,0:T(8,128)(2,1)S(1)} %get-tuple-element.117), kind=kOutput, calls=%fused_computation.7 | convolution fusion | flops 6464471040 | bytes 20971520 | tf_op jit(solution)/shard_map/dot_general | solution.py:56
  299.3 18.5 %convolution_convert_fusion.2.refs_0_ = bf16[1024,2048]{1,0:T(8,128)(2,1)} fusion(bf16[2048,3072]{1,0:T(8,128)(2,1)} %get-tuple-element.75, bf16[1024,1536]{1,0:T(8,128)(2,1)} %get-tuple-element.118, bf16[1024,1536]{1,0:T(8,128)(2,1)S(1)} %get-tuple-element.117), kind=kOutput, calls=%fused_computation.33 | convolution fusion | flops 12899581952 | bytes 23068672 | tf_op jit(solution)/shard_map/dot_general | solution.py:1226
  317.8 126.1 %turn.1 = (f32[1024,512]{1,0:T(8,128)}, bf16[1024,2048]{1,0:T(8,128)(2,1)}, f32[8,2048]{1,0:T(8,128)}, bf16[2,1024,1024]{2,1,0:T(8,128)(2,1)}) custom-call(bf16[1024,2048]{1,0:T(8,128)(2,1)} %convolution_convert_fusion.2.refs_0_, bf16[1024,2048]{1,0:T(8,128)(2,1)} %refs_1_.3, bf16[1024,2048]{1,0:T(8,128)(2,1)} %get-tuple-element.71.refs_2_, ...), custom_call_target="tpu_custom_call" | custom-call | bytes 400000000 | tf_op jit(solution)/shard_map/turn/pallas_call | solution.py:488
  443.9 7.1 %fusion.68.up_ref = f32[1024,640]{1,0:T(8,128)} fusion(bf16[1024,2048]{1,0:T(8,128)(2,1)} %get-tuple-element.85, bf16[640,2048]{1,0:T(8,128)(2,1)S(1)} %copy-done.4), kind=kOutput, calls=%fused_computation.130 | convolution fusion | flops 2684354560 | bytes 9437184 | tf_op jit(solution)/shard_map/dot_general | solution.py:1237
  451.1 18.3 %reduce-scatter.7.cloned.1.call-done = bf16[256,3072]{1,0:T(8,128)(2,1)} async-done(((bf16[1024,3072]{1,0:T(8,128)(2,1)}), bf16[256,3072]{1,0:T(8,128)(2,1)}) %reduce-scatter.7.cloned.1.call-update) | async-done | bytes 1572880 | tf_op jit(solution)/shard_map/reduce_scatter | solution.py:63
  469.4 11.5 %recur_adjoint.1 = (f32[1024,640]{1,0:T(8,128)}, f32[1024,640]{1,0:T(8,128)}, f32[8,640]{1,0:T(8,128)}, bf16[1024,640]{1,0:T(8,128)(2,1)}) custom-call(f32[1024,640]{1,0:T(8,128)} %get-tuple-element.83.rate_ref, f32[1024,640]{1,0:T(8,128)} %fusion.68.up_ref, bf16[1024,1280]{1,0:T(8,128)(2,1)} %copy-done, f32[1024,640]{1,0:T(8,128)} %get-tuple-element.86.state_ref, ...), custom_call_target="tpu_custom_call" | custom-call | flops 5242880 | bytes 10485760 | tf_op jit(solution)/shard_map/recur_adjoint/pallas_call | solution.py:982
  485.8 19.0 %recur_backward.1 = (bf16[1024,1280]{1,0:T(8,128)(2,1)}, f32[8,640]{1,0:T(8,128)}, f32[8,640]{1,0:T(8,128)}, f32[640,1280]{1,0:T(8,128)}, f32[16,640]{1,0:T(8,128)}) custom-call(f32[1024,640]{1,0:T(8,128)} %get-tuple-element.87.grad_ref, f32[1024,640]{1,0:T(8,128)} %get-tuple-element.88.run_ref, f32[1,640]{1,0:T(1,128)} %slice.153.enter_ref, ...), custom_call_target="tpu_custom_call" | custom-call | flops 3355443200 | bytes 18350080 | tf_op jit(solution)/shard_map/recur_backward/pallas_call | solution.py:1097
  509.5 11.7 %multiply_reduce_fusion = (f32[1024]{0:T(1024)}, f32[2048]{0:T(1024)S(1)}, bf16[1024,2048]{1,0:T(8,128)(2,1)}) fusion(bf16[1024,2048]{1,0:T(8,128)(2,1)} %refs_1_.3, f32[2048]{0:T(1024)S(1)} %bitcast.78, f32[1024]{0:T(1024)S(1)} %get-tuple-element.138, bf16[1024,1280]{1,0:T(8,128)(2,1)} %fusion.52, bf16[2048,1280]{1,0:T(8,128)(2,1)} %get-tuple-element.65), kind=kOutput, calls=%fused_computation.11 | convolution fusion | flops 5385483264 | bytes 16277504 | tf_op jit(solution)/shard_map/dot_general | solution.py:1246
  531.7 3.2 convolution_convert_fusion.7
  542.9 4.4 add_convert_fusion.2.part_in
  547.3 54.1 %leave.1 = (bf16[512,1280]{1,0:T(8,128)(2,1)}, bf16[640,512]{1,0:T(8,128)(2,1)}, bf16[160,1280]{1,0:T(8,128)(2,1)}, f32[16,640]{1,0:T(8,128)}, f32[8,2048]{1,0:T(8,128)}, /*index=5*/f32[8,128]{1,0:T(8,128)}) custom-call(bf16[1024,1280]{1,0:T(8,128)(2,1)} %add_convert_fusion.2.part_in, bf16[640,1024]{1,0:T(8,128)(2,1)} %add_convert_fusion.3.part_merge, ...), custom_call_target="tpu_custom_call" | custom-call | bytes 160000000 | tf_op jit(solution)/shard_map/leave/pallas_call | solution.py:714
  614.3 3.6 fusion.17
  (137 shorter events, 56.7 us)
Async XLA Ops:
  7.2 436.7 %reduce-scatter.5.cloned.1.call-start = ((), (), s32[]{:S(2)}) async-start(), calls=%async_computation.4 | async-start | bytes 5242880 | tf_op jit(solution)/shard_map/reduce_scatter | solution.py:1224
  56.6 11.5 %copy-start.16 = (bf16[640]{0:T(1024)(128)(2,1)S(1)}, bf16[640]{0:T(1024)(128)(2,1)}, u32[]{:S(2)}) copy-start(bf16[640]{0:T(1024)(128)(2,1)} %param.34) | copy-start | bytes 3844
  56.7 11.5 %copy-start.17 = (bf16[640]{0:T(1024)(128)(2,1)S(1)}, bf16[640]{0:T(1024)(128)(2,1)}, u32[]{:S(2)}) copy-start(bf16[640]{0:T(1024)(128)(2,1)} %param.33) | copy-start | bytes 3844
  56.7 11.6 %copy-start.10 = (f32[640]{0:T(1024)S(1)}, f32[640]{0:T(1024)}, u32[]{:S(2)}) copy-start(f32[640]{0:T(1024)} %param.35) | copy-start | bytes 7684
  56.7 11.6 %copy-start.8 = (bf16[4,160,160]{2,1,0:T(8,128)(2,1)S(1)}, bf16[4,160,160]{2,1,0:T(8,128)(2,1)}, u32[]{:S(2)}) copy-start(bf16[4,160,160]{2,1,0:T(8,128)(2,1)} %param.32) | copy-start | bytes 614404
  56.7 11.6 %copy-start.9 = (bf16[4,160,160]{2,1,0:T(8,128)(2,1)S(1)}, bf16[4,160,160]{2,1,0:T(8,128)(2,1)}, u32[]{:S(2)}) copy-start(bf16[4,160,160]{2,1,0:T(8,128)(2,1)} %param.31) | copy-start | bytes 614404
  56.7 14.3 %copy-start.14 = (bf16[4,640]{1,0:T(4,128)(2,1)S(1)}, bf16[4,640]{1,0:T(4,128)(2,1)}, u32[]{:S(2)}) copy-start(bf16[4,640]{1,0:T(4,128)(2,1)} %param.29) | copy-start | bytes 15364
  56.7 14.9 %copy-start.18 = (bf16[640]{0:T(1024)(128)(2,1)S(1)}, bf16[640]{0:T(1024)(128)(2,1)}, u32[]{:S(2)}) copy-start(bf16[640]{0:T(1024)(128)(2,1)} %param.30) | copy-start | bytes 3844
  65.7 7.0 %collective-permute-start = (bf16[8,640]{1,0:T(8,128)(2,1)S(1)}, bf16[8,640]{1,0:T(8,128)(2,1)S(1)}, u32[]{:S(2)}, u32[]{:S(2)}) collective-permute-start(bf16[8,640]{1,0:T(8,128)(2,1)S(1)} %slice.149), channel_id=1, source_target_pairs={{0,4},{1,5},{2,6},{3,7},{8,12},{9,13},{10,14},{11,15},{16,20},{17,... | collective-permute-start | bytes 30728 | tf_op jit(solution)/shard_map/ppermute | solution.py:26
  88.4 2.1 collective-permute-start.1
  221.9 17.2 %copy-start.1 = (bf16[1024,2048]{1,0:T(8,128)(2,1)S(1)}, bf16[1024,2048]{1,0:T(8,128)(2,1)}, u32[]{:S(2)}) copy-start(bf16[1024,2048]{1,0:T(8,128)(2,1)} %refs_3_.3) | copy-start | bytes 12582916
  222.0 17.2 %copy-start.19 = (bf16[1536,2048]{1,0:T(8,128)(2,1)S(1)}, bf16[1536,2048]{1,0:T(8,128)(2,1)}, u32[]{:S(2)}) copy-start(bf16[1536,2048]{1,0:T(8,128)(2,1)} %get-tuple-element.74) | copy-start | bytes 18874372
  261.6 182.3 %reduce-scatter.9.cloned.1.call-start = ((), (), s32[]{:S(2)}) async-start(), calls=%async_computation.6 | async-start | bytes 3932160 | tf_op jit(solution)/shard_map/reduce_scatter | solution.py:63
  268.0 9.5 %collective-permute-start.2 = (bf16[1536,1024]{1,0:T(8,128)(2,1)S(1)}, bf16[1536,1024]{1,0:T(8,128)(2,1)S(1)}, u32[]{:S(2)}, u32[]{:S(2)}) collective-permute-start(bf16[1536,1024]{1,0:T(8,128)(2,1)S(1)} %convolution_convert_fusion.8), channel_id=1, source_target_pairs={{0,4},{4,0},{1,5},{5,1},{2,6},{6,2},{3,7},{7,3},{8,12},{12,8},{9,1... | collective-permute-start | bytes 9437192 | tf_op jit(solution)/shard_map/ppermute | solution.py:20
  277.0 10.6 %collective-permute-start.3 = (bf16[1024,3072]{1,0:T(8,128)(2,1)}, bf16[1024,3072]{1,0:T(8,128)(2,1)}, u32[]{:S(2)}, u32[]{:S(2)}) collective-permute-start(bf16[1024,3072]{1,0:T(8,128)(2,1)} %convolution_convert_fusion), channel_id=1, source_target_pairs={{0,4},{4,0},{1,5},{5,1},{2,6},{6,2},{3,7},{7,3},{8,12},{12,8},{9,1... | collective-permute-start | bytes 18874376 | tf_op jit(solution)/shard_map/ppermute | solution.py:20
  282.4 187.0 %reduce-scatter.7.cloned.1.call-start = ((), (), s32[]{:S(2)}) async-start(), calls=%async_computation.5 | async-start | bytes 7864320 | tf_op jit(solution)/shard_map/reduce_scatter | solution.py:63
  299.2 315.1 %reduce-scatter.11.cloned.1.call-start = ((), (), s32[]{:S(2)}) async-start(), calls=%async_computation.7 | async-start | bytes 5242880 | tf_op jit(solution)/shard_map/reduce_scatter | solution.py:1247
  317.8 126.1 %copy-start.4 = (bf16[640,2048]{1,0:T(8,128)(2,1)S(1)}, bf16[640,2048]{1,0:T(8,128)(2,1)}, u32[]{:S(2)}) copy-start(bf16[640,2048]{1,0:T(8,128)(2,1)} %get-tuple-element.68.weight_ref) | copy-start | bytes 7864324
  480.9 4.4 collective-permute-start.4
  504.8 3.3 collective-permute-start.5
  522.3 2.4 collective-permute-start.9
  526.9 11.6 %collective-permute-start.8 = (bf16[256,3072]{1,0:T(8,128)(2,1)S(1)}, bf16[256,3072]{1,0:T(8,128)(2,1)S(1)}, u32[]{:S(2)}, u32[]{:S(2)}) collective-permute-start(bf16[256,3072]{1,0:T(8,128)(2,1)S(1)} %copy-done.6), channel_id=1, source_target_pairs={{0,4},{4,0},{1,5},{5,1},{2,6},{6,2},{3,7},{7,3},{8,12},{12,8},{9,1... | collective-permute-start | bytes 4718600 | tf_op jit(solution)/shard_map/ppermute | solution.py:20
  528.9 7.0 %collective-permute-start.7 = (bf16[640,1024]{1,0:T(8,128)(2,1)S(1)}, bf16[640,1024]{1,0:T(8,128)(2,1)S(1)}, u32[]{:S(2)}, u32[]{:S(2)}) collective-permute-start(bf16[640,1024]{1,0:T(8,128)(2,1)S(1)} %fusion.45), channel_id=1, source_target_pairs={{0,4},{4,0},{1,5},{5,1},{2,6},{6,2},{3,7},{7,3},{8,12},{12,8},{9,1... | collective-permute-start | bytes 3932168 | tf_op jit(solution)/shard_map/ppermute | solution.py:20
  535.0 7.9 %collective-permute-start.6 = (bf16[1024,1280]{1,0:T(8,128)(2,1)S(1)}, bf16[1024,1280]{1,0:T(8,128)(2,1)S(1)}, u32[]{:S(2)}, u32[]{:S(2)}) collective-permute-start(bf16[1024,1280]{1,0:T(8,128)(2,1)S(1)} %convolution_convert_fusion.7), channel_id=1, source_target_pairs={{0,4},{4,0},{1,5},{5,1},{2,6},{6,2},{3,7},{7,3},{8,12},{12,8},{9,1... | collective-permute-start | bytes 7864328 | tf_op jit(solution)/shard_map/ppermute | solution.py:20
  (19 other events, 114.7 us)
Sparse Core Ops, SparseCore 0:
  261.7 82.7 reduce-scatter.4
  348.1 48.2 reduce-scatter.8
  399.4 70.0 reduce-scatter.6
  521.3 81.3 reduce-scatter.10

commit v5 on v4

--- a/solution.py
+++ b/solution.py
@@ -48,7 +48,7 @@
     ]
 
 
-def pair_sums(left, right, dim):
+def pair_sums(left, right, dim, behind=None):
     rows_to_rows = (((0,), (0,)), ((), ()))
 
     def product(index):
@@ -56,6 +56,8 @@
         return lax.dot_general(*pair, rows_to_rows, preferred_element_type=F32)
 
     arrived = swap_cores(product(1).astype(BF16))
+    if behind is not None:
+        arrived, left = after((arrived, left), behind)
     return (product(0) + arrived.astype(F32)).astype(BF16)
 
 
@@ -380,7 +382,23 @@
     return [pltpu.VMEM((2, chunks, CHUNK, features), BF16), dma, dma, dma, dma]
 
 
-def middle_kernel(gathers, part, tokens, gains, *refs):
+class Fetch:
+    def __init__(self, sources, targets, sems):
+        self.copies = [pltpu.make_async_copy(a, b, sems.at[k]) for k, (a, b) in enumerate(zip(sources, targets))]
+
+    def start(self):
+        for copy in self.copies:
+            copy.start()
+
+    def wait(self):
+        for copy in self.copies:
+            copy.wait()
+
+
+def middle_kernel(gathers, part, far_tokens, gains, *refs):
+    *refs, tokens, fetch_sems = refs
+    fetch = Fetch((far_tokens,), (tokens,), fetch_sems)
+    fetch.start()
     if gathers:
         gate, up, down, merged, normed, halves, whole_in, whole_down = refs[:8]
         inbox, *rest = refs[8:]
@@ -404,6 +422,10 @@
             put_split(halves, rows, block)
 
     def between(t):
+        @pl.when(t == 0)
+        def _():
+            fetch.wait()
+
         if gathers:
             for w in range(3):
                 @pl.when(t == 5 + 4 * w)
@@ -435,10 +457,11 @@
         ]
         specs += [NEAR, ANY, ANY]
         scratch += gather_scratch(shards)
+    scratch += [pltpu.VMEM((rows, features), BF16), pltpu.SemaphoreType.DMA((1,))]
     return pl.pallas_call(
         lambda *refs: middle_kernel(bool(shards), *refs),
         out_shape=tuple(outs),
-        in_specs=[NEAR, NEAR, NEAR] + [ANY] * len(shards),
+        in_specs=[NEAR, ANY, NEAR] + [ANY] * len(shards),
         out_specs=specs,
         scratch_shapes=scratch,
         compiler_params=pltpu.CompilerParams(collective_id=2, has_side_effects=True),
@@ -447,11 +470,12 @@
     )(part, tokens, gains, *shards)
 
 
-def turn_kernel(split, part, tokens, merged, upstream, gains, own, grad_in, gain_sum, *refs):
+def turn_kernel(split, part, far_tokens, far_merged, far_upstream, gains, own, grad_in, gain_sum, *refs):
     if split:
-        halves, whole, wide, inbox, *sems = refs
-    else:
-        whole, wide, inbox, *sems = refs
+        halves, *refs = refs
+    whole, wide, tokens, merged, upstream, fetch_sems, inbox, *sems = refs
+    fetch = Fetch((far_tokens, far_merged, far_upstream), (tokens, merged, upstream), fetch_sems)
+    fetch.start()
     greet(True, False)
     gain_sum[...] = jnp.zeros_like(gain_sum)
     width = own.shape[1]
@@ -472,7 +496,12 @@
         if split:
             put_split(halves, rows, grad)
 
-    line_sum(part, whole, inbox, sems, finish, lambda t: None)
+    def between(t):
+        @pl.when(t == 0)
+        def _():
+            fetch.wait()
+
+    line_sum(part, whole, inbox, sems, finish, between)
 
 
 def turn(part, tokens, merged, upstream, gains, split):
@@ -488,9 +517,11 @@
     return pl.pallas_call(
         lambda *refs: turn_kernel(split, *refs),
         out_shape=tuple(outs),
-        in_specs=[NEAR] * 5,
+        in_specs=[NEAR, ANY, ANY, ANY, NEAR],
         out_specs=[NEAR] * len(outs),
         scratch_shapes=[pltpu.VMEM((rows, features), BF16), pltpu.VMEM((CHUNK, features), F32)]
+        + [pltpu.VMEM((rows, features), BF16)] * 3
+        + [pltpu.SemaphoreType.DMA((3,))]
         + line_scratch(rows, features),
         compiler_params=pltpu.CompilerParams(collective_id=3, has_side_effects=True),
         cost_estimate=LINE_COST,
@@ -633,6 +664,7 @@
     gate_copy(0).start()
     core_copy(0).start()
     core_copy(1).start()
+    scatter.start(0)
     for k in range(count):
         @pl.when(place != k)
         def _():
@@ -651,7 +683,6 @@
         cols = slice(k * gate_cols, (k + 1) * gate_cols)
         gate_half[k] = rounded_sum(gates[my_rows, cols], gate_core[:, cols])
         gate_copy(1 + k).start()
-    scatter.start(0)
     scatter.start(1)
     for k in (0, 1):
         for j in range(3):
@@ -1225,7 +1256,7 @@
     hidden = after(hidden, part_feed)
     part_two = lax.dot_general(d_mid, after(whole_mid, part_feed), rows_to_features, preferred_element_type=F32).astype(BF16)
     pair_down = pair_sums(cotangent_split, hidden, 1)
-    pair_mid = pair_sums(after(normed_two_split, part_feed), d_mid, 0)
+    pair_mid = pair_sums(after(normed_two_split, part_feed), d_mid, 0, part_two)
     part_two = after(part_two, pair_down, pair_mid)
     turned = turn(part_two, tokens, merged, cotangent, gains, square)
     own_resid_grad, d_merge_in, feed_sums = turned[:3]
@@ -1235,10 +1266,10 @@
     d_merge_in = after(d_merge_in, half_down, feed)
 
     d_gated = lax.dot_general(d_merge_in, whole_merge, rows_to_features, preferred_element_type=F32)
-    local_grad, grad_run, first, d_gelu_pre = recur_adjoint(after(rate, half_mid), d_gated, branches, states, masks, softer)
+    local_grad, grad_run, first, d_gelu_pre = recur_adjoint(rate, d_gated, branches, states, masks, softer)
     grad_in = shifted(first, "ctx", -1)[0:1]
     back, tail, head, gate_grads, sums = recur_backward(
-        local_grad, grad_run, grad_in, rate, entry, conv, states, masks, branches, d_gelu_pre,
+        local_grad, grad_run, grad_in, rate, after(entry, half_mid), conv, states, masks, branches, d_gelu_pre,
         halo, taps, gates, softer
     )
     returned = shifted(head, "ctx", -1)

time: 630 us -> 617 us (0.979)
  waiting for transfers between devices: 25.8 us -> 9.84 us
    reduce_scatter x2, waiting for transfers between devices: 18.4 us -> 7.38 us  [half_to_owners(): return lax.psum_scatter(mine, 'fsdp', scatter_dimension=dim, tiled=True)]
  transfers between devices with their start and end apart: 14 -> 14, of which waited for: 5 -> 4; matrix products, arithmetic and copies ran while one was open for 16% -> 17% of each run, Pallas kernels for 29% -> 32%
where the time goes in v5:
time: 617 us; the launch traced here: 612 us
  Pallas kernels  404 us (65%)
  matrix products  130 us (21%)
  other arithmetic  22.5 us (4%)
  local copies, waits for them, and re-layouts  22.2 us (4%)
  between operations  14.6 us (2%)
  waiting for transfers between devices  9.84 us (2%)
  starting transfers between devices  9.04 us (1%)
    pallas_call x1, Pallas kernels, turn(): pl.pallas_call(lambda *refs: turn_kernel(split, *refs), out_shape=tuple(o...  129 us
    pallas_call x1, Pallas kernels, middle(): pl.pallas_call(lambda *refs: middle_kernel(bool(shards), *refs), out_shap...  119 us
    pallas_call x1, Pallas kernels, leave(): pl.pallas_call(leave_kernel, out_shape=(shape((part_in.shape[0] // 2, par...  52.6 us
    pallas_call x1, Pallas kernels, enter(): pl.pallas_call(enter_kernel, out_shape=(shape((rows, features), BF16), sh...  47.4 us
    dot_general x8, matrix products, product(): return lax.dot_general(*pair, rows_to_rows, preferred_element_type=F32)  44.2 us
    dot_general x1, matrix products, shards(): lax.dot_general(d_mid, after(whole_mid, part_feed), rows_to_features, pre...  19.6 us
    pallas_call x1, Pallas kernels, recur_backward(): pl.pallas_call(backward_kernel, grid=(count,), out_shape=(jax.ShapeDtypeS...  19 us
    dot_general x1, matrix products, shards(): jnp.dot(normed_two, whole_mid, preferred_element_type=F32).astype(BF16)  17.1 us
  transfers between devices with their start and end apart: 14, of which 4 were waited for; matrix products, arithmetic and copies ran while one was open for 17% of the time, Pallas kernels for 32%

profile of v5, /device:TPU:0, one launch (start us, length us, event | category | flops | bytes accessed | tf_op | source)
XLA Modules:
  0.0 611.8 jit_solution(3776694021169023649)
XLA Ops:
  9.2 47.4 %enter.1 = (bf16[1024,2048]{1,0:T(8,128)(2,1)}, bf16[2,1024,1024]{2,1,0:T(8,128)(2,1)}, bf16[2,1024,1024]{2,1,0:T(8,128)(2,1)}, f32[8,2048]{1,0:T(8,128)}, bf16[...) custom-call(bf16[1024,2048]{1,0:T(8,128)(2,1)} %refs_1_.3, bf16[1024,2048]{1,0:T(8,128)(2,1)} %refs_3_.3, ...), custom_call_target="tpu_custom_call" | custom-call | tf_op jit(solution)/shard_map/enter/pallas_call | solution.py:361
  56.7 8.9 %convolution_convert_fusion.5.branch_ref.pre_ref = bf16[1024,1280]{1,0:T(8,128)(2,1)S(1)} fusion(bf16[1024,2048]{1,0:T(8,128)(2,1)} %get-tuple-element.66, bf16[2048,1280]{1,0:T(8,128)(2,1)} %get-tuple-element.67), kind=kOutput, calls=%fused_computation.36 | convolution fusion | flops 5370019840 | bytes 12058624 | tf_op jit(solution)/shard_map/dot_general | solution.py:1226
  73.4 14.3 %recur_forward.1 = (bf16[1024,640]{1,0:T(8,128)(2,1)}, f32[1024,640]{1,0:T(8,128)}, f32[1024,640]{1,0:T(8,128)}, f32[1024,640]{1,0:T(8,128)}, f32[1024,640]{1,0:T(8,128)}, /*index=5*/bf16[640,1280]{1,0:T(8,128)(2,1)}) custom-call(bf16[1024,1280]{1,0:T(8,128)(2,1)} %copy-done, bf16[8,640]{1,0:T(8,128)(2,1)} %copy-done.12, ...), custom_call_target="tpu_custom_call" | custom-call | flops 1677721600 | bytes 15728640 | tf_op jit(solution)/shard_map/recur_forward/pallas_call | solution.py:913
  91.1 10.7 %merge_states.1 = (f32[1024,640]{1,0:T(8,128)}, bf16[1024,640]{1,0:T(8,128)(2,1)}, bf16[1024,2048]{1,0:T(8,128)(2,1)}) custom-call(f32[1024,640]{1,0:T(8,128)} %get-tuple-element.68.local_ref, f32[1024,640]{1,0:T(8,128)} %get-tuple-element.69.run_ref, f32[1,640]{1,0:T(1,128)} %slice.150.enter_ref, bf16[1024,1280]{1,0:T(8,128)(2,1)} %copy-done, ...), custom_call_target="tpu_custom_call" | custom-call | flops 2684354560 | bytes 10485760 | tf_op jit(solution)/shard_map/merge_states/pallas_call | solution.py:959
  101.8 119.0 %middle.1 = (bf16[1024,2048]{1,0:T(8,128)(2,1)}, bf16[1024,2048]{1,0:T(8,128)(2,1)}, bf16[2,1024,1024]{2,1,0:T(8,128)(2,1)}, bf16[2048,3072]{1,0:T(8,128)(2,1)}, bf16[1536,2048]{1,0:T(8,128)(2,1)}) custom-call(bf16[1024,2048]{1,0:T(8,128)(2,1)} %get-tuple-element.71.refs_0_, bf16[1024,2048]{1,0:T(8,128)(2,1)} %refs_1_.3, ...), custom_call_target="tpu_custom_call" | custom-call | bytes 400000000 | tf_op jit(solution)/shard_map/middle/pallas_call | solution.py:461
  220.8 17.1 %convolution_convert_fusion.1 = bf16[1024,3072]{1,0:T(8,128)(2,1)S(1)} fusion(bf16[1024,2048]{1,0:T(8,128)(2,1)} %get-tuple-element.74, bf16[2048,3072]{1,0:T(8,128)(2,1)} %get-tuple-element.77), kind=kOutput, calls=%fused_computation.31 | convolution fusion | flops 12888047616 | bytes 23068672 | tf_op jit(solution)/shard_map/dot_general | solution.py:1245
  237.9 12.6 %fusion.7 = (bf16[1024,1536]{1,0:T(8,128)(2,1)S(1)}, bf16[1024,1536]{1,0:T(8,128)(2,1)}, bf16[1024,1536]{1,0:T(8,128)(2,1)S(1)}) fusion(bf16[1024,3072]{1,0:T(8,128)(2,1)S(1)} %convolution_convert_fusion.1, bf16[1536,2048]{1,0:T(8,128)(2,1)S(1)} %copy-done.19, bf16[1024,2048]{1,0:T(8,128)(2,1)S(1)} %copy-done.1), kind=kOutput, calls=%fused_computation.21 | convolution fusion | flops 6488064000 | bytes 26214400 | tf_op jit(solution)/shard_map/dot_general | solution.py:1246
  252.2 8.2 %convolution_convert_fusion.4 = bf16[1024,2048]{1,0:T(8,128)(2,1)} fusion(bf16[1024,1536]{1,0:T(8,128)(2,1)S(1)} %get-tuple-element.78, bf16[1536,2048]{1,0:T(8,128)(2,1)S(1)} %copy-done.19), kind=kOutput, calls=%fused_computation.35 | convolution fusion | flops 6444548096 | bytes 13631488 | tf_op jit(solution)/shard_map/dot_general | solution.py:1254
  260.6 6.2 %convolution_convert_fusion.8 = bf16[1536,1024]{1,0:T(8,128)(2,1)S(1)} fusion(bf16[1024,1536]{1,0:T(8,128)(2,1)} %copy-done.29, bf16[2,1024,1024]{2,1,0:T(8,128)(2,1)} %get-tuple-element.79), kind=kOutput, calls=%fused_computation.39 | convolution fusion | flops 3222798336 | bytes 8388608 | tf_op jit(solution)/shard_map/dot_general | solution.py:56
  266.9 8.9 %convolution_convert_fusion = bf16[1024,3072]{1,0:T(8,128)(2,1)} fusion(bf16[2,1024,1024]{2,1,0:T(8,128)(2,1)S(1)} %copy-done.23, bf16[1024,1536]{1,0:T(8,128)(2,1)S(1)} %copy-done.28, bf16[1024,1536]{1,0:T(8,128)(2,1)S(1)} %get-tuple-element.121), kind=kOutput, calls=%fused_computation.30 | convolution fusion | flops 6458179584 | bytes 14680064 | tf_op jit(solution)/shard_map/dot_general | solution.py:56
  276.3 4.8 add_convert_fusion.1
  281.4 19.6 %convolution_convert_fusion.2.refs_0_ = bf16[1024,2048]{1,0:T(8,128)(2,1)} fusion(bf16[2048,3072]{1,0:T(8,128)(2,1)} %get-tuple-element.77, bf16[1024,1536]{1,0:T(8,128)(2,1)} %get-tuple-element.122, bf16[1024,1536]{1,0:T(8,128)(2,1)} %copy-done.27), kind=kOutput, calls=%fused_computation.33 | convolution fusion | flops 12899581952 | bytes 23068672 | tf_op jit(solution)/shard_map/dot_general | solution.py:1257
  301.1 12.5 %add_convert_fusion = bf16[1024,3072]{1,0:T(8,128)(2,1)} fusion(bf16[1024,3072]{1,0:T(8,128)(2,1)} %collective-permute-done.3, bf16[2,1024,1024]{2,1,0:T(8,128)(2,1)S(1)} %copy-done.24, bf16[1024,1536]{1,0:T(8,128)(2,1)} %get-tuple-element.122, bf16[1024,1536]{1,0:T(8,128)(2,1)} %copy-done.27), kind=kOutput, calls=%fused_computation.7 | convolution fusion | flops 6464471040 | bytes 20971520 | tf_op jit(solution)/shard_map/dot_general | solution.py:56
  313.6 129.3 %turn.1 = (f32[1024,512]{1,0:T(8,128)}, bf16[1024,2048]{1,0:T(8,128)(2,1)}, f32[8,2048]{1,0:T(8,128)}, bf16[2,1024,1024]{2,1,0:T(8,128)(2,1)}) custom-call(bf16[1024,2048]{1,0:T(8,128)(2,1)} %convolution_convert_fusion.2.refs_0_, bf16[1024,2048]{1,0:T(8,128)(2,1)} %refs_1_.3, bf16[1024,2048]{1,0:T(8,128)(2,1)} %get-tuple-element.73.refs_2_, ...), custom_call_target="tpu_custom_call" | custom-call | bytes 400000000 | tf_op jit(solution)/shard_map/turn/pallas_call | solution.py:517
  443.0 7.3 %fusion.68.up_ref = f32[1024,640]{1,0:T(8,128)} fusion(bf16[1024,2048]{1,0:T(8,128)(2,1)} %get-tuple-element.88, bf16[640,2048]{1,0:T(8,128)(2,1)S(1)} %copy-done.4), kind=kOutput, calls=%fused_computation.130 | convolution fusion | flops 2684354560 | bytes 9437184 | tf_op jit(solution)/shard_map/dot_general | solution.py:1268
  450.3 11.8 %recur_adjoint.1 = (f32[1024,640]{1,0:T(8,128)}, f32[1024,640]{1,0:T(8,128)}, f32[8,640]{1,0:T(8,128)}, bf16[1024,640]{1,0:T(8,128)(2,1)}) custom-call(f32[1024,640]{1,0:T(8,128)} %get-tuple-element.86.rate_ref, f32[1024,640]{1,0:T(8,128)} %fusion.68.up_ref, bf16[1024,1280]{1,0:T(8,128)(2,1)} %copy-done, f32[1024,640]{1,0:T(8,128)} %get-tuple-element.89.state_ref, ...), custom_call_target="tpu_custom_call" | custom-call | flops 5242880 | bytes 10485760 | tf_op jit(solution)/shard_map/recur_adjoint/pallas_call | solution.py:1013
  467.1 7.4 %reduce-scatter.9.cloned.1.call-done = bf16[256,3072]{1,0:T(8,128)(2,1)} async-done(((bf16[1024,3072]{1,0:T(8,128)(2,1)}), bf16[256,3072]{1,0:T(8,128)(2,1)}) %reduce-scatter.9.cloned.1.call-update) | async-done | bytes 1572880 | tf_op jit(solution)/shard_map/reduce_scatter | solution.py:65
  474.4 19.0 %recur_backward.1 = (bf16[1024,1280]{1,0:T(8,128)(2,1)}, f32[8,640]{1,0:T(8,128)}, f32[8,640]{1,0:T(8,128)}, f32[640,1280]{1,0:T(8,128)}, f32[16,640]{1,0:T(8,128)}) custom-call(f32[1024,640]{1,0:T(8,128)} %get-tuple-element.90.grad_ref, f32[1024,640]{1,0:T(8,128)} %get-tuple-element.91.run_ref, f32[1,640]{1,0:T(1,128)} %slice.153.enter_ref, ...), custom_call_target="tpu_custom_call" | custom-call | flops 3355443200 | bytes 18350080 | tf_op jit(solution)/shard_map/recur_backward/pallas_call | solution.py:1128
  498.1 11.7 %multiply_reduce_fusion = (f32[1024]{0:T(1024)}, f32[2048]{0:T(1024)S(1)}, bf16[1024,2048]{1,0:T(8,128)(2,1)}) fusion(bf16[1024,2048]{1,0:T(8,128)(2,1)} %refs_1_.3, f32[2048]{0:T(1024)S(1)} %bitcast.78, f32[1024]{0:T(1024)S(1)} %get-tuple-element.142, bf16[1024,1280]{1,0:T(8,128)(2,1)} %fusion.52, bf16[2048,1280]{1,0:T(8,128)(2,1)} %get-tuple-element.67), kind=kOutput, calls=%fused_computation.11 | convolution fusion | flops 5385483264 | bytes 16277504 | tf_op jit(solution)/shard_map/dot_general | solution.py:1277
  520.3 3.2 convolution_convert_fusion.7
  528.4 3.1 fusion.65
  531.5 4.4 add_convert_fusion.2.part_in
  535.9 52.6 %leave.1 = (bf16[512,1280]{1,0:T(8,128)(2,1)}, bf16[640,512]{1,0:T(8,128)(2,1)}, bf16[160,1280]{1,0:T(8,128)(2,1)}, f32[16,640]{1,0:T(8,128)}, f32[8,2048]{1,0:T(8,128)}, /*index=5*/f32[8,128]{1,0:T(8,128)}) custom-call(bf16[1024,1280]{1,0:T(8,128)(2,1)} %add_convert_fusion.2.part_in, bf16[640,1024]{1,0:T(8,128)(2,1)} %add_convert_fusion.3.part_merge, ...), custom_call_target="tpu_custom_call" | custom-call | bytes 160000000 | tf_op jit(solution)/shard_map/leave/pallas_call | solution.py:745
  601.4 3.7 fusion.17
  (141 shorter events, 53.5 us)
Async XLA Ops:
  7.2 435.8 %reduce-scatter.5.cloned.1.call-start = ((), (), s32[]{:S(2)}) async-start(), calls=%async_computation.4 | async-start | bytes 5242880 | tf_op jit(solution)/shard_map/reduce_scatter | solution.py:1255
  56.7 11.5 %copy-start.10 = (f32[640]{0:T(1024)S(1)}, f32[640]{0:T(1024)}, u32[]{:S(2)}) copy-start(f32[640]{0:T(1024)} %param.35) | copy-start | bytes 7684
  56.7 11.6 %copy-start.8 = (bf16[4,160,160]{2,1,0:T(8,128)(2,1)S(1)}, bf16[4,160,160]{2,1,0:T(8,128)(2,1)}, u32[]{:S(2)}) copy-start(bf16[4,160,160]{2,1,0:T(8,128)(2,1)} %param.32) | copy-start | bytes 614404
  56.7 11.6 %copy-start.9 = (bf16[4,160,160]{2,1,0:T(8,128)(2,1)S(1)}, bf16[4,160,160]{2,1,0:T(8,128)(2,1)}, u32[]{:S(2)}) copy-start(bf16[4,160,160]{2,1,0:T(8,128)(2,1)} %param.31) | copy-start | bytes 614404
  56.7 14.3 %copy-start.14 = (bf16[4,640]{1,0:T(4,128)(2,1)S(1)}, bf16[4,640]{1,0:T(4,128)(2,1)}, u32[]{:S(2)}) copy-start(bf16[4,640]{1,0:T(4,128)(2,1)} %param.29) | copy-start | bytes 15364
  56.7 14.9 %copy-start.18 = (bf16[640]{0:T(1024)(128)(2,1)S(1)}, bf16[640]{0:T(1024)(128)(2,1)}, u32[]{:S(2)}) copy-start(bf16[640]{0:T(1024)(128)(2,1)} %param.30) | copy-start | bytes 3844
  65.7 7.0 %collective-permute-start = (bf16[8,640]{1,0:T(8,128)(2,1)S(1)}, bf16[8,640]{1,0:T(8,128)(2,1)S(1)}, u32[]{:S(2)}, u32[]{:S(2)}) collective-permute-start(bf16[8,640]{1,0:T(8,128)(2,1)S(1)} %slice.149), channel_id=1, source_target_pairs={{0,4},{1,5},{2,6},{3,7},{8,12},{9,13},{10,14},{11,15},{16,20},{17,... | collective-permute-start | bytes 30728 | tf_op jit(solution)/shard_map/ppermute | solution.py:26
  88.4 2.1 collective-permute-start.1
  220.7 17.2 %copy-start.1 = (bf16[1024,2048]{1,0:T(8,128)(2,1)S(1)}, bf16[1024,2048]{1,0:T(8,128)(2,1)}, u32[]{:S(2)}) copy-start(bf16[1024,2048]{1,0:T(8,128)(2,1)} %refs_3_.3) | copy-start | bytes 12582916
  220.8 17.2 %copy-start.19 = (bf16[1536,2048]{1,0:T(8,128)(2,1)S(1)}, bf16[1536,2048]{1,0:T(8,128)(2,1)}, u32[]{:S(2)}) copy-start(bf16[1536,2048]{1,0:T(8,128)(2,1)} %get-tuple-element.76) | copy-start | bytes 18874372
  250.5 16.4 %copy-start.27 = (bf16[1024,1536]{1,0:T(8,128)(2,1)}, bf16[1024,1536]{1,0:T(8,128)(2,1)S(1)}, u32[]{:S(2)}) copy-start(bf16[1024,1536]{1,0:T(8,128)(2,1)S(1)} %get-tuple-element.121) | copy-start | bytes 9437188
  260.4 182.6 %reduce-scatter.7.cloned.1.call-start = ((), (), s32[]{:S(2)}) async-start(), calls=%async_computation.5 | async-start | bytes 3932160 | tf_op jit(solution)/shard_map/reduce_scatter | solution.py:65
  266.8 9.5 %collective-permute-start.2 = (bf16[1536,1024]{1,0:T(8,128)(2,1)S(1)}, bf16[1536,1024]{1,0:T(8,128)(2,1)S(1)}, u32[]{:S(2)}, u32[]{:S(2)}) collective-permute-start(bf16[1536,1024]{1,0:T(8,128)(2,1)S(1)} %convolution_convert_fusion.8), channel_id=1, source_target_pairs={{0,4},{4,0},{1,5},{5,1},{2,6},{6,2},{3,7},{7,3},{8,12},{12,8},{9,1... | collective-permute-start | bytes 9437192 | tf_op jit(solution)/shard_map/ppermute | solution.py:20
  275.8 25.2 %collective-permute-start.3 = (bf16[1024,3072]{1,0:T(8,128)(2,1)}, bf16[1024,3072]{1,0:T(8,128)(2,1)}, u32[]{:S(2)}, u32[]{:S(2)}) collective-permute-start(bf16[1024,3072]{1,0:T(8,128)(2,1)} %convolution_convert_fusion), channel_id=1, source_target_pairs={{0,4},{4,0},{1,5},{5,1},{2,6},{6,2},{3,7},{7,3},{8,12},{12,8},{9,1... | collective-permute-start | bytes 18874376 | tf_op jit(solution)/shard_map/ppermute | solution.py:20
  281.2 193.2 %reduce-scatter.9.cloned.1.call-start = ((), (), s32[]{:S(2)}) async-start(), calls=%async_computation.6 | async-start | bytes 7864320 | tf_op jit(solution)/shard_map/reduce_scatter | solution.py:65
  281.4 19.6 %copy-start.24 = (bf16[2,1024,1024]{2,1,0:T(8,128)(2,1)S(1)}, bf16[2,1024,1024]{2,1,0:T(8,128)(2,1)}, u32[]{:S(2)}) copy-start(bf16[2,1024,1024]{2,1,0:T(8,128)(2,1)} %get-tuple-element.82) | copy-start | bytes 12582916
  313.6 287.9 %reduce-scatter.11.cloned.1.call-start = ((), (), s32[]{:S(2)}) async-start(), calls=%async_computation.7 | async-start | bytes 5242880 | tf_op jit(solution)/shard_map/reduce_scatter | solution.py:1278
  313.6 129.4 %copy-start.4 = (bf16[640,2048]{1,0:T(8,128)(2,1)S(1)}, bf16[640,2048]{1,0:T(8,128)(2,1)}, u32[]{:S(2)}) copy-start(bf16[640,2048]{1,0:T(8,128)(2,1)} %get-tuple-element.70.weight_ref) | copy-start | bytes 7864324
  462.1 4.4 collective-permute-start.4
  493.5 3.3 collective-permute-start.5
  510.9 2.4 collective-permute-start.9
  515.5 11.6 %collective-permute-start.8 = (bf16[256,3072]{1,0:T(8,128)(2,1)S(1)}, bf16[256,3072]{1,0:T(8,128)(2,1)S(1)}, u32[]{:S(2)}, u32[]{:S(2)}) collective-permute-start(bf16[256,3072]{1,0:T(8,128)(2,1)S(1)} %copy-done.6), channel_id=1, source_target_pairs={{0,4},{4,0},{1,5},{5,1},{2,6},{6,2},{3,7},{7,3},{8,12},{12,8},{9,1... | collective-permute-start | bytes 4718600 | tf_op jit(solution)/shard_map/ppermute | solution.py:20
  517.5 7.1 %collective-permute-start.7 = (bf16[640,1024]{1,0:T(8,128)(2,1)S(1)}, bf16[640,1024]{1,0:T(8,128)(2,1)S(1)}, u32[]{:S(2)}, u32[]{:S(2)}) collective-permute-start(bf16[640,1024]{1,0:T(8,128)(2,1)S(1)} %fusion.45), channel_id=1, source_target_pairs={{0,4},{4,0},{1,5},{5,1},{2,6},{6,2},{3,7},{7,3},{8,12},{12,8},{9,1... | collective-permute-start | bytes 3932168 | tf_op jit(solution)/shard_map/ppermute | solution.py:20
  523.6 7.9 %collective-permute-start.6 = (bf16[1024,1280]{1,0:T(8,128)(2,1)S(1)}, bf16[1024,1280]{1,0:T(8,128)(2,1)S(1)}, u32[]{:S(2)}, u32[]{:S(2)}) collective-permute-start(bf16[1024,1280]{1,0:T(8,128)(2,1)S(1)} %convolution_convert_fusion.7), channel_id=1, source_target_pairs={{0,4},{4,0},{1,5},{5,1},{2,6},{6,2},{3,7},{7,3},{8,12},{12,8},{9,1... | collective-permute-start | bytes 7864328 | tf_op jit(solution)/shard_map/ppermute | solution.py:20
  (21 other events, 137.9 us)
Sparse Core Ops, SparseCore 0:
  260.5 89.2 reduce-scatter.4
  353.4 47.9 reduce-scatter.6
  404.4 70.0 reduce-scatter.8
  509.9 81.3 reduce-scatter.10

commit v6 on v5

--- a/solution.py
+++ b/solution.py
@@ -612,9 +612,9 @@
 
 
 def leave_kernel(
-    part_in, part_merge, gates, sums, norms, stats,
-    own_in, own_merge, gate_sums, row_sums, norm_sums, stat_sums,
-    box_in, box_merge, last_in, last_merge, send, arrive,
+    part_in, gates, sums, norms, stats,
+    own_in, gate_sums, row_sums, norm_sums, stat_sums,
+    box_in, last_in, send, arrive,
     gate_core, gate_half, gate_near, gate_pair, gate_far, gate_send, gate_arrive,
     core_sums, core_norms, box_sums, box_norms, sum_send, sum_arrive,
     line_norms, line_stats, norm_send, norm_arrive, stat_send, stat_arrive,
@@ -658,13 +658,10 @@
             return remote(gate_half.at[k], gate_near.at[k], send, arrive, fsdp=square.near[k])
         return remote(gate_pair.at[k], gate_far.at[k], send, arrive, fsdp=square.near[1 - k])
 
-    scatter = Scatter(
-        [(part_merge, own_merge, 1), (part_in, own_in, 0)], (box_merge, box_in), (last_merge, last_in), send, arrive
-    )
+    scatter = Scatter([(part_in, own_in, 0)], (box_in,), (last_in,), send, arrive)
     gate_copy(0).start()
     core_copy(0).start()
     core_copy(1).start()
-    scatter.start(0)
     for k in range(count):
         @pl.when(place != k)
         def _():
@@ -683,7 +680,7 @@
         cols = slice(k * gate_cols, (k + 1) * gate_cols)
         gate_half[k] = rounded_sum(gates[my_rows, cols], gate_core[:, cols])
         gate_copy(1 + k).start()
-    scatter.start(1)
+    scatter.start(0)
     for k in (0, 1):
         for j in range(3):
             square_copy(k, j).wait_recv()
@@ -699,7 +696,6 @@
         gate_pair[k] = rounded_sum(gate_half[k], gate_near[k])
         gate_copy(3 + k).start()
     scatter.relay(0)
-    scatter.relay(1)
     for k in (0, 1):
         cols = slice(k * gate_cols, (k + 1) * gate_cols)
         gate_copy(3 + k).wait_recv()
@@ -719,9 +715,7 @@
     norm_sums[...] = total
     stat_sums[...] = stat
     scatter.finish(0)
-    scatter.finish(1)
-    for w in (0, 1):
-        scatter.drain(w)
+    scatter.drain(0)
     gate_copy(5).wait_recv()
     for j in range(6):
         gate_copy(j).wait_send()
@@ -736,7 +730,7 @@
             stat_copy(k, place).wait_send()
 
 
-def leave(part_in, part_merge, gates, sums, norms, stats):
+def leave(part_in, gates, sums, norms, stats):
     shape = jax.ShapeDtypeStruct
     count = lax.axis_size("tp")
     dma = pltpu.SemaphoreType.DMA
@@ -746,18 +740,15 @@
         leave_kernel,
         out_shape=(
             shape((part_in.shape[0] // 2, part_in.shape[1]), BF16),
-            shape((part_merge.shape[0], part_merge.shape[1] // 2), BF16),
             shape(gates.shape, BF16),
             shape(sums.shape, F32),
             shape(norms.shape, F32),
             shape(stats.shape, F32),
         ),
-        in_specs=[NEAR] * 6,
-        out_specs=[NEAR] * 6,
+        in_specs=[NEAR] * 5,
+        out_specs=[NEAR] * 5,
         scratch_shapes=(
-            (lambda boxes: [boxes[1], boxes[0], boxes[3], boxes[2], boxes[4], boxes[5]])(
-                scatter_scratch([(part_merge.shape, 1), (part_in.shape, 0)])
-            )
+            scatter_scratch([(part_in.shape, 0)])
             + [pltpu.VMEM((height, 2 * width), BF16), quarter, quarter, quarter, quarter, dma((6,)), dma((6,))]
             + [pltpu.VMEM(sums.shape, F32), pltpu.VMEM(norms.shape, F32)]
             + [pltpu.VMEM((4, *sums.shape), F32), pltpu.VMEM((4, *norms.shape), F32), dma((8,)), dma((8,))]
@@ -767,7 +758,7 @@
         compiler_params=pltpu.CompilerParams(collective_id=4, has_side_effects=True),
         cost_estimate=pl.CostEstimate(flops=0, bytes_accessed=160_000_000, transcendentals=0),
         name="leave",
-    )(part_in, part_merge, gates, sums, norms, stats)
+    )(part_in, gates, sums, norms, stats)
 
 
 def gelu_pair(q):
@@ -1133,7 +1124,7 @@
             edge,
             edge,
             jax.ShapeDtypeStruct((chans, 2 * chans), F32),
-            jax.ShapeDtypeStruct((16, chans), F32),
+            jax.ShapeDtypeStruct((8, chans), F32),
         ),
         in_specs=[
             wide, wide, fixed_spec((1, chans)), wide, wide, wide, wide,
@@ -1150,7 +1141,7 @@
             fixed_spec((8, chans)),
             fixed_spec((8, chans)),
             fixed_spec((chans, 2 * chans)),
-            fixed_spec((16, chans)),
+            fixed_spec((8, chans)),
         ],
         scratch_shapes=[
             pltpu.VMEM((taps.shape[0] - 1, TILE + 8, chans), F32),
@@ -1243,20 +1234,23 @@
 
     units = w_gate.shape[1]
     pre_mid = jnp.dot(normed_two, whole_mid, preferred_element_type=F32).astype(BF16)
-    d_hidden = lax.dot_general(cotangent, whole_down, rows_to_features, preferred_element_type=F32).astype(BF16)
+    gate_act = gelu_pair(pre_mid[:, :units].astype(F32))[0]
+    hidden = (gate_act * pre_mid[:, units:].astype(F32)).astype(BF16)
+    part_feed = jnp.dot(hidden, whole_down, preferred_element_type=F32).astype(BF16)
+    feed = lax.psum_scatter(part_feed, "tp", scatter_dimension=1, tiled=True)
+    hidden, pre_mid, whole_mid, late_cotangent, normed_two_split = after(
+        (hidden, pre_mid, whole_mid, cotangent, normed_two_split), part_feed
+    )
+    d_hidden = lax.dot_general(late_cotangent, whole_down, rows_to_features, preferred_element_type=F32).astype(BF16)
     gate_act, gate_slope = gelu_pair(pre_mid[:, :units].astype(F32))
     up_vals = pre_mid[:, units:].astype(F32)
     wide_hidden = d_hidden.astype(F32)
-    hidden = (gate_act * up_vals).astype(BF16)
     d_mid = jnp.concatenate(
         [(wide_hidden * up_vals * gate_slope).astype(BF16), (wide_hidden * gate_act).astype(BF16)], axis=1
     )
-    part_feed = jnp.dot(hidden, whole_down, preferred_element_type=F32).astype(BF16)
-    feed = lax.psum_scatter(part_feed, "tp", scatter_dimension=1, tiled=True)
-    hidden = after(hidden, part_feed)
-    part_two = lax.dot_general(d_mid, after(whole_mid, part_feed), rows_to_features, preferred_element_type=F32).astype(BF16)
+    part_two = lax.dot_general(d_mid, whole_mid, rows_to_features, preferred_element_type=F32).astype(BF16)
     pair_down = pair_sums(cotangent_split, hidden, 1)
-    pair_mid = pair_sums(after(normed_two_split, part_feed), d_mid, 0, part_two)
+    pair_mid = pair_sums(normed_two_split, d_mid, 0, part_two)
     part_two = after(part_two, pair_down, pair_mid)
     turned = turn(part_two, tokens, merged, cotangent, gains, square)
     own_resid_grad, d_merge_in, feed_sums = turned[:3]
@@ -1265,19 +1259,22 @@
     half_mid = half_to_owners(pair_mid, 0)
     d_merge_in = after(d_merge_in, half_down, feed)
 
+    shard_down = both_halves(half_down, 1)
+    pair_merge = pair_sums(d_merge_split, gated, 1)
+    half_merge = half_to_owners(pair_merge, 1)
     d_gated = lax.dot_general(d_merge_in, whole_merge, rows_to_features, preferred_element_type=F32)
     local_grad, grad_run, first, d_gelu_pre = recur_adjoint(rate, d_gated, branches, states, masks, softer)
     grad_in = shifted(first, "ctx", -1)[0:1]
     back, tail, head, gate_grads, sums = recur_backward(
-        local_grad, grad_run, grad_in, rate, after(entry, half_mid), conv, states, masks, branches, d_gelu_pre,
+        local_grad, grad_run, grad_in, rate, after(entry, half_mid, shard_down, pair_merge), conv, states, masks, branches, d_gelu_pre,
         halo, taps, gates, softer
     )
     returned = shifted(head, "ctx", -1)
     d_in = lax.dynamic_update_slice(back, (tail + returned).astype(BF16), (piece - 8, 0))
     part_one = lax.dot_general(d_in, whole_in, rows_to_features, preferred_element_type=F32).astype(BF16)
+    part_one = after(part_one, half_merge)
     d_normed = lax.psum_scatter(part_one, "tp", scatter_dimension=1, tiled=True)
 
-    pair_merge = pair_sums(d_merge_split, after(gated, part_one), 1)
     pair_in = pair_sums(normed_split, after(d_in, part_one), 0)
     inputs = tokens.astype(F32)
     scale_one = rms_scale(inputs)
@@ -1289,22 +1286,21 @@
     diagonal = sum(jnp.where(spread == i, gate_grads[i * block : (i + 1) * block], 0.0) for i in range(heads))
     diagonal = diagonal.astype(BF16)
     if square:
-        norm_sums = jnp.pad(norm_sums, ((0, 6), (0, 0)))
-        own_in, own_merge, gate_sums, row_sums, both_norms, line_stats = leave(
-            pair_in, pair_merge, diagonal, sums, norm_sums, stat_one.reshape(-1, 128)
+        own_in, gate_sums, row_sums, both_norms, line_stats = leave(
+            pair_in, diagonal, sums, norm_sums.reshape(-1, 128), stat_one.reshape(-1, 128)
         )
-        shard_in, shard_merge = own_in.astype(F32), own_merge.astype(F32)
+        shard_in = own_in.astype(F32)
+        both_norms = both_norms.reshape(2, features)
         stat_one = line_stats.reshape(-1)
     else:
         shard_in = both_halves(half_to_owners(pair_in, 0), 0)
-        shard_merge = both_halves(half_to_owners(pair_merge, 1), 1)
         gate_sums = lax.psum(diagonal, ("fsdp", "ctx"))
         row_sums = lax.psum(sums, ("fsdp", "ctx"))
         both_norms = lax.psum(norm_sums, ("fsdp", "ctx", "tp"))
         stat_one = lax.psum(stat_one, "tp")
     stat_one = stat_one[:, None] / features
-    shard_down = both_halves(half_down, 1)
     shard_mid = both_halves(half_mid, 0)
+    shard_merge = both_halves(half_merge, 1)
     gate_sums = gate_sums.astype(F32).reshape(block, 2, heads, block).transpose(1, 2, 0, 3)
 
     def own(block):

time: 617 us -> 598 us (0.969)
  Pallas kernels: 404 us -> 374 us
  matrix products: 130 us -> 140 us
    pallas_call x1, Pallas kernels: 129 us -> 114 us  [turn(): pl.pallas_call(lambda *refs: turn_kernel(split, *refs), out_shape=tuple(o...]
    pallas_call x1, Pallas kernels: 52.6 us -> 38.8 us  [leave(): pl.pallas_call(leave_kernel, out_shape=(shape((part_in.shape[0] // 2, par...]
    dot_general x8, matrix products: 44.2 us -> 53.3 us  [product(): return lax.dot_general(*pair, rows_to_rows, preferred_element_type=F32)]
    reduce_scatter x2 -> x3, waiting for transfers between devices: 7.38 us -> 0.01 us  [half_to_owners(): return lax.psum_scatter(mine, 'fsdp', scatter_dimension=dim, tiled=True)]
  transfers between devices with their start and end apart: 14 -> 16, of which waited for: 4 -> 4; matrix products, arithmetic and copies ran while one was open for 17% -> 24% of each run, Pallas kernels for 32% -> 31%
where the time goes in v6:
time: 598 us; the launch traced here: 592 us
  Pallas kernels  374 us (63%)
  matrix products  140 us (23%)
  other arithmetic  27.2 us (5%)
  local copies, waits for them, and re-layouts  24.3 us (4%)
  between operations  14.6 us (2%)
  starting transfers between devices  8.16 us (1%)
    pallas_call x1, Pallas kernels, middle(): pl.pallas_call(lambda *refs: middle_kernel(bool(shards), *refs), out_shap...  119 us
    pallas_call x1, Pallas kernels, turn(): pl.pallas_call(lambda *refs: turn_kernel(split, *refs), out_shape=tuple(o...  114 us
    dot_general x8, matrix products, product(): return lax.dot_general(*pair, rows_to_rows, preferred_element_type=F32)  53.3 us
    pallas_call x1, Pallas kernels, enter(): pl.pallas_call(enter_kernel, out_shape=(shape((rows, features), BF16), sh...  47.4 us
    pallas_call x1, Pallas kernels, leave(): pl.pallas_call(leave_kernel, out_shape=(shape((part_in.shape[0] // 2, par...  38.8 us
    dot_general x1, matrix products, shards(): lax.dot_general(d_mid, whole_mid, rows_to_features, preferred_element_typ...  20.1 us
    pallas_call x1, Pallas kernels, recur_backward(): pl.pallas_call(backward_kernel, grid=(count,), out_shape=(jax.ShapeDtypeS...  18.9 us
    dot_general x1, matrix products, shards(): jnp.dot(normed_two, whole_mid, preferred_element_type=F32).astype(BF16)  17 us
  transfers between devices with their start and end apart: 16, of which 4 were waited for; matrix products, arithmetic and copies ran while one was open for 24% of the time, Pallas kernels for 31%

profile of v6, /device:TPU:0, one launch (start us, length us, event | category | flops | bytes accessed | tf_op | source)
XLA Modules:
  0.0 592.4 jit_solution(7351464306987482401)
XLA Ops:
  9.2 47.4 %enter.1 = (bf16[1024,2048]{1,0:T(8,128)(2,1)}, bf16[2,1024,1024]{2,1,0:T(8,128)(2,1)}, bf16[2,1024,1024]{2,1,0:T(8,128)(2,1)}, f32[8,2048]{1,0:T(8,128)}, bf16[...) custom-call(bf16[1024,2048]{1,0:T(8,128)(2,1)} %refs_1_.3, bf16[1024,2048]{1,0:T(8,128)(2,1)} %refs_3_.3, ...), custom_call_target="tpu_custom_call" | custom-call | tf_op jit(solution)/shard_map/enter/pallas_call | solution.py:361
  56.7 8.9 %convolution_convert_fusion.5.branch_ref.pre_ref = bf16[1024,1280]{1,0:T(8,128)(2,1)S(1)} fusion(bf16[1024,2048]{1,0:T(8,128)(2,1)} %get-tuple-element.67, bf16[2048,1280]{1,0:T(8,128)(2,1)} %get-tuple-element.68), kind=kOutput, calls=%fused_computation.45 | convolution fusion | flops 5370019840 | bytes 12058624 | tf_op jit(solution)/shard_map/dot_general | solution.py:1217
  73.4 14.3 %recur_forward.1 = (bf16[1024,640]{1,0:T(8,128)(2,1)}, f32[1024,640]{1,0:T(8,128)}, f32[1024,640]{1,0:T(8,128)}, f32[1024,640]{1,0:T(8,128)}, f32[1024,640]{1,0:T(8,128)}, /*index=5*/bf16[640,1280]{1,0:T(8,128)(2,1)}) custom-call(bf16[1024,1280]{1,0:T(8,128)(2,1)} %copy-done.1, bf16[8,640]{1,0:T(8,128)(2,1)} %copy-done.18, ...), custom_call_target="tpu_custom_call" | custom-call | flops 1677721600 | bytes 15728640 | tf_op jit(solution)/shard_map/recur_forward/pallas_call | solution.py:904
  91.1 10.7 %merge_states.1 = (f32[1024,640]{1,0:T(8,128)}, bf16[1024,640]{1,0:T(8,128)(2,1)}, bf16[1024,2048]{1,0:T(8,128)(2,1)}) custom-call(f32[1024,640]{1,0:T(8,128)} %get-tuple-element.69.local_ref, f32[1024,640]{1,0:T(8,128)} %get-tuple-element.70.run_ref, f32[1,640]{1,0:T(1,128)} %slice.158.enter_ref, bf16[1024,1280]{1,0:T(8,128)(2,1)} %copy-done.1, ...), custom_call_target="tpu_custom_call" | custom-call | flops 2684354560 | bytes 10485760 | tf_op jit(solution)/shard_map/merge_states/pallas_call | solution.py:950
  101.8 118.5 %middle.1 = (bf16[1024,2048]{1,0:T(8,128)(2,1)}, bf16[1024,2048]{1,0:T(8,128)(2,1)}, bf16[2,1024,1024]{2,1,0:T(8,128)(2,1)}, bf16[2048,3072]{1,0:T(8,128)(2,1)}, bf16[1536,2048]{1,0:T(8,128)(2,1)}) custom-call(bf16[1024,2048]{1,0:T(8,128)(2,1)} %get-tuple-element.72.refs_0_, bf16[1024,2048]{1,0:T(8,128)(2,1)} %refs_1_.3, ...), custom_call_target="tpu_custom_call" | custom-call | bytes 400000000 | tf_op jit(solution)/shard_map/middle/pallas_call | solution.py:461
  220.3 17.0 %convolution_convert_fusion.1 = bf16[1024,3072]{1,0:T(8,128)(2,1)S(1)} fusion(bf16[1024,2048]{1,0:T(8,128)(2,1)} %get-tuple-element.75, bf16[2048,3072]{1,0:T(8,128)(2,1)} %get-tuple-element.81), kind=kOutput, calls=%fused_computation.40 | convolution fusion | flops 12888047616 | bytes 23068672 | tf_op jit(solution)/shard_map/dot_general | solution.py:1236
  243.6 8.3 %convolution_convert_fusion.4 = bf16[1024,2048]{1,0:T(8,128)(2,1)} fusion(bf16[1024,1536]{1,0:T(8,128)(2,1)S(1)} %fusion.11, bf16[1536,2048]{1,0:T(8,128)(2,1)S(1)} %copy-done.25), kind=kOutput, calls=%fused_computation.44 | convolution fusion | flops 6444548096 | bytes 13631488 | tf_op jit(solution)/shard_map/dot_general | solution.py:1239
  252.0 6.2 %convolution_convert_fusion.8 = bf16[1536,1024]{1,0:T(8,128)(2,1)S(1)} fusion(bf16[1024,1536]{1,0:T(8,128)(2,1)} %copy-done.7, bf16[2,1024,1024]{2,1,0:T(8,128)(2,1)} %get-tuple-element.83), kind=kOutput, calls=%fused_computation.48 | convolution fusion | flops 3222798336 | bytes 8388608 | tf_op jit(solution)/shard_map/dot_general | solution.py:56
  258.3 14.5 %fusion.7 = (bf16[1024,1536]{1,0:T(8,128)(2,1)}, bf16[1024,1536]{1,0:T(8,128)(2,1)}) fusion(bf16[1024,3072]{1,0:T(8,128)(2,1)S(1)} %bitcast.71, bf16[1024,2048]{1,0:T(8,128)(2,1)S(1)} %copy-done.3, bf16[1536,2048]{1,0:T(8,128)(2,1)} %get-tuple-element.77), kind=kOutput, calls=%fused_computation.26 | convolution fusion | flops 6484918272 | bytes 23068672 | tf_op jit(solution)/shard_map/dot_general | solution.py:1244
  272.8 11.8 %convolution_convert_fusion = bf16[1024,3072]{1,0:T(8,128)(2,1)} fusion(bf16[2,1024,1024]{2,1,0:T(8,128)(2,1)S(1)} %copy-done.29, bf16[1024,1536]{1,0:T(8,128)(2,1)} %get-tuple-element.124, bf16[1024,1536]{1,0:T(8,128)(2,1)} %get-tuple-element.123), kind=kOutput, calls=%fused_computation.39 | convolution fusion | flops 6458179584 | bytes 14680064 | tf_op jit(solution)/shard_map/dot_general | solution.py:56
  284.9 4.9 add_convert_fusion.1
  289.9 20.1 %convolution_convert_fusion.2.refs_0_ = bf16[1024,2048]{1,0:T(8,128)(2,1)} fusion(bf16[2048,3072]{1,0:T(8,128)(2,1)} %get-tuple-element.81, bf16[1024,1536]{1,0:T(8,128)(2,1)} %get-tuple-element.124, bf16[1024,1536]{1,0:T(8,128)(2,1)} %get-tuple-element.123), kind=kOutput, calls=%fused_computation.42 | convolution fusion | flops 12899581952 | bytes 23068672 | tf_op jit(solution)/shard_map/dot_general | solution.py:1251
  310.0 12.5 %add_convert_fusion = bf16[1024,3072]{1,0:T(8,128)(2,1)} fusion(bf16[1024,3072]{1,0:T(8,128)(2,1)} %collective-permute-done.3, bf16[2,1024,1024]{2,1,0:T(8,128)(2,1)S(1)} %copy-done.30, bf16[1024,1536]{1,0:T(8,128)(2,1)} %get-tuple-element.124, bf16[1024,1536]{1,0:T(8,128)(2,1)} %get-tuple-element.123), kind=kOutput, calls=%fused_computation.7 | convolution fusion | flops 6464471040 | bytes 20971520 | tf_op jit(solution)/shard_map/dot_general | solution.py:56
  322.6 114.2 %turn.1 = (f32[1024,512]{1,0:T(8,128)}, bf16[1024,2048]{1,0:T(8,128)(2,1)}, f32[8,2048]{1,0:T(8,128)}, bf16[2,1024,1024]{2,1,0:T(8,128)(2,1)}) custom-call(bf16[1024,2048]{1,0:T(8,128)(2,1)} %convolution_convert_fusion.2.refs_0_, bf16[1024,2048]{1,0:T(8,128)(2,1)} %refs_1_.3, bf16[1024,2048]{1,0:T(8,128)(2,1)} %get-tuple-element.74.refs_2_, ...), custom_call_target="tpu_custom_call" | custom-call | bytes 400000000 | tf_op jit(solution)/shard_map/turn/pallas_call | solution.py:517
  436.8 4.8 fusion.50
  442.2 7.1 %fusion.73.up_ref = f32[1024,640]{1,0:T(8,128)} fusion(bf16[1024,2048]{1,0:T(8,128)(2,1)} %get-tuple-element.91, bf16[640,2048]{1,0:T(8,128)(2,1)S(1)} %copy-done.9), kind=kOutput, calls=%fused_computation.141 | convolution fusion | flops 2684354560 | bytes 9437184 | tf_op jit(solution)/shard_map/dot_general | solution.py:1265
  449.3 11.6 %recur_adjoint.1 = (f32[1024,640]{1,0:T(8,128)}, f32[1024,640]{1,0:T(8,128)}, f32[8,640]{1,0:T(8,128)}, bf16[1024,640]{1,0:T(8,128)(2,1)}) custom-call(f32[1024,640]{1,0:T(8,128)} %get-tuple-element.89.rate_ref, f32[1024,640]{1,0:T(8,128)} %fusion.73.up_ref, bf16[1024,1280]{1,0:T(8,128)(2,1)} %copy-done.1, f32[1024,640]{1,0:T(8,128)} %get-tuple-element.92.state_ref, ...), custom_call_target="tpu_custom_call" | custom-call | flops 5242880 | bytes 10485760 | tf_op jit(solution)/shard_map/recur_adjoint/pallas_call | solution.py:1004
  462.3 4.6 add_convert_fusion.3
  469.8 18.9 %recur_backward.1 = (bf16[1024,1280]{1,0:T(8,128)(2,1)}, f32[8,640]{1,0:T(8,128)}, f32[8,640]{1,0:T(8,128)}, f32[640,1280]{1,0:T(8,128)}, f32[8,640]{1,0:T(8,128)}) custom-call(f32[1024,640]{1,0:T(8,128)} %get-tuple-element.93.grad_ref, f32[1024,640]{1,0:T(8,128)} %get-tuple-element.94.run_ref, f32[1,640]{1,0:T(1,128)} %slice.161.enter_ref, ...), custom_call_target="tpu_custom_call" | custom-call | flops 3355443200 | bytes 18350080 | tf_op jit(solution)/shard_map/recur_backward/pallas_call | solution.py:1119
  493.4 10.3 %convolution_convert_fusion.6 = bf16[1024,2048]{1,0:T(8,128)(2,1)} fusion(bf16[1024,1280]{1,0:T(8,128)(2,1)} %fusion.57, bf16[2048,1280]{1,0:T(8,128)(2,1)} %get-tuple-element.68), kind=kOutput, calls=%fused_computation.46 | convolution fusion | flops 5370806272 | bytes 12058624 | tf_op jit(solution)/shard_map/dot_general | solution.py:1274
  512.1 4.3 convolution_convert_fusion.7
  523.4 3.7 fusion.70
  528.7 4.3 add_convert_fusion.2.part_in
  533.0 38.8 %leave.1 = (bf16[512,1280]{1,0:T(8,128)(2,1)}, bf16[160,1280]{1,0:T(8,128)(2,1)}, f32[8,640]{1,0:T(8,128)}, f32[32,128]{1,0:T(8,128)}, f32[8,128]{1,0:T(8,128)}) custom-call(bf16[1024,1280]{1,0:T(8,128)(2,1)} %add_convert_fusion.2.part_in, bf16[160,1280]{1,0:T(8,128)(2,1)} %add_convert_fusion.4.gates, f32[8,640]{1,0:T(8,128)} %get-tuple-element.110.sums, ...), custom_call_target="tpu_custom_call" | custom-call | bytes 160000000 | tf_op jit(solution)/shard_map/leave/pallas_call | solution.py:739
  (162 shorter events, 60.0 us)
Async XLA Ops:
  7.2 434.5 %reduce-scatter.6.cloned.1.call-start = ((), (), s32[]{:S(2)}) async-start(), calls=%async_computation.5 | async-start | bytes 5242880 | tf_op jit(solution)/shard_map/reduce_scatter | solution.py:1240
  56.7 14.3 %copy-start.20 = (bf16[4,640]{1,0:T(4,128)(2,1)S(1)}, bf16[4,640]{1,0:T(4,128)(2,1)}, u32[]{:S(2)}) copy-start(bf16[4,640]{1,0:T(4,128)(2,1)} %param.29) | copy-start | bytes 15364
  56.7 14.9 %copy-start.24 = (bf16[640]{0:T(1024)(128)(2,1)S(1)}, bf16[640]{0:T(1024)(128)(2,1)}, u32[]{:S(2)}) copy-start(bf16[640]{0:T(1024)(128)(2,1)} %param.30) | copy-start | bytes 3844
  65.7 7.0 %collective-permute-start = (bf16[8,640]{1,0:T(8,128)(2,1)S(1)}, bf16[8,640]{1,0:T(8,128)(2,1)S(1)}, u32[]{:S(2)}, u32[]{:S(2)}) collective-permute-start(bf16[8,640]{1,0:T(8,128)(2,1)S(1)} %slice.157), channel_id=1, source_target_pairs={{0,4},{1,5},{2,6},{3,7},{8,12},{9,13},{10,14},{11,15},{16,20},{17,... | collective-permute-start | bytes 30728 | tf_op jit(solution)/shard_map/ppermute | solution.py:26
  88.4 2.1 collective-permute-start.1
  251.9 189.7 %reduce-scatter.8.cloned.1.call-start = ((), (), s32[]{:S(2)}) async-start(), calls=%async_computation.6 | async-start | bytes 3932160 | tf_op jit(solution)/shard_map/reduce_scatter | solution.py:65
  258.1 14.7 %copy-start.29 = (bf16[2,1024,1024]{2,1,0:T(8,128)(2,1)S(1)}, bf16[2,1024,1024]{2,1,0:T(8,128)(2,1)}, u32[]{:S(2)}) copy-start(bf16[2,1024,1024]{2,1,0:T(8,128)(2,1)} %get-tuple-element.85) | copy-start | bytes 12582916
  258.2 26.8 %collective-permute-start.2 = (bf16[1536,1024]{1,0:T(8,128)(2,1)S(1)}, bf16[1536,1024]{1,0:T(8,128)(2,1)S(1)}, u32[]{:S(2)}, u32[]{:S(2)}) collective-permute-start(bf16[1536,1024]{1,0:T(8,128)(2,1)S(1)} %convolution_convert_fusion.8), channel_id=1, source_target_pairs={{0,4},{4,0},{1,5},{5,1},{2,6},{6,2},{3,7},{7,3},{8,12},{12,8},{9,1... | collective-permute-start | bytes 9437192 | tf_op jit(solution)/shard_map/ppermute | solution.py:20
  272.8 12.1 %copy-start.8 = (bf16[1024,1536]{1,0:T(8,128)(2,1)S(1)}, bf16[1024,1536]{1,0:T(8,128)(2,1)}, u32[]{:S(2)}) copy-start(bf16[1024,1536]{1,0:T(8,128)(2,1)} %copy-done.7) | copy-start | bytes 9437188
  272.8 12.1 %copy-start.28 = (bf16[2,1024,1024]{2,1,0:T(8,128)(2,1)S(1)}, bf16[2,1024,1024]{2,1,0:T(8,128)(2,1)}, u32[]{:S(2)}) copy-start(bf16[2,1024,1024]{2,1,0:T(8,128)(2,1)} %get-tuple-element.83) | copy-start | bytes 12582916
  284.6 25.4 %collective-permute-start.3 = (bf16[1024,3072]{1,0:T(8,128)(2,1)}, bf16[1024,3072]{1,0:T(8,128)(2,1)}, u32[]{:S(2)}, u32[]{:S(2)}) collective-permute-start(bf16[1024,3072]{1,0:T(8,128)(2,1)} %convolution_convert_fusion), channel_id=1, source_target_pairs={{0,4},{4,0},{1,5},{5,1},{2,6},{6,2},{3,7},{7,3},{8,12},{12,8},{9,1... | collective-permute-start | bytes 18874376 | tf_op jit(solution)/shard_map/ppermute | solution.py:20
  289.9 180.0 %reduce-scatter.10.cloned.1.call-start = ((), (), s32[]{:S(2)}) async-start(), calls=%async_computation.7 | async-start | bytes 7864320 | tf_op jit(solution)/shard_map/reduce_scatter | solution.py:65
  289.9 20.1 %copy-start.30 = (bf16[2,1024,1024]{2,1,0:T(8,128)(2,1)S(1)}, bf16[2,1024,1024]{2,1,0:T(8,128)(2,1)}, u32[]{:S(2)}) copy-start(bf16[2,1024,1024]{2,1,0:T(8,128)(2,1)} %get-tuple-element.85) | copy-start | bytes 12582916
  322.6 181.1 %reduce-scatter.12.cloned.1.call-start = ((), (), s32[]{:S(2)}) async-start(), calls=%async_computation.8 | async-start | bytes 1638400 | tf_op jit(solution)/shard_map/reduce_scatter | solution.py:65
  441.6 20.7 %collective-permute-start.6 = (bf16[640,1024]{1,0:T(8,128)(2,1)}, bf16[640,1024]{1,0:T(8,128)(2,1)}, u32[]{:S(2)}, u32[]{:S(2)}) collective-permute-start(bf16[640,1024]{1,0:T(8,128)(2,1)} %fusion.50), channel_id=1, source_target_pairs={{0,4},{4,0},{1,5},{5,1},{2,6},{6,2},{3,7},{7,3},{8,12},{12,8},{9,1... | collective-permute-start | bytes 3932168 | tf_op jit(solution)/shard_map/ppermute | solution.py:20
  441.6 25.9 %collective-permute-start.5 = (bf16[1536,256]{1,0:T(8,128)(2,1)}, bf16[1536,256]{1,0:T(8,128)(2,1)S(1)}, u32[]{:S(2)}, u32[]{:S(2)}) collective-permute-start(bf16[1536,256]{1,0:T(8,128)(2,1)} %reduce-scatter.8.cloned.1.call-done), channel_id=1, source_target_pairs={{0,4},{4,0},{1,5},{5,1},{2,6},{6,2},{3,7},{7,3},{8,12},{12,8},{9,1... | collective-permute-start | bytes 2359304 | tf_op jit(solution)/shard_map/ppermute | solution.py:20
  449.3 13.0 %copy-start.33 = (bf16[1024,640]{1,0:T(8,128)(2,1)S(1)}, bf16[1024,640]{1,0:T(8,128)(2,1)}, u32[]{:S(2)}) copy-start(bf16[1024,640]{1,0:T(8,128)(2,1)} %get-tuple-element.97) | copy-start | bytes 3932164
  460.9 6.1 %collective-permute-start.4 = (f32[8,640]{1,0:T(8,128)}, f32[8,640]{1,0:T(8,128)S(1)}, u32[]{:S(2)}, u32[]{:S(2)}) collective-permute-start(f32[8,640]{1,0:T(8,128)} %get-tuple-element.95), channel_id=1, source_target_pairs={{4,0},{5,1},{6,2},{7,3},{12,8},{13,9},{14,10},{15,11},{20,16},{21,... | collective-permute-start | bytes 61448 | tf_op jit(solution)/shard_map/ppermute | solution.py:26
  466.9 115.1 %reduce-scatter.14.cloned.1.call-start = ((), (), s32[]{:S(2)}) async-start(), calls=%async_computation.9 | async-start | bytes 5242880 | tf_op jit(solution)/shard_map/reduce_scatter | solution.py:1276
  488.7 3.3 collective-permute-start.7
  507.9 1.7 collective-permute-start.9
  510.9 9.6 %collective-permute-start.10 = (bf16[256,3072]{1,0:T(8,128)(2,1)}, bf16[256,3072]{1,0:T(8,128)(2,1)}, u32[]{:S(2)}, u32[]{:S(2)}) collective-permute-start(bf16[256,3072]{1,0:T(8,128)(2,1)} %reduce-scatter.10.cloned.1.call-done), channel_id=1, source_target_pairs={{0,4},{4,0},{1,5},{5,1},{2,6},{6,2},{3,7},{7,3},{8,12},{12,8},{9,1... | collective-permute-start | bytes 4718600 | tf_op jit(solution)/shard_map/ppermute | solution.py:20
  516.4 10.7 %collective-permute-start.8 = (bf16[1024,1280]{1,0:T(8,128)(2,1)}, bf16[1024,1280]{1,0:T(8,128)(2,1)S(1)}, u32[]{:S(2)}, u32[]{:S(2)}) collective-permute-start(bf16[1024,1280]{1,0:T(8,128)(2,1)} %convolution_convert_fusion.7), channel_id=1, source_target_pairs={{0,4},{4,0},{1,5},{5,1},{2,6},{6,2},{3,7},{7,3},{8,12},{12,8},{9,1... | collective-permute-start | bytes 7864328 | tf_op jit(solution)/shard_map/ppermute | solution.py:20
  533.0 44.9 %copy-start.17 = (f32[640]{0:T(1024)S(1)}, f32[640]{0:T(1024)}, u32[]{:S(2)}) copy-start(f32[640]{0:T(1024)} %param.35) | copy-start | bytes 7684
  (28 other events, 181.4 us)
Sparse Core Ops, SparseCore 0:
  252.0 74.8 reduce-scatter.5
  330.5 45.2 reduce-scatter.7
  378.8 70.0 reduce-scatter.9
  467.1 30.3 reduce-scatter.11
  503.8 78.1 reduce-scatter.13

commit v7 on v6

--- a/solution.py
+++ b/solution.py
@@ -298,9 +298,9 @@
 
 
 def enter_kernel(
-    tokens, upstream, gain_shard, recur, gelu, merge,
-    normed, halves, upstream_halves, gains, whole_in, whole_merge,
-    stage_recur, stage_gelu, stage_merge, send, arrive, local, gain_send, gain_arrive,
+    tokens, upstream, gain_shard, recur, gelu,
+    normed, halves, upstream_halves, gains, whole_in,
+    stage_recur, stage_gelu, send, arrive, local, gain_send, gain_arrive,
 ):
     square = Square()
     greet(False, True)
@@ -314,10 +314,10 @@
     for k, target in enumerate(others):
         gain_copy(k, square.me, target).start()
     gather = Gather(
-        [(recur, whole_in, 0, 0), (gelu, whole_in, 0, recur.shape[1]), (merge, whole_merge, 1, 0)],
-        (stage_recur, stage_gelu, stage_merge), send, arrive, local,
+        [(recur, whole_in, 0, 0), (gelu, whole_in, 0, recur.shape[1])],
+        (stage_recur, stage_gelu), send, arrive, local,
     )
-    for w in range(3):
+    for w in range(2):
         gather.start(w)
     gains[:, pl.ds(pl.multiple_of(square.me * width, 128), width)] = gain_shard[...]
     for k, owner in enumerate(others):
@@ -333,11 +333,11 @@
         return carry
 
     lax.fori_loop(0, tokens.shape[0] // CHUNK, norm, 0)
-    for w in range(3):
+    for w in range(2):
         gather.forward(w)
-    for w in range(3):
+    for w in range(2):
         gather.hand_over(w)
-    for w in range(3):
+    for w in range(2):
         gather.finish(w)
     for k, target in enumerate(others):
         gain_copy(k, square.me, target).wait_send()
@@ -353,7 +353,7 @@
     return [pltpu.VMEM(w.shape, w.dtype) for w in shards] + [dma((count, 7)), dma((count, 7)), dma((count, 2))]
 
 
-def enter(tokens, upstream, gain_shard, recur, gelu, merge):
+def enter(tokens, upstream, gain_shard, recur, gelu):
     rows, features = tokens.shape
     shape = jax.ShapeDtypeStruct
     inner = recur.shape[1]
@@ -366,14 +366,13 @@
             shape((2, rows, features // 2), BF16),
             shape((8, features), F32),
             shape((features, 2 * inner), BF16),
-            shape((inner, features), BF16),
         ),
-        in_specs=[NEAR, NEAR, NEAR, ANY, ANY, ANY],
-        out_specs=[NEAR, NEAR, NEAR, NEAR, ANY, ANY],
-        scratch_shapes=gather_scratch([recur, gelu, merge]) + [dma((3,)), dma((3,))],
+        in_specs=[NEAR, NEAR, NEAR, ANY, ANY],
+        out_specs=[NEAR, NEAR, NEAR, NEAR, ANY],
+        scratch_shapes=gather_scratch([recur, gelu]) + [dma((3,)), dma((3,))],
         compiler_params=pltpu.CompilerParams(collective_id=1, has_side_effects=True),
         name="enter",
-    )(tokens, upstream, gain_shard, recur, gelu, merge)
+    )(tokens, upstream, gain_shard, recur, gelu)
 
 
 def line_scratch(rows, features):
@@ -833,6 +832,9 @@
         carry_ref[8:9, lanes] = product[last : last + 1, :]
 
 
+BIAS, RATE, ENTRY, SOFTER = slice(4, 5), slice(5, 6), slice(6, 7), slice(7, 8)
+
+
 def spread_blocks(blocks_ref, out_ref):
     chans, size = blocks_ref.shape[1:]
     row = lax.broadcasted_iota(jnp.int32, (chans, chans), 0)
@@ -851,7 +853,7 @@
 
 
 def forward_kernel(
-    branch_ref, halo_ref, mask_ref, taps_ref, bias_ref, blocks_ref, gate_bias_ref, softer_ref,
+    branch_ref, halo_ref, mask_ref, chan_ref, blocks_ref,
     conv_ref, rate_ref, entry_ref, state_ref, run_ref, gates_ref,
     window, decay, value, inner, product, carry,
 ):
@@ -870,19 +872,19 @@
         window[0:8, :] = window[rows : rows + 8, :]
 
     window[8 : rows + 8, :] = branch_ref[...].astype(F32)
-    mixed = bias_ref[...] + taps_ref[0:1, :] * window[8 : rows + 8, :]
-    for shift in range(1, taps_ref.shape[0]):
+    mixed = chan_ref[BIAS, :] + chan_ref[0:1, :] * window[8 : rows + 8, :]
+    for shift in range(1, mask_ref.shape[1]):
         moved = window[8 - shift : 8 - shift + rows, :]
-        mixed = mixed + taps_ref[shift : shift + 1, :] * (moved * mask_ref[:, shift : shift + 1])
+        mixed = mixed + chan_ref[shift : shift + 1, :] * (moved * mask_ref[:, shift : shift + 1])
     conv = mixed.astype(BF16)
     conv_ref[...] = conv
-    pre = jnp.dot(conv, gates_ref[...], preferred_element_type=F32) + gate_bias_ref[...]
-    rate = jax.nn.sigmoid(pre[:, :chans])
-    entry = jax.nn.sigmoid(pre[:, chans:])
+    pre = jnp.dot(conv, gates_ref[...], preferred_element_type=F32)
+    rate = jax.nn.sigmoid(pre[:, :chans] + chan_ref[RATE, :])
+    entry = jax.nn.sigmoid(pre[:, chans:] + chan_ref[ENTRY, :])
     rate_ref[...] = rate
     entry_ref[...] = entry
     keep = jnp.broadcast_to(mask_ref[:, 0:1], (rows, chans)) > 0.5
-    step, square = decay_parts(rate, softer_ref[...], keep)
+    step, square = decay_parts(rate, chan_ref[SOFTER, :], keep)
     put_lanes(decay, step, rows)
     put_lanes(value, jnp.sqrt(square) * entry * conv.astype(F32), rows)
     sweep(decay, value, inner, product, state_ref, run_ref, carry, False, 0)
@@ -898,7 +900,7 @@
     return pl.BlockSpec(shape, lambda i: (0, 0))
 
 
-def recur_forward(branch, halo, masks, taps, bias, blocks, gate_bias, softer):
+def recur_forward(branch, halo, masks, channels, blocks):
     rows, chans = branch.shape[0], halo.shape[1]
     wide = jax.ShapeDtypeStruct((rows, chans), F32)
     return pl.pallas_call(
@@ -912,11 +914,8 @@
             tile_spec(chans),
             fixed_spec((8, chans)),
             tile_spec(masks.shape[1]),
-            fixed_spec(taps.shape),
-            fixed_spec((1, chans)),
+            fixed_spec(channels.shape),
             pl.BlockSpec(blocks.shape, lambda i: (0, 0, 0)),
-            fixed_spec((1, 2 * chans)),
-            fixed_spec((1, chans)),
         ],
         out_specs=[tile_spec(chans)] * 5 + [fixed_spec((chans, 2 * chans))],
         scratch_shapes=[
@@ -931,10 +930,24 @@
             flops=2 * rows * chans * 2 * chans, bytes_accessed=24 * rows * chans, transcendentals=5 * rows * chans
         ),
         name="recur_forward",
-    )(branch, halo, masks, taps, bias, blocks, gate_bias, softer)
-
-
-def merge_kernel(local_ref, run_ref, enter_ref, pre_ref, weight_ref, state_ref, gated_ref, part_ref):
+    )(branch, halo, masks, channels, blocks)
+
+
+def merge_kernel(local_ref, run_ref, enter_ref, pre_ref, *refs):
+    *halves, state_ref, gated_ref, part_ref, weight_ref = refs
+    core = lax.axis_index("ctx")
+
+    @pl.when(pl.program_id(0) == 0)
+    def _():
+        if len(halves) == 1:
+            weight_ref[...] = halves[0][...]
+        else:
+            owners, _, size = halves[0].shape
+            for owner in range(owners):
+                for index, half in ((core, halves[0]), (1 - core, halves[1])):
+                    low = pl.multiple_of((2 * owner + index) * size, 128)
+                    weight_ref[:, pl.ds(low, size)] = half[owner]
+
     state = local_ref[...] + run_ref[...] * enter_ref[0:1, :]
     state_ref[...] = state
     pre = pre_ref[...].astype(F32)
@@ -943,29 +956,31 @@
     part_ref[...] = jnp.dot(gated, weight_ref[...], preferred_element_type=F32).astype(BF16)
 
 
-def merge_states(local, run, enter, branches, weight):
+def merge_states(local, run, enter, branches, weights, features):
     rows, chans = local.shape
-    features = weight.shape[1]
     shape = jax.ShapeDtypeStruct
     return pl.pallas_call(
         merge_kernel,
         grid=(rows // TILE,),
-        out_shape=(shape((rows, chans), F32), shape((rows, chans), BF16), shape((rows, features), BF16)),
+        out_shape=(
+            shape((rows, chans), F32), shape((rows, chans), BF16), shape((rows, features), BF16),
+            shape((chans, features), BF16),
+        ),
         in_specs=[
             tile_spec(chans), tile_spec(chans), fixed_spec((1, chans)),
             pl.BlockSpec((TILE, chans), lambda i: (i, 1)),
-            fixed_spec(weight.shape),
-        ],
-        out_specs=[tile_spec(chans), tile_spec(chans), tile_spec(features)],
+        ]
+        + [pl.BlockSpec(w.shape, lambda i, rank=w.ndim: (0,) * rank) for w in weights],
+        out_specs=[tile_spec(chans), tile_spec(chans), tile_spec(features), fixed_spec((chans, features))],
         cost_estimate=pl.CostEstimate(
             flops=2 * rows * chans * features, bytes_accessed=16 * rows * chans, transcendentals=rows * chans
         ),
         name="merge_states",
-    )(local, run, enter, branches, weight)
+    )(local, run, enter, branches, *weights)
 
 
 def adjoint_kernel(
-    rate_ref, up_ref, pre_ref, state_ref, mask_ref, softer_ref,
+    rate_ref, up_ref, pre_ref, state_ref, mask_ref, chan_ref,
     grad_ref, run_ref, head_ref, pre_grad_ref,
     decay, value, inner, product, carry,
 ):
@@ -986,7 +1001,7 @@
             decay[lane, rows : rows + 8, :] = decay[lane, 0:8, :]
 
     keep = jnp.broadcast_to(mask_ref[:, 0:1], (rows, chans)) > 0.5
-    gap = CGAIN * rate_ref[...] * softer_ref[...]
+    gap = CGAIN * rate_ref[...] * chan_ref[SOFTER, :]
     step = jnp.where(keep, jnp.exp(-gap), 0.0)
     put_lanes(decay, step, rows)
     gate, slope = gelu_pair(pre_ref[...].astype(F32))
@@ -997,7 +1012,7 @@
     head_ref[...] = jnp.broadcast_to(step[0:1, :] * carry[0:1, :], (8, chans))
 
 
-def recur_adjoint(rate, up, branches, state, masks, softer):
+def recur_adjoint(rate, up, branches, state, masks, channels):
     rows, chans = rate.shape
     count = rows // TILE
     wide = jax.ShapeDtypeStruct((rows, chans), F32)
@@ -1013,7 +1028,7 @@
             pl.BlockSpec((TILE, chans), lambda i: (count - 1 - i, 1)),
             tile_spec(chans, count),
             tile_spec(masks.shape[1], count),
-            fixed_spec((1, chans)),
+            fixed_spec(channels.shape),
         ],
         out_specs=[tile_spec(chans, count), tile_spec(chans, count), fixed_spec((8, chans)), tile_spec(chans, count)],
         scratch_shapes=[
@@ -1027,17 +1042,17 @@
             flops=8 * rows * chans, bytes_accessed=16 * rows * chans, transcendentals=rows * chans
         ),
         name="recur_adjoint",
-    )(rate, up, branches, state, masks, softer)
+    )(rate, up, branches, state, masks, channels)
 
 
 def backward_kernel(
     grad_ref, run_ref, enter_ref, rate_ref, entry_ref, conv_ref, state_ref, mask_ref,
-    branch_ref, pre_grad_ref, halo_ref, taps_ref, gates_ref, softer_ref,
+    branch_ref, pre_grad_ref, halo_ref, chan_ref, gates_ref,
     back_ref, tail_ref, head_ref, gate_grad_ref, sums_ref,
     shifts, edge,
 ):
     rows, chans = conv_ref.shape
-    width = taps_ref.shape[0]
+    width = mask_ref.shape[1]
     spot = pl.program_id(0)
     last = pl.num_programs(0) - 1
 
@@ -1054,7 +1069,7 @@
             shifts[shift - 1, rows : rows + 8, :] = shifts[shift - 1, 0:8, :]
 
     keep = jnp.broadcast_to(mask_ref[:, 0:1], (rows, chans)) > 0.5
-    softer = softer_ref[...]
+    softer = chan_ref[SOFTER, :]
     rate = rate_ref[...]
     entry = entry_ref[...]
     conv = conv_ref[...].astype(F32)
@@ -1085,12 +1100,12 @@
     add_row(2, d_entry.astype(F32))
     add_row(3, d_conv)
     add_row(4, d_conv * branch)
-    back = taps_ref[0:1, :] * d_conv
+    back = chan_ref[0:1, :] * d_conv
     for shift in range(1, width):
         shifts[shift - 1, 0:rows, :] = d_conv * mask_ref[:, shift : shift + 1]
         moved = shifts[shift - 1, shift : shift + rows, :]
         add_row(4 + shift, moved * branch)
-        back = back + taps_ref[shift : shift + 1, :] * moved
+        back = back + chan_ref[shift : shift + 1, :] * moved
     back_ref[:, 0:chans] = back.astype(BF16)
     back_ref[:, chans:] = pre_grad_ref[...]
 
@@ -1107,11 +1122,11 @@
             edge[8:16, :] = shifts[shift - 1, 0:8, :]
             moved = edge[shift : shift + 8, :]
             add_row(4 + shift, moved * halo)
-            head = head + taps_ref[shift : shift + 1, :] * moved
+            head = head + chan_ref[shift : shift + 1, :] * moved
         head_ref[...] = head
 
 
-def recur_backward(grad, run, enter, rate, entry, conv, state, masks, branch, pre_grad, halo, taps, gates, softer):
+def recur_backward(grad, run, enter, rate, entry, conv, state, masks, branch, pre_grad, halo, channels, gates):
     rows, chans = rate.shape
     count = rows // TILE
     edge = jax.ShapeDtypeStruct((8, chans), F32)
@@ -1132,9 +1147,8 @@
             wide,
             wide,
             fixed_spec((8, chans)),
-            fixed_spec(taps.shape),
+            fixed_spec(channels.shape),
             fixed_spec(gates.shape),
-            fixed_spec((1, chans)),
         ],
         out_specs=[
             tile_spec(2 * chans, count),
@@ -1144,14 +1158,14 @@
             fixed_spec((8, chans)),
         ],
         scratch_shapes=[
-            pltpu.VMEM((taps.shape[0] - 1, TILE + 8, chans), F32),
+            pltpu.VMEM((masks.shape[1] - 1, TILE + 8, chans), F32),
             pltpu.VMEM((16, chans), F32),
         ],
         cost_estimate=pl.CostEstimate(
             flops=8 * rows * chans * chans, bytes_accessed=28 * rows * chans, transcendentals=2 * rows * chans
         ),
         name="recur_backward",
-    )(grad, run, enter, rate, entry, conv, state, masks, branch, pre_grad, halo, taps, gates, softer)
+    )(grad, run, enter, rate, entry, conv, state, masks, branch, pre_grad, halo, channels, gates)
 
 
 def shards(
@@ -1183,14 +1197,20 @@
     feat_local = features // lax.axis_size("tp")
     feat_start = lax.axis_index("tp") * feat_local
 
+    def own(block):
+        return lax.dynamic_slice_in_dim(block, feat_start, feat_local, 1)
+
     square = lax.axis_size("fsdp") == 4
     gain_shard = jnp.concatenate(
         [jnp.stack([norm_mix, norm_feed]).astype(F32), jnp.zeros((6, norm_mix.shape[0]), F32)], axis=0
     )
     if square:
-        normed, normed_split, cotangent_split, gains, whole_in, whole_merge = enter(
-            tokens, cotangent, gain_shard, w_recur, w_gelu, w_merge
+        half = w_merge.shape[1] // 2
+        half_shard = lax.dynamic_slice_in_dim(w_merge, lax.axis_index("ctx") * half, half, 1)
+        normed, normed_split, cotangent_split, gains, whole_in = enter(
+            tokens, cotangent, gain_shard, w_recur, w_gelu
         )
+        merge_mine = lax.all_gather(after(half_shard, normed), "fsdp", axis=0)
     else:
         whole_in = gather_halves(jnp.concatenate([w_recur, w_gelu], axis=1), 0)
         whole_merge = gather_halves(w_merge, 1)
@@ -1208,19 +1228,21 @@
         [(local_ids[edge - max(shift, 1) : edge - max(shift, 1) + piece] == own_ids) for shift in range(width)],
         axis=1,
     ).astype(F32)
-    taps = conv_taps.astype(F32)
     blocks = jnp.stack([rate_gate.reshape(chans, block), entry_gate.reshape(chans, block)])
-    gate_bias = jnp.concatenate([rate_bias, entry_bias]).astype(F32)[None, :]
-    softer = jax.nn.softplus(-decay_logit)[None, :]
+    channels = jnp.concatenate(
+        [conv_taps.astype(F32)]
+        + [row.astype(F32)[None, :] for row in (conv_bias, rate_bias, entry_bias, jax.nn.softplus(-decay_logit))]
+    )
 
     rows_to_features = (((1,), (1,)), ((), ()))
     branches = jnp.dot(normed, whole_in, preferred_element_type=F32).astype(BF16)
     halo = shifted(branches[piece - 8 :, :chans], "ctx", 1)
-    conv, rate, entry, local_state, run, gates = recur_forward(
-        branches, halo, masks, taps, conv_bias.astype(F32)[None, :], blocks, gate_bias, softer
+    conv, rate, entry, local_state, run, gates = recur_forward(branches, halo, masks, channels, blocks)
+    state_in = shifted(local_state[piece - 8 :], "ctx", 1)[7:8]
+    merge_weights = (merge_mine, swap_cores(after(merge_mine, conv))) if square else (whole_merge,)
+    states, gated, part_merge, whole_merge = merge_states(
+        local_state, run, state_in, branches, merge_weights, features
     )
-    state_in = shifted(local_state[piece - 8 :], "ctx", 1)[7:8]
-    states, gated, part_merge = merge_states(local_state, run, state_in, branches, whole_merge)
 
     if square:
         merged, normed_two, normed_two_split, whole_mid, whole_down = middle(
@@ -1263,11 +1285,11 @@
     pair_merge = pair_sums(d_merge_split, gated, 1)
     half_merge = half_to_owners(pair_merge, 1)
     d_gated = lax.dot_general(d_merge_in, whole_merge, rows_to_features, preferred_element_type=F32)
-    local_grad, grad_run, first, d_gelu_pre = recur_adjoint(rate, d_gated, branches, states, masks, softer)
+    local_grad, grad_run, first, d_gelu_pre = recur_adjoint(rate, d_gated, branches, states, masks, channels)
     grad_in = shifted(first, "ctx", -1)[0:1]
     back, tail, head, gate_grads, sums = recur_backward(
         local_grad, grad_run, grad_in, rate, after(entry, half_mid, shard_down, pair_merge), conv, states, masks, branches, d_gelu_pre,
-        halo, taps, gates, softer
+        halo, channels, gates
     )
     returned = shifted(head, "ctx", -1)
     d_in = lax.dynamic_update_slice(back, (tail + returned).astype(BF16), (piece - 8, 0))
@@ -1275,7 +1297,8 @@
     part_one = after(part_one, half_merge)
     d_normed = lax.psum_scatter(part_one, "tp", scatter_dimension=1, tiled=True)
 
-    pair_in = pair_sums(normed_split, after(d_in, part_one), 0)
+    output = (own(tokens).astype(F32) + own(merged).astype(F32) + after(feed, part_one).astype(F32)).astype(BF16)
+    pair_in = after(pair_sums(normed_split, after(d_in, part_one), 0), output)
     inputs = tokens.astype(F32)
     scale_one = rms_scale(inputs)
     wide_part = part_one.astype(F32)
@@ -1303,11 +1326,7 @@
     shard_merge = both_halves(half_merge, 1)
     gate_sums = gate_sums.astype(F32).reshape(block, 2, heads, block).transpose(1, 2, 0, 3)
 
-    def own(block):
-        return lax.dynamic_slice_in_dim(block, feat_start, feat_local, 1)
-
     own_inputs = own(tokens).astype(F32)
-    output = (own_inputs + own(merged).astype(F32) + feed.astype(F32)).astype(BF16)
     grad_tokens = (
         own_resid_grad
         + scale_one * d_normed.astype(F32) * own(gain_one)

time: 598 us -> 596 us (level)
  Pallas kernels: 374 us -> 365 us
    pallas_call x1, Pallas kernels: 47.4 us -> 36.8 us  [enter(): pl.pallas_call(enter_kernel, out_shape=(shape((rows, features), BF16), sh...]
  transfers between devices with their start and end apart: 16 -> 18, of which waited for: 4 -> 3; matrix products, arithmetic and copies ran while one was open for 24% -> 26% of each run, Pallas kernels for 31% -> 34%
where the time goes in v7:
time: 596 us; the launch traced here: 590 us
  Pallas kernels  365 us (61%)
  matrix products  141 us (24%)
  other arithmetic  30.5 us (5%)
  local copies, waits for them, and re-layouts  25.6 us (4%)
  between operations  15 us (3%)
  starting transfers between devices  9.35 us (2%)
    pallas_call x1, Pallas kernels, middle(): pl.pallas_call(lambda *refs: middle_kernel(bool(shards), *refs), out_shap...  119 us
    pallas_call x1, Pallas kernels, turn(): pl.pallas_call(lambda *refs: turn_kernel(split, *refs), out_shape=tuple(o...  114 us
    dot_general x8, matrix products, product(): return lax.dot_general(*pair, rows_to_rows, preferred_element_type=F32)  54 us
    pallas_call x1, Pallas kernels, leave(): pl.pallas_call(leave_kernel, out_shape=(shape((part_in.shape[0] // 2, par...  39.1 us
    pallas_call x1, Pallas kernels, enter(): pl.pallas_call(enter_kernel, out_shape=(shape((rows, features), BF16), sh...  36.8 us
    dot_general x1, matrix products, shards(): lax.dot_general(d_mid, whole_mid, rows_to_features, preferred_element_typ...  20.1 us
    pallas_call x1, Pallas kernels, recur_backward(): pl.pallas_call(backward_kernel, grid=(count,), out_shape=(jax.ShapeDtypeS...  19.2 us
    dot_general x1, matrix products, shards(): jnp.dot(normed_two, whole_mid, preferred_element_type=F32).astype(BF16)  17 us
  transfers between devices with their start and end apart: 18, of which 3 were waited for; matrix products, arithmetic and copies ran while one was open for 26% of the time, Pallas kernels for 34%

profile of v7, /device:TPU:0, one launch (start us, length us, event | category | flops | bytes accessed | tf_op | source)
XLA Modules:
  0.0 590.2 jit_solution(1802265791738344571)
XLA Ops:
  10.0 36.8 %enter.1 = (bf16[1024,2048]{1,0:T(8,128)(2,1)}, bf16[2,1024,1024]{2,1,0:T(8,128)(2,1)}, bf16[2,1024,1024]{2,1,0:T(8,128)(2,1)}, f32[8,2048]{1,0:T(8,128)}, bf16[2048,1280]{1,0:T(8,128)(2,1)}) custom-call(bf16[1024,2048]{1,0:T(8,128)(2,1)} %refs_1_.3, bf16[1024,2048]{1,0:T(8,128)(2,1)} %refs_3_.3, f32[8,512]{1,0:T(8,128)} %fusion.59.gain_shard, ...), custom_call_target="tpu_custom_call" | custom-call | tf_op jit(solution)/shard_map/enter/pallas_call | solution.py:361
  47.1 8.9 %convolution_convert_fusion.5.branch_ref.pre_ref = bf16[1024,1280]{1,0:T(8,128)(2,1)S(1)} fusion(bf16[1024,2048]{1,0:T(8,128)(2,1)} %get-tuple-element.71, bf16[2048,1280]{1,0:T(8,128)(2,1)} %get-tuple-element.72), kind=kOutput, calls=%fused_computation.45 | convolution fusion | flops 5370019840 | bytes 12058624 | tf_op jit(solution)/shard_map/dot_general | solution.py:1238
  62.0 14.4 %recur_forward.1 = (bf16[1024,640]{1,0:T(8,128)(2,1)}, f32[1024,640]{1,0:T(8,128)}, f32[1024,640]{1,0:T(8,128)}, f32[1024,640]{1,0:T(8,128)}, f32[1024,640]{1,0:T(8,128)}, /*index=5*/bf16[640,1280]{1,0:T(8,128)(2,1)}) custom-call(bf16[1024,1280]{1,0:T(8,128)(2,1)} %copy-done.3, bf16[8,640]{1,0:T(8,128)(2,1)} %copy-done.20, ...), custom_call_target="tpu_custom_call" | custom-call | flops 1677721600 | bytes 15728640 | tf_op jit(solution)/shard_map/recur_forward/pallas_call | solution.py:906
  82.0 11.6 %merge_states.1 = (f32[1024,640]{1,0:T(8,128)}, bf16[1024,640]{1,0:T(8,128)(2,1)}, bf16[1024,2048]{1,0:T(8,128)(2,1)}, bf16[640,2048]{1,0:T(8,128)(2,1)}) custom-call(f32[1024,640]{1,0:T(8,128)} %get-tuple-element.73.local_ref, f32[1024,640]{1,0:T(8,128)} %get-tuple-element.74.run_ref, f32[1,640]{1,0:T(1,128)} %slice.158.enter_ref, ...), custom_call_target="tpu_custom_call" | custom-call | flops 2684354560 | bytes 10485760 | tf_op jit(solution)/shard_map/merge_states/pallas_call | solution.py:962
  93.6 118.5 %middle.1 = (bf16[1024,2048]{1,0:T(8,128)(2,1)}, bf16[1024,2048]{1,0:T(8,128)(2,1)}, bf16[2,1024,1024]{2,1,0:T(8,128)(2,1)}, bf16[2048,3072]{1,0:T(8,128)(2,1)}, bf16[1536,2048]{1,0:T(8,128)(2,1)}) custom-call(bf16[1024,2048]{1,0:T(8,128)(2,1)} %get-tuple-element.78.refs_0_, bf16[1024,2048]{1,0:T(8,128)(2,1)} %refs_1_.3, ...), custom_call_target="tpu_custom_call" | custom-call | bytes 400000000 | tf_op jit(solution)/shard_map/middle/pallas_call | solution.py:460
  212.2 17.0 %convolution_convert_fusion.1 = bf16[1024,3072]{1,0:T(8,128)(2,1)S(1)} fusion(bf16[1024,2048]{1,0:T(8,128)(2,1)} %get-tuple-element.81, bf16[2048,3072]{1,0:T(8,128)(2,1)} %get-tuple-element.88), kind=kOutput, calls=%fused_computation.40 | convolution fusion | flops 12888047616 | bytes 23068672 | tf_op jit(solution)/shard_map/dot_general | solution.py:1258
  235.4 8.3 %convolution_convert_fusion.4 = bf16[1024,2048]{1,0:T(8,128)(2,1)} fusion(bf16[1024,1536]{1,0:T(8,128)(2,1)S(1)} %fusion.11, bf16[1536,2048]{1,0:T(8,128)(2,1)S(1)} %copy-done.27), kind=kOutput, calls=%fused_computation.44 | convolution fusion | flops 6444548096 | bytes 13631488 | tf_op jit(solution)/shard_map/dot_general | solution.py:1261
  243.8 6.2 %convolution_convert_fusion.8 = bf16[1536,1024]{1,0:T(8,128)(2,1)S(1)} fusion(bf16[1024,1536]{1,0:T(8,128)(2,1)} %copy-done.8, bf16[2,1024,1024]{2,1,0:T(8,128)(2,1)} %get-tuple-element.90), kind=kOutput, calls=%fused_computation.48 | convolution fusion | flops 3222798336 | bytes 8388608 | tf_op jit(solution)/shard_map/dot_general | solution.py:56
  250.1 14.5 %fusion.7 = (bf16[1024,1536]{1,0:T(8,128)(2,1)}, bf16[1024,1536]{1,0:T(8,128)(2,1)}) fusion(bf16[1024,3072]{1,0:T(8,128)(2,1)S(1)} %bitcast.72, bf16[1024,2048]{1,0:T(8,128)(2,1)S(1)} %copy-done.5, bf16[1536,2048]{1,0:T(8,128)(2,1)} %get-tuple-element.83), kind=kOutput, calls=%fused_computation.26 | convolution fusion | flops 6484918272 | bytes 23068672 | tf_op jit(solution)/shard_map/dot_general | solution.py:1266
  264.7 11.8 %convolution_convert_fusion = bf16[1024,3072]{1,0:T(8,128)(2,1)} fusion(bf16[2,1024,1024]{2,1,0:T(8,128)(2,1)S(1)} %copy-done.31, bf16[1024,1536]{1,0:T(8,128)(2,1)} %get-tuple-element.132, bf16[1024,1536]{1,0:T(8,128)(2,1)} %get-tuple-element.131), kind=kOutput, calls=%fused_computation.39 | convolution fusion | flops 6458179584 | bytes 14680064 | tf_op jit(solution)/shard_map/dot_general | solution.py:56
  276.8 4.9 add_convert_fusion.1
  281.7 20.1 %convolution_convert_fusion.2.refs_0_ = bf16[1024,2048]{1,0:T(8,128)(2,1)} fusion(bf16[2048,3072]{1,0:T(8,128)(2,1)} %get-tuple-element.88, bf16[1024,1536]{1,0:T(8,128)(2,1)} %get-tuple-element.132, bf16[1024,1536]{1,0:T(8,128)(2,1)} %get-tuple-element.131), kind=kOutput, calls=%fused_computation.42 | convolution fusion | flops 12899581952 | bytes 23068672 | tf_op jit(solution)/shard_map/dot_general | solution.py:1273
  301.8 12.5 %add_convert_fusion = bf16[1024,3072]{1,0:T(8,128)(2,1)} fusion(bf16[1024,3072]{1,0:T(8,128)(2,1)} %collective-permute-done.4, bf16[2,1024,1024]{2,1,0:T(8,128)(2,1)S(1)} %copy-done.32, bf16[1024,1536]{1,0:T(8,128)(2,1)} %get-tuple-element.132, bf16[1024,1536]{1,0:T(8,128)(2,1)} %get-tuple-element.131), kind=kOutput, calls=%fused_computation.7 | convolution fusion | flops 6464471040 | bytes 20971520 | tf_op jit(solution)/shard_map/dot_general | solution.py:56
  314.4 114.0 %turn.1 = (f32[1024,512]{1,0:T(8,128)}, bf16[1024,2048]{1,0:T(8,128)(2,1)}, f32[8,2048]{1,0:T(8,128)}, bf16[2,1024,1024]{2,1,0:T(8,128)(2,1)}) custom-call(bf16[1024,2048]{1,0:T(8,128)(2,1)} %convolution_convert_fusion.2.refs_0_, bf16[1024,2048]{1,0:T(8,128)(2,1)} %refs_1_.3, bf16[1024,2048]{1,0:T(8,128)(2,1)} %get-tuple-element.80.refs_2_, ...), custom_call_target="tpu_custom_call" | custom-call | bytes 400000000 | tf_op jit(solution)/shard_map/turn/pallas_call | solution.py:516
  428.4 4.2 fusion.50
  433.1 8.0 %fusion.73.up_ref = f32[1024,640]{1,0:T(8,128)} fusion(bf16[1024,2048]{1,0:T(8,128)(2,1)} %get-tuple-element.96, bf16[640,2048]{1,0:T(8,128)(2,1)} %get-tuple-element.97), kind=kOutput, calls=%fused_computation.141 | convolution fusion | flops 2684354560 | bytes 9437184 | tf_op jit(solution)/shard_map/dot_general | solution.py:1287
  441.0 11.5 %recur_adjoint.1 = (f32[1024,640]{1,0:T(8,128)}, f32[1024,640]{1,0:T(8,128)}, f32[8,640]{1,0:T(8,128)}, bf16[1024,640]{1,0:T(8,128)(2,1)}) custom-call(f32[1024,640]{1,0:T(8,128)} %get-tuple-element.84.rate_ref, f32[1024,640]{1,0:T(8,128)} %fusion.73.up_ref, bf16[1024,1280]{1,0:T(8,128)(2,1)} %copy-done.3, f32[1024,640]{1,0:T(8,128)} %get-tuple-element.98.state_ref, ...), custom_call_target="tpu_custom_call" | custom-call | flops 5242880 | bytes 10485760 | tf_op jit(solution)/shard_map/recur_adjoint/pallas_call | solution.py:1019
  454.0 4.6 add_convert_fusion.3
  461.5 19.2 %recur_backward.1 = (bf16[1024,1280]{1,0:T(8,128)(2,1)}, f32[8,640]{1,0:T(8,128)}, f32[8,640]{1,0:T(8,128)}, f32[640,1280]{1,0:T(8,128)}, f32[8,640]{1,0:T(8,128)}) custom-call(f32[1024,640]{1,0:T(8,128)} %get-tuple-element.99.grad_ref, f32[1024,640]{1,0:T(8,128)} %get-tuple-element.100.run_ref, f32[1,640]{1,0:T(1,128)} %slice.161.enter_ref, ...), custom_call_target="tpu_custom_call" | custom-call | flops 3355443200 | bytes 18350080 | tf_op jit(solution)/shard_map/recur_backward/pallas_call | solution.py:1134
  485.4 10.3 %convolution_convert_fusion.6 = bf16[1024,2048]{1,0:T(8,128)(2,1)} fusion(bf16[1024,1280]{1,0:T(8,128)(2,1)} %fusion.57, bf16[2048,1280]{1,0:T(8,128)(2,1)} %get-tuple-element.72), kind=kOutput, calls=%fused_computation.46 | convolution fusion | flops 5370806272 | bytes 12058624 | tf_op jit(solution)/shard_map/dot_general | solution.py:1296
  505.9 4.3 convolution_convert_fusion.7
  525.0 5.7 add_convert_fusion.2.part_in
  530.7 39.1 %leave.1 = (bf16[512,1280]{1,0:T(8,128)(2,1)}, bf16[160,1280]{1,0:T(8,128)(2,1)}, f32[8,640]{1,0:T(8,128)}, f32[32,128]{1,0:T(8,128)}, f32[8,128]{1,0:T(8,128)}) custom-call(bf16[1024,1280]{1,0:T(8,128)(2,1)} %add_convert_fusion.2.part_in, bf16[160,1280]{1,0:T(8,128)(2,1)} %add_convert_fusion.4.gates, f32[8,640]{1,0:T(8,128)} %get-tuple-element.118.sums, ...), custom_call_target="tpu_custom_call" | custom-call | bytes 160000000 | tf_op jit(solution)/shard_map/leave/pallas_call | solution.py:738
  579.3 3.8 fusion.22
  (172 shorter events, 65.0 us)
Async XLA Ops:
  7.2 69.1 %all-gather.3.cloned.1.call-start = ((), (), s32[]{:S(2)}) async-start(), calls=%async_computation.10 | async-start | bytes 1638400 | tf_op jit(solution)/shard_map/all_gather | solution.py:1213
  46.9 385.7 %reduce-scatter.6.cloned.1.call-start = ((), (), s32[]{:S(2)}) async-start(), calls=%async_computation.5 | async-start | bytes 5242880 | tf_op jit(solution)/shard_map/reduce_scatter | solution.py:1262
  47.0 13.7 %copy-start.26 = (bf16[640]{0:T(1024)(128)(2,1)S(1)}, bf16[640]{0:T(1024)(128)(2,1)}, u32[]{:S(2)}) copy-start(bf16[640]{0:T(1024)(128)(2,1)} %param.34) | copy-start | bytes 3844
  47.0 13.7 %copy-start.22 = (bf16[4,640]{1,0:T(4,128)(2,1)S(1)}, bf16[4,640]{1,0:T(4,128)(2,1)}, u32[]{:S(2)}) copy-start(bf16[4,640]{1,0:T(4,128)(2,1)} %param.29) | copy-start | bytes 15364
  56.0 5.3 collective-permute-start
  76.3 4.6 collective-permute-start.2
  77.2 3.2 collective-permute-start.1
  243.7 188.8 %reduce-scatter.8.cloned.1.call-start = ((), (), s32[]{:S(2)}) async-start(), calls=%async_computation.6 | async-start | bytes 3932160 | tf_op jit(solution)/shard_map/reduce_scatter | solution.py:65
  250.0 14.7 %copy-start.31 = (bf16[2,1024,1024]{2,1,0:T(8,128)(2,1)S(1)}, bf16[2,1024,1024]{2,1,0:T(8,128)(2,1)}, u32[]{:S(2)}) copy-start(bf16[2,1024,1024]{2,1,0:T(8,128)(2,1)} %get-tuple-element.92) | copy-start | bytes 12582916
  250.0 26.8 %collective-permute-start.3 = (bf16[1536,1024]{1,0:T(8,128)(2,1)S(1)}, bf16[1536,1024]{1,0:T(8,128)(2,1)S(1)}, u32[]{:S(2)}, u32[]{:S(2)}) collective-permute-start(bf16[1536,1024]{1,0:T(8,128)(2,1)S(1)} %convolution_convert_fusion.8), channel_id=1, source_target_pairs={{0,4},{4,0},{1,5},{5,1},{2,6},{6,2},{3,7},{7,3},{8,12},{12,8},{9,1... | collective-permute-start | bytes 9437192 | tf_op jit(solution)/shard_map/ppermute | solution.py:20
  276.4 25.4 %collective-permute-start.4 = (bf16[1024,3072]{1,0:T(8,128)(2,1)}, bf16[1024,3072]{1,0:T(8,128)(2,1)}, u32[]{:S(2)}, u32[]{:S(2)}) collective-permute-start(bf16[1024,3072]{1,0:T(8,128)(2,1)} %convolution_convert_fusion), channel_id=1, source_target_pairs={{0,4},{4,0},{1,5},{5,1},{2,6},{6,2},{3,7},{7,3},{8,12},{12,8},{9,1... | collective-permute-start | bytes 18874376 | tf_op jit(solution)/shard_map/ppermute | solution.py:20
  281.7 179.8 %reduce-scatter.10.cloned.1.call-start = ((), (), s32[]{:S(2)}) async-start(), calls=%async_computation.7 | async-start | bytes 7864320 | tf_op jit(solution)/shard_map/reduce_scatter | solution.py:65
  281.7 20.1 %copy-start.32 = (bf16[2,1024,1024]{2,1,0:T(8,128)(2,1)S(1)}, bf16[2,1024,1024]{2,1,0:T(8,128)(2,1)}, u32[]{:S(2)}) copy-start(bf16[2,1024,1024]{2,1,0:T(8,128)(2,1)} %get-tuple-element.92) | copy-start | bytes 12582916
  314.3 181.4 %reduce-scatter.12.cloned.1.call-start = ((), (), s32[]{:S(2)}) async-start(), calls=%async_computation.8 | async-start | bytes 1638400 | tf_op jit(solution)/shard_map/reduce_scatter | solution.py:65
  314.4 114.0 %copy-start.35 = (bf16[1024,640]{1,0:T(8,128)(2,1)S(1)}, bf16[1024,640]{1,0:T(8,128)(2,1)}, u32[]{:S(2)}) copy-start(bf16[1024,640]{1,0:T(8,128)(2,1)} %get-tuple-element.103) | copy-start | bytes 3932164
  432.6 21.5 %collective-permute-start.7 = (bf16[640,1024]{1,0:T(8,128)(2,1)}, bf16[640,1024]{1,0:T(8,128)(2,1)}, u32[]{:S(2)}, u32[]{:S(2)}) collective-permute-start(bf16[640,1024]{1,0:T(8,128)(2,1)} %fusion.50), channel_id=1, source_target_pairs={{0,4},{4,0},{1,5},{5,1},{2,6},{6,2},{3,7},{7,3},{8,12},{12,8},{9,1... | collective-permute-start | bytes 3932168 | tf_op jit(solution)/shard_map/ppermute | solution.py:20
  432.6 26.7 %collective-permute-start.6 = (bf16[1536,256]{1,0:T(8,128)(2,1)}, bf16[1536,256]{1,0:T(8,128)(2,1)S(1)}, u32[]{:S(2)}, u32[]{:S(2)}) collective-permute-start(bf16[1536,256]{1,0:T(8,128)(2,1)} %reduce-scatter.8.cloned.1.call-done), channel_id=1, source_target_pairs={{0,4},{4,0},{1,5},{5,1},{2,6},{6,2},{3,7},{7,3},{8,12},{12,8},{9,1... | collective-permute-start | bytes 2359304 | tf_op jit(solution)/shard_map/ppermute | solution.py:20
  452.6 6.1 %collective-permute-start.5 = (f32[8,640]{1,0:T(8,128)}, f32[8,640]{1,0:T(8,128)S(1)}, u32[]{:S(2)}, u32[]{:S(2)}) collective-permute-start(f32[8,640]{1,0:T(8,128)} %get-tuple-element.101), channel_id=1, source_target_pairs={{4,0},{5,1},{6,2},{7,3},{12,8},{13,9},{14,10},{15,11},{20,16},{21,... | collective-permute-start | bytes 61448 | tf_op jit(solution)/shard_map/ppermute | solution.py:26
  458.6 120.7 %reduce-scatter.14.cloned.1.call-start = ((), (), s32[]{:S(2)}) async-start(), calls=%async_computation.9 | async-start | bytes 5242880 | tf_op jit(solution)/shard_map/reduce_scatter | solution.py:1298
  480.7 3.3 collective-permute-start.8
  499.9 1.7 collective-permute-start.10
  502.9 14.4 %collective-permute-start.11 = (bf16[256,3072]{1,0:T(8,128)(2,1)S(1)}, bf16[256,3072]{1,0:T(8,128)(2,1)}, u32[]{:S(2)}, u32[]{:S(2)}) collective-permute-start(bf16[256,3072]{1,0:T(8,128)(2,1)S(1)} %copy-done.10), channel_id=1, source_target_pairs={{0,4},{4,0},{1,5},{5,1},{2,6},{6,2},{3,7},{7,3},{8,12},{12,8},{9,1... | collective-permute-start | bytes 4718600 | tf_op jit(solution)/shard_map/ppermute | solution.py:20
  510.2 13.2 %collective-permute-start.9 = (bf16[1024,1280]{1,0:T(8,128)(2,1)}, bf16[1024,1280]{1,0:T(8,128)(2,1)}, u32[]{:S(2)}, u32[]{:S(2)}) collective-permute-start(bf16[1024,1280]{1,0:T(8,128)(2,1)} %convolution_convert_fusion.7), channel_id=1, source_target_pairs={{0,4},{4,0},{1,5},{5,1},{2,6},{6,2},{3,7},{7,3},{8,12},{12,8},{9,1... | collective-permute-start | bytes 7864328 | tf_op jit(solution)/shard_map/ppermute | solution.py:20
  530.7 45.1 %copy-start.19 = (f32[640]{0:T(1024)S(1)}, f32[640]{0:T(1024)}, u32[]{:S(2)}) copy-start(f32[640]{0:T(1024)} %param.35) | copy-start | bytes 7684
  (32 other events, 215.0 us)
Sparse Core Ops, SparseCore 0:
  47.0 28.9 all-gather.2
  243.9 74.7 reduce-scatter.5
  322.3 45.1 reduce-scatter.7
  370.3 70.0 reduce-scatter.9
  458.7 30.2 reduce-scatter.11
  495.8 78.1 reduce-scatter.13

commit v8 on v7

--- a/solution.py
+++ b/solution.py
@@ -68,6 +68,10 @@
 def both_halves(total, dim):
     other = swap_cores(total)
     core = lax.axis_index("ctx")
+    if dim == 0:
+        place = lax.broadcasted_iota(jnp.int32, (2, *total.shape), 0)
+        both = jnp.where(place == core, total[None], other[None])
+        return both.reshape(2 * total.shape[0], total.shape[1])
     first = jnp.where(core == 0, total, other)
     second = jnp.where(core == 0, other, total)
     return jnp.concatenate([first, second], axis=dim).astype(F32)
@@ -294,12 +298,13 @@
 
 
 CHUNK = 32
+LANES = 128
 LINE_COST = pl.CostEstimate(flops=0, bytes_accessed=400_000_000, transcendentals=0)
 
 
 def enter_kernel(
     tokens, upstream, gain_shard, recur, gelu,
-    normed, halves, upstream_halves, gains, whole_in,
+    normed, halves, upstream_halves, gains, scales, whole_in,
     stage_recur, stage_gelu, send, arrive, local, gain_send, gain_arrive,
 ):
     square = Square()
@@ -326,7 +331,9 @@
     def norm(t, carry):
         rows = pl.ds(pl.multiple_of(t * CHUNK, CHUNK), CHUNK)
         block = tokens[rows, :].astype(F32)
-        block = (block * rms_scale(block) * gains[0:1, :]).astype(BF16)
+        scale = rms_scale(block)
+        scales[rows, :] = jnp.broadcast_to(scale, (CHUNK, LANES))
+        block = (block * scale * gains[0:1, :]).astype(BF16)
         normed[rows, :] = block
         put_split(halves, rows, block)
         put_split(upstream_halves, rows, upstream[rows, :])
@@ -365,10 +372,11 @@
             shape((2, rows, features // 2), BF16),
             shape((2, rows, features // 2), BF16),
             shape((8, features), F32),
+            shape((rows, LANES), F32),
             shape((features, 2 * inner), BF16),
         ),
         in_specs=[NEAR, NEAR, NEAR, ANY, ANY],
-        out_specs=[NEAR, NEAR, NEAR, NEAR, ANY],
+        out_specs=[NEAR, NEAR, NEAR, NEAR, NEAR, ANY],
         scratch_shapes=gather_scratch([recur, gelu]) + [dma((3,)), dma((3,))],
         compiler_params=pltpu.CompilerParams(collective_id=1, has_side_effects=True),
         name="enter",
@@ -661,6 +669,7 @@
     gate_copy(0).start()
     core_copy(0).start()
     core_copy(1).start()
+    scatter.start(0)
     for k in range(count):
         @pl.when(place != k)
         def _():
@@ -679,7 +688,6 @@
         cols = slice(k * gate_cols, (k + 1) * gate_cols)
         gate_half[k] = rounded_sum(gates[my_rows, cols], gate_core[:, cols])
         gate_copy(1 + k).start()
-    scatter.start(0)
     for k in (0, 1):
         for j in range(3):
             square_copy(k, j).wait_recv()
@@ -783,9 +791,6 @@
     return jnp.where(keep, decay, 0.0), jnp.where(keep, square, 1.0)
 
 
-LANES = 128
-
-
 def put_lanes(ref, block, rows):
     for lane in range(ref.shape[0]):
         ref[lane, 0:rows, :] = block[:, lane * LANES : (lane + 1) * LANES]
@@ -854,7 +859,7 @@
 
 def forward_kernel(
     branch_ref, halo_ref, mask_ref, chan_ref, blocks_ref,
-    conv_ref, rate_ref, entry_ref, state_ref, run_ref, gates_ref,
+    conv_ref, rate_ref, entry_ref, state_ref, run_ref, gates_ref, tail_ref,
     window, decay, value, inner, product, carry,
 ):
     rows, chans = conv_ref.shape
@@ -888,6 +893,7 @@
     put_lanes(decay, step, rows)
     put_lanes(value, jnp.sqrt(square) * entry * conv.astype(F32), rows)
     sweep(decay, value, inner, product, state_ref, run_ref, carry, False, 0)
+    tail_ref[...] = state_ref[rows - 8 :, :]
 
 
 def tile_spec(width, count=None):
@@ -909,6 +915,7 @@
         out_shape=(
             jax.ShapeDtypeStruct((rows, chans), BF16), wide, wide, wide, wide,
             jax.ShapeDtypeStruct((chans, 2 * chans), BF16),
+            jax.ShapeDtypeStruct((8, chans), F32),
         ),
         in_specs=[
             tile_spec(chans),
@@ -917,7 +924,7 @@
             fixed_spec(channels.shape),
             pl.BlockSpec(blocks.shape, lambda i: (0, 0, 0)),
         ],
-        out_specs=[tile_spec(chans)] * 5 + [fixed_spec((chans, 2 * chans))],
+        out_specs=[tile_spec(chans)] * 5 + [fixed_spec((chans, 2 * chans)), fixed_spec((8, chans))],
         scratch_shapes=[
             pltpu.VMEM((TILE + 8, chans), F32),
             pltpu.VMEM((chans // LANES, TILE, LANES), F32),
@@ -948,7 +955,7 @@
                     low = pl.multiple_of((2 * owner + index) * size, 128)
                     weight_ref[:, pl.ds(low, size)] = half[owner]
 
-    state = local_ref[...] + run_ref[...] * enter_ref[0:1, :]
+    state = local_ref[...] + run_ref[...] * enter_ref[7:8, :]
     state_ref[...] = state
     pre = pre_ref[...].astype(F32)
     gated = (state * gelu_pair(pre)[0]).astype(BF16)
@@ -967,7 +974,7 @@
             shape((chans, features), BF16),
         ),
         in_specs=[
-            tile_spec(chans), tile_spec(chans), fixed_spec((1, chans)),
+            tile_spec(chans), tile_spec(chans), fixed_spec((8, chans)),
             pl.BlockSpec((TILE, chans), lambda i: (i, 1)),
         ]
         + [pl.BlockSpec(w.shape, lambda i, rank=w.ndim: (0,) * rank) for w in weights],
@@ -1142,7 +1149,7 @@
             jax.ShapeDtypeStruct((8, chans), F32),
         ),
         in_specs=[
-            wide, wide, fixed_spec((1, chans)), wide, wide, wide, wide,
+            wide, wide, fixed_spec((8, chans)), wide, wide, wide, wide,
             tile_spec(masks.shape[1], count),
             wide,
             wide,
@@ -1207,7 +1214,7 @@
     if square:
         half = w_merge.shape[1] // 2
         half_shard = lax.dynamic_slice_in_dim(w_merge, lax.axis_index("ctx") * half, half, 1)
-        normed, normed_split, cotangent_split, gains, whole_in = enter(
+        normed, normed_split, cotangent_split, gains, scales, whole_in = enter(
             tokens, cotangent, gain_shard, w_recur, w_gelu
         )
         merge_mine = lax.all_gather(after(half_shard, normed), "fsdp", axis=0)
@@ -1219,6 +1226,7 @@
         normed = (inputs * rms_scale(inputs) * gains[0:1]).astype(BF16)
         normed_split = split_features(normed)
         cotangent_split = split_features(cotangent)
+        scales = rms_scale(inputs)
     gain_one = gains[0:1]
 
     padded_ids = jnp.concatenate([jnp.full((edge,), -1, jnp.int32), segments])
@@ -1237,8 +1245,8 @@
     rows_to_features = (((1,), (1,)), ((), ()))
     branches = jnp.dot(normed, whole_in, preferred_element_type=F32).astype(BF16)
     halo = shifted(branches[piece - 8 :, :chans], "ctx", 1)
-    conv, rate, entry, local_state, run, gates = recur_forward(branches, halo, masks, channels, blocks)
-    state_in = shifted(local_state[piece - 8 :], "ctx", 1)[7:8]
+    conv, rate, entry, local_state, run, gates, state_tail = recur_forward(branches, halo, masks, channels, blocks)
+    state_in = shifted(state_tail, "ctx", 1)
     merge_weights = (merge_mine, swap_cores(after(merge_mine, conv))) if square else (whole_merge,)
     states, gated, part_merge, whole_merge = merge_states(
         local_state, run, state_in, branches, merge_weights, features
@@ -1279,14 +1287,14 @@
     d_merge_split = turned[3] if square else split_features(d_merge_in)
     half_down = half_to_owners(pair_down, 1)
     half_mid = half_to_owners(pair_mid, 0)
-    d_merge_in = after(d_merge_in, half_down, feed)
+    d_merge_in, d_merge_split = after((d_merge_in, d_merge_split), feed)
 
     shard_down = both_halves(half_down, 1)
     pair_merge = pair_sums(d_merge_split, gated, 1)
     half_merge = half_to_owners(pair_merge, 1)
     d_gated = lax.dot_general(d_merge_in, whole_merge, rows_to_features, preferred_element_type=F32)
-    local_grad, grad_run, first, d_gelu_pre = recur_adjoint(rate, d_gated, branches, states, masks, channels)
-    grad_in = shifted(first, "ctx", -1)[0:1]
+    local_grad, grad_run, first, d_gelu_pre = recur_adjoint(after(rate, half_down), d_gated, branches, states, masks, channels)
+    grad_in = shifted(first, "ctx", -1)
     back, tail, head, gate_grads, sums = recur_backward(
         local_grad, grad_run, grad_in, rate, after(entry, half_mid, shard_down, pair_merge), conv, states, masks, branches, d_gelu_pre,
         halo, channels, gates
@@ -1297,10 +1305,9 @@
     part_one = after(part_one, half_merge)
     d_normed = lax.psum_scatter(part_one, "tp", scatter_dimension=1, tiled=True)
 
-    output = (own(tokens).astype(F32) + own(merged).astype(F32) + after(feed, part_one).astype(F32)).astype(BF16)
-    pair_in = after(pair_sums(normed_split, after(d_in, part_one), 0), output)
+    pair_in = pair_sums(normed_split, after(d_in, part_one), 0)
     inputs = tokens.astype(F32)
-    scale_one = rms_scale(inputs)
+    scale_one = scales[:, :1]
     wide_part = part_one.astype(F32)
     stat_one = jnp.sum(wide_part * inputs * gain_one, axis=-1)
     grad_mix = jnp.sum(wide_part * inputs * scale_one, axis=0)
@@ -1312,7 +1319,7 @@
         own_in, gate_sums, row_sums, both_norms, line_stats = leave(
             pair_in, diagonal, sums, norm_sums.reshape(-1, 128), stat_one.reshape(-1, 128)
         )
-        shard_in = own_in.astype(F32)
+        shard_in = own_in
         both_norms = both_norms.reshape(2, features)
         stat_one = line_stats.reshape(-1)
     else:
@@ -1327,6 +1334,7 @@
     gate_sums = gate_sums.astype(F32).reshape(block, 2, heads, block).transpose(1, 2, 0, 3)
 
     own_inputs = own(tokens).astype(F32)
+    output = (own_inputs + own(merged).astype(F32) + feed.astype(F32)).astype(BF16)
     grad_tokens = (
         own_resid_grad
         + scale_one * d_normed.astype(F32) * own(gain_one)
@@ -1339,11 +1347,11 @@
     return (
         output,
         grad_tokens,
-        shard_in[:, :chans],
-        shard_in[:, chans:],
+        shard_in[:, :chans].astype(F32),
+        shard_in[:, chans:].astype(F32),
         shard_merge,
-        shard_mid[:, :units],
-        shard_mid[:, units:],
+        shard_mid[:, :units].astype(F32),
+        shard_mid[:, units:].astype(F32),
         shard_down,
         own_norms[0],
         own_norms[1],

time: 596 us -> 590 us (0.990)
  local copies, waits for them, and re-layouts: 25.6 us -> 18.6 us
    slice x5 -> x0, local copies, waits for them, and re-layouts: 7.21 us -> none  [the longest x1 3.65 us: shards(): shard_mid[:, units:]]
  transfers between devices with their start and end apart: 18 -> 18, of which waited for: 3 -> 3; matrix products, arithmetic and copies ran while one was open for 26% -> 25% of each run, Pallas kernels for 34% -> 34%
where the time goes in v8:
time: 590 us; the launch traced here: 584 us
  Pallas kernels  365 us (62%)
  matrix products  144 us (24%)
  other arithmetic  28 us (5%)
  local copies, waits for them, and re-layouts  18.6 us (3%)
  between operations  15.1 us (3%)
  starting transfers between devices  9.36 us (2%)
    pallas_call x1, Pallas kernels, middle(): pl.pallas_call(lambda *refs: middle_kernel(bool(shards), *refs), out_shap...  119 us
    pallas_call x1, Pallas kernels, turn(): pl.pallas_call(lambda *refs: turn_kernel(split, *refs), out_shape=tuple(o...  114 us
    dot_general x8, matrix products, product(): return lax.dot_general(*pair, rows_to_rows, preferred_element_type=F32)  56.7 us
    pallas_call x1, Pallas kernels, leave(): pl.pallas_call(leave_kernel, out_shape=(shape((part_in.shape[0] // 2, par...  38.4 us
    pallas_call x1, Pallas kernels, enter(): pl.pallas_call(enter_kernel, out_shape=(shape((rows, features), BF16), sh...  36.9 us
    dot_general x1, matrix products, shards(): lax.dot_general(d_mid, whole_mid, rows_to_features, preferred_element_typ...  20.1 us
    pallas_call x1, Pallas kernels, recur_backward(): pl.pallas_call(backward_kernel, grid=(count,), out_shape=(jax.ShapeDtypeS...  19.3 us
    dot_general x1, matrix products, shards(): jnp.dot(normed_two, whole_mid, preferred_element_type=F32).astype(BF16)  17.1 us
  transfers between devices with their start and end apart: 18, of which 3 were waited for; matrix products, arithmetic and copies ran while one was open for 25% of the time, Pallas kernels for 34%

profile of v8, /device:TPU:0, one launch (start us, length us, event | category | flops | bytes accessed | tf_op | source)
XLA Modules:
  0.0 583.8 jit_solution(2510670207258334653)
XLA Ops:
  10.0 36.9 %enter.1 = (bf16[1024,2048]{1,0:T(8,128)(2,1)}, bf16[2,1024,1024]{2,1,0:T(8,128)(2,1)}, bf16[2,1024,1024]{2,1,0:T(8,128)(2,1)}, f32[8,2048]{1,0:T(8,128)}, f32[1...) custom-call(bf16[1024,2048]{1,0:T(8,128)(2,1)} %refs_1_.3, bf16[1024,2048]{1,0:T(8,128)(2,1)} %refs_3_.3, ...), custom_call_target="tpu_custom_call" | custom-call | tf_op jit(solution)/shard_map/enter/pallas_call | solution.py:368
  47.1 8.9 %convolution_convert_fusion.5.branch_ref.pre_ref = bf16[1024,1280]{1,0:T(8,128)(2,1)S(1)} fusion(bf16[1024,2048]{1,0:T(8,128)(2,1)} %get-tuple-element.73, bf16[2048,1280]{1,0:T(8,128)(2,1)} %get-tuple-element.74), kind=kOutput, calls=%fused_computation.43 | convolution fusion | flops 5370019840 | bytes 12058624 | tf_op jit(solution)/shard_map/dot_general | solution.py:1246
  62.0 14.4 %recur_forward.1 = (bf16[1024,640]{1,0:T(8,128)(2,1)}, f32[1024,640]{1,0:T(8,128)}, f32[1024,640]{1,0:T(8,128)}, f32[1024,640]{1,0:T(8,128)}, f32[1024,640]{1,0:...) custom-call(bf16[1024,1280]{1,0:T(8,128)(2,1)} %copy-done.3, bf16[8,640]{1,0:T(8,128)(2,1)} %copy-done.24, ...), custom_call_target="tpu_custom_call" | custom-call | flops 1677721600 | bytes 15728640 | tf_op jit(solution)/shard_map/recur_forward/pallas_call | solution.py:912
  81.0 11.6 %merge_states.1 = (f32[1024,640]{1,0:T(8,128)}, bf16[1024,640]{1,0:T(8,128)(2,1)}, bf16[1024,2048]{1,0:T(8,128)(2,1)}, bf16[640,2048]{1,0:T(8,128)(2,1)}) custom-call(f32[1024,640]{1,0:T(8,128)} %get-tuple-element.75.local_ref, f32[1024,640]{1,0:T(8,128)} %get-tuple-element.76.run_ref, f32[8,640]{1,0:T(8,128)} %copy-done.20, bf16[1024,1280]{1,0:T(8,128)(2,1)} %copy-done.3, ...), custom_call_target="tpu_custom_call" | custom-call | flops 2684354560 | bytes 10485760 | tf_op jit(solution)/shard_map/merge_states/pallas_call | solution.py:969
  92.6 118.6 %middle.1 = (bf16[1024,2048]{1,0:T(8,128)(2,1)}, bf16[1024,2048]{1,0:T(8,128)(2,1)}, bf16[2,1024,1024]{2,1,0:T(8,128)(2,1)}, bf16[2048,3072]{1,0:T(8,128)(2,1)}, bf16[1536,2048]{1,0:T(8,128)(2,1)}) custom-call(bf16[1024,2048]{1,0:T(8,128)(2,1)} %get-tuple-element.81.refs_0_, bf16[1024,2048]{1,0:T(8,128)(2,1)} %refs_1_.3, ...), custom_call_target="tpu_custom_call" | custom-call | bytes 400000000 | tf_op jit(solution)/shard_map/middle/pallas_call | solution.py:468
  211.2 17.1 %convolution_convert_fusion.1 = bf16[1024,3072]{1,0:T(8,128)(2,1)S(1)} fusion(bf16[1024,2048]{1,0:T(8,128)(2,1)} %get-tuple-element.84, bf16[2048,3072]{1,0:T(8,128)(2,1)} %get-tuple-element.90), kind=kOutput, calls=%fused_computation.38 | convolution fusion | flops 12888047616 | bytes 23068672 | tf_op jit(solution)/shard_map/dot_general | solution.py:1266
  234.5 8.3 %convolution_convert_fusion.4 = bf16[1024,2048]{1,0:T(8,128)(2,1)} fusion(bf16[1024,1536]{1,0:T(8,128)(2,1)S(1)} %fusion.10, bf16[1536,2048]{1,0:T(8,128)(2,1)S(1)} %copy-done.31), kind=kOutput, calls=%fused_computation.42 | convolution fusion | flops 6444548096 | bytes 13631488 | tf_op jit(solution)/shard_map/dot_general | solution.py:1269
  242.9 6.2 %convolution_convert_fusion.8 = bf16[1536,1024]{1,0:T(8,128)(2,1)S(1)} fusion(bf16[1024,1536]{1,0:T(8,128)(2,1)} %copy-done.8, bf16[2,1024,1024]{2,1,0:T(8,128)(2,1)} %get-tuple-element.92), kind=kOutput, calls=%fused_computation.46 | convolution fusion | flops 3222798336 | bytes 8388608 | tf_op jit(solution)/shard_map/dot_general | solution.py:56
  249.2 14.5 %fusion.6 = (bf16[1024,1536]{1,0:T(8,128)(2,1)}, bf16[1024,1536]{1,0:T(8,128)(2,1)}) fusion(bf16[1024,3072]{1,0:T(8,128)(2,1)S(1)} %bitcast.76, bf16[1024,2048]{1,0:T(8,128)(2,1)S(1)} %copy-done.5, bf16[1536,2048]{1,0:T(8,128)(2,1)} %get-tuple-element.86), kind=kOutput, calls=%fused_computation.24 | convolution fusion | flops 6484918272 | bytes 23068672 | tf_op jit(solution)/shard_map/dot_general | solution.py:1274
  263.8 11.8 %convolution_convert_fusion = bf16[1024,3072]{1,0:T(8,128)(2,1)} fusion(bf16[2,1024,1024]{2,1,0:T(8,128)(2,1)S(1)} %copy-done.34, bf16[1024,1536]{1,0:T(8,128)(2,1)} %get-tuple-element.138, bf16[1024,1536]{1,0:T(8,128)(2,1)} %get-tuple-element.137), kind=kOutput, calls=%fused_computation.37 | convolution fusion | flops 6458179584 | bytes 14680064 | tf_op jit(solution)/shard_map/dot_general | solution.py:56
  275.9 4.9 add_convert_fusion.1
  280.8 20.1 %convolution_convert_fusion.2.refs_0_ = bf16[1024,2048]{1,0:T(8,128)(2,1)} fusion(bf16[2048,3072]{1,0:T(8,128)(2,1)} %get-tuple-element.90, bf16[1024,1536]{1,0:T(8,128)(2,1)} %get-tuple-element.138, bf16[1024,1536]{1,0:T(8,128)(2,1)} %get-tuple-element.137), kind=kOutput, calls=%fused_computation.40 | convolution fusion | flops 12899581952 | bytes 23068672 | tf_op jit(solution)/shard_map/dot_general | solution.py:1281
  301.0 12.5 %add_convert_fusion = bf16[1024,3072]{1,0:T(8,128)(2,1)} fusion(bf16[1024,3072]{1,0:T(8,128)(2,1)} %collective-permute-done.4, bf16[2,1024,1024]{2,1,0:T(8,128)(2,1)S(1)} %copy-done.35, bf16[1024,1536]{1,0:T(8,128)(2,1)} %get-tuple-element.138, bf16[1024,1536]{1,0:T(8,128)(2,1)} %get-tuple-element.137), kind=kOutput, calls=%fused_computation.7 | convolution fusion | flops 6464471040 | bytes 20971520 | tf_op jit(solution)/shard_map/dot_general | solution.py:56
  313.6 114.4 %turn.1 = (f32[1024,512]{1,0:T(8,128)}, bf16[1024,2048]{1,0:T(8,128)(2,1)}, f32[8,2048]{1,0:T(8,128)}, bf16[2,1024,1024]{2,1,0:T(8,128)(2,1)}) custom-call(bf16[1024,2048]{1,0:T(8,128)(2,1)} %convolution_convert_fusion.2.refs_0_, bf16[1024,2048]{1,0:T(8,128)(2,1)} %refs_1_.3, bf16[1024,2048]{1,0:T(8,128)(2,1)} %get-tuple-element.83.refs_2_, ...), custom_call_target="tpu_custom_call" | custom-call | bytes 400000000 | tf_op jit(solution)/shard_map/turn/pallas_call | solution.py:524
  428.1 4.2 fusion.49
  432.8 8.0 %fusion.71.up_ref = f32[1024,640]{1,0:T(8,128)} fusion(bf16[1024,2048]{1,0:T(8,128)(2,1)} %get-tuple-element.103, bf16[640,2048]{1,0:T(8,128)(2,1)} %get-tuple-element.104), kind=kOutput, calls=%fused_computation.141 | convolution fusion | flops 2684354560 | bytes 9437184 | tf_op jit(solution)/shard_map/dot_general | solution.py:1295
  440.8 11.6 %recur_adjoint.1 = (f32[1024,640]{1,0:T(8,128)}, f32[1024,640]{1,0:T(8,128)}, f32[8,640]{1,0:T(8,128)}, bf16[1024,640]{1,0:T(8,128)(2,1)}) custom-call(f32[1024,640]{1,0:T(8,128)} %get-tuple-element.100.rate_ref, f32[1024,640]{1,0:T(8,128)} %fusion.71.up_ref, bf16[1024,1280]{1,0:T(8,128)(2,1)} %copy-done.3, f32[1024,640]{1,0:T(8,128)} %get-tuple-element.105.state_ref, ...), custom_call_target="tpu_custom_call" | custom-call | flops 5242880 | bytes 10485760 | tf_op jit(solution)/shard_map/recur_adjoint/pallas_call | solution.py:1026
  453.8 4.6 add_convert_fusion.3
  461.3 19.3 %recur_backward.1 = (bf16[1024,1280]{1,0:T(8,128)(2,1)}, f32[8,640]{1,0:T(8,128)}, f32[8,640]{1,0:T(8,128)}, f32[640,1280]{1,0:T(8,128)}, f32[8,640]{1,0:T(8,128)}) custom-call(f32[1024,640]{1,0:T(8,128)} %get-tuple-element.106.grad_ref, f32[1024,640]{1,0:T(8,128)} %get-tuple-element.107.run_ref, f32[8,640]{1,0:T(8,128)} %copy-done.19, ...), custom_call_target="tpu_custom_call" | custom-call | flops 3355443200 | bytes 18350080 | tf_op jit(solution)/shard_map/recur_backward/pallas_call | solution.py:1141
  485.2 10.4 %convolution_convert_fusion.6 = bf16[1024,2048]{1,0:T(8,128)(2,1)} fusion(bf16[1024,1280]{1,0:T(8,128)(2,1)} %fusion.57, bf16[2048,1280]{1,0:T(8,128)(2,1)} %get-tuple-element.74), kind=kOutput, calls=%fused_computation.44 | convolution fusion | flops 5370806272 | bytes 12058624 | tf_op jit(solution)/shard_map/dot_general | solution.py:1304
  497.3 7.0 %convolution_convert_fusion.7 = bf16[1024,1280]{1,0:T(8,128)(2,1)} fusion(bf16[1024,1280]{1,0:T(8,128)(2,1)} %fusion.57, bf16[2,1024,1024]{2,1,0:T(8,128)(2,1)} %get-tuple-element.119), kind=kOutput, calls=%fused_computation.45 | convolution fusion | flops 2685665280 | bytes 7340032 | tf_op jit(solution)/shard_map/dot_general | solution.py:56
  513.7 4.1 slice_convert_fusion
  519.0 5.6 add_convert_fusion.2.part_in
  524.6 38.4 %leave.1 = (bf16[512,1280]{1,0:T(8,128)(2,1)}, bf16[160,1280]{1,0:T(8,128)(2,1)}, f32[8,640]{1,0:T(8,128)}, f32[32,128]{1,0:T(8,128)}, f32[8,128]{1,0:T(8,128)}) custom-call(bf16[1024,1280]{1,0:T(8,128)(2,1)} %add_convert_fusion.2.part_in, bf16[160,1280]{1,0:T(8,128)(2,1)} %add_convert_fusion.4.gates, f32[8,640]{1,0:T(8,128)} %get-tuple-element.122.sums, ...), custom_call_target="tpu_custom_call" | custom-call | bytes 160000000 | tf_op jit(solution)/shard_map/leave/pallas_call | solution.py:746
  (173 shorter events, 55.5 us)
Async XLA Ops:
  7.2 69.2 %all-gather.3.cloned.1.call-start = ((), (), s32[]{:S(2)}) async-start(), calls=%async_computation.10 | async-start | bytes 1638400 | tf_op jit(solution)/shard_map/all_gather | solution.py:1220
  47.0 381.1 %reduce-scatter.6.cloned.1.call-start = ((), (), s32[]{:S(2)}) async-start(), calls=%async_computation.5 | async-start | bytes 5242880 | tf_op jit(solution)/shard_map/reduce_scatter | solution.py:1270
  47.1 12.5 %copy-start.30 = (bf16[640]{0:T(1024)(128)(2,1)S(1)}, bf16[640]{0:T(1024)(128)(2,1)}, u32[]{:S(2)}) copy-start(bf16[640]{0:T(1024)(128)(2,1)} %param.34) | copy-start | bytes 3844
  47.1 13.7 %copy-start.26 = (bf16[4,640]{1,0:T(4,128)(2,1)S(1)}, bf16[4,640]{1,0:T(4,128)(2,1)}, u32[]{:S(2)}) copy-start(bf16[4,640]{1,0:T(4,128)(2,1)} %param.29) | copy-start | bytes 15364
  56.1 5.3 collective-permute-start
  76.4 3.5 collective-permute-start.2
  76.5 3.4 collective-permute-start.1
  242.8 189.4 %reduce-scatter.8.cloned.1.call-start = ((), (), s32[]{:S(2)}) async-start(), calls=%async_computation.6 | async-start | bytes 3932160 | tf_op jit(solution)/shard_map/reduce_scatter | solution.py:65
  249.1 14.7 %copy-start.34 = (bf16[2,1024,1024]{2,1,0:T(8,128)(2,1)S(1)}, bf16[2,1024,1024]{2,1,0:T(8,128)(2,1)}, u32[]{:S(2)}) copy-start(bf16[2,1024,1024]{2,1,0:T(8,128)(2,1)} %get-tuple-element.94) | copy-start | bytes 12582916
  249.1 26.8 %collective-permute-start.3 = (bf16[1536,1024]{1,0:T(8,128)(2,1)S(1)}, bf16[1536,1024]{1,0:T(8,128)(2,1)S(1)}, u32[]{:S(2)}, u32[]{:S(2)}) collective-permute-start(bf16[1536,1024]{1,0:T(8,128)(2,1)S(1)} %convolution_convert_fusion.8), channel_id=1, source_target_pairs={{0,4},{4,0},{1,5},{5,1},{2,6},{6,2},{3,7},{7,3},{8,12},{12,8},{9,1... | collective-permute-start | bytes 9437192 | tf_op jit(solution)/shard_map/ppermute | solution.py:20
  275.5 25.4 %collective-permute-start.4 = (bf16[1024,3072]{1,0:T(8,128)(2,1)}, bf16[1024,3072]{1,0:T(8,128)(2,1)}, u32[]{:S(2)}, u32[]{:S(2)}) collective-permute-start(bf16[1024,3072]{1,0:T(8,128)(2,1)} %convolution_convert_fusion), channel_id=1, source_target_pairs={{0,4},{4,0},{1,5},{5,1},{2,6},{6,2},{3,7},{7,3},{8,12},{12,8},{9,1... | collective-permute-start | bytes 18874376 | tf_op jit(solution)/shard_map/ppermute | solution.py:20
  280.8 179.9 %reduce-scatter.10.cloned.1.call-start = ((), (), s32[]{:S(2)}) async-start(), calls=%async_computation.7 | async-start | bytes 7864320 | tf_op jit(solution)/shard_map/reduce_scatter | solution.py:65
  280.8 20.1 %copy-start.35 = (bf16[2,1024,1024]{2,1,0:T(8,128)(2,1)S(1)}, bf16[2,1024,1024]{2,1,0:T(8,128)(2,1)}, u32[]{:S(2)}) copy-start(bf16[2,1024,1024]{2,1,0:T(8,128)(2,1)} %get-tuple-element.94) | copy-start | bytes 12582916
  313.5 182.1 %reduce-scatter.12.cloned.1.call-start = ((), (), s32[]{:S(2)}) async-start(), calls=%async_computation.8 | async-start | bytes 1638400 | tf_op jit(solution)/shard_map/reduce_scatter | solution.py:65
  313.5 114.5 %copy-start.37 = (bf16[1024,640]{1,0:T(8,128)(2,1)S(1)}, bf16[1024,640]{1,0:T(8,128)(2,1)}, u32[]{:S(2)}) copy-start(bf16[1024,640]{1,0:T(8,128)(2,1)} %get-tuple-element.110) | copy-start | bytes 3932164
  432.3 21.5 %collective-permute-start.7 = (bf16[640,1024]{1,0:T(8,128)(2,1)}, bf16[640,1024]{1,0:T(8,128)(2,1)}, u32[]{:S(2)}, u32[]{:S(2)}) collective-permute-start(bf16[640,1024]{1,0:T(8,128)(2,1)} %fusion.49), channel_id=1, source_target_pairs={{0,4},{4,0},{1,5},{5,1},{2,6},{6,2},{3,7},{7,3},{8,12},{12,8},{9,1... | collective-permute-start | bytes 3932168 | tf_op jit(solution)/shard_map/ppermute | solution.py:20
  432.3 26.2 %collective-permute-start.6 = (bf16[1536,256]{1,0:T(8,128)(2,1)}, bf16[1536,256]{1,0:T(8,128)(2,1)S(1)}, u32[]{:S(2)}, u32[]{:S(2)}) collective-permute-start(bf16[1536,256]{1,0:T(8,128)(2,1)} %reduce-scatter.8.cloned.1.call-done), channel_id=1, source_target_pairs={{0,4},{4,0},{1,5},{5,1},{2,6},{6,2},{3,7},{7,3},{8,12},{12,8},{9,1... | collective-permute-start | bytes 2359304 | tf_op jit(solution)/shard_map/ppermute | solution.py:20
  452.3 8.3 %collective-permute-start.5 = (f32[8,640]{1,0:T(8,128)}, f32[8,640]{1,0:T(8,128)S(1)}, u32[]{:S(2)}, u32[]{:S(2)}) collective-permute-start(f32[8,640]{1,0:T(8,128)} %get-tuple-element.108), channel_id=1, source_target_pairs={{4,0},{5,1},{6,2},{7,3},{12,8},{13,9},{14,10},{15,11},{20,16},{21,... | collective-permute-start | bytes 61448 | tf_op jit(solution)/shard_map/ppermute | solution.py:26
  458.4 114.6 %reduce-scatter.14.cloned.1.call-start = ((), (), s32[]{:S(2)}) async-start(), calls=%async_computation.9 | async-start | bytes 5242880 | tf_op jit(solution)/shard_map/reduce_scatter | solution.py:1306
  480.5 3.3 collective-permute-start.8
  497.0 8.8 %collective-permute-start.10 = (bf16[640,256]{1,0:T(8,128)(2,1)S(1)}, bf16[640,256]{1,0:T(8,128)(2,1)S(1)}, u32[]{:S(2)}, u32[]{:S(2)}) collective-permute-start(bf16[640,256]{1,0:T(8,128)(2,1)S(1)} %copy-done.18), channel_id=1, source_target_pairs={{0,4},{4,0},{1,5},{5,1},{2,6},{6,2},{3,7},{7,3},{8,12},{12,8},{9,1... | collective-permute-start | bytes 983048 | tf_op jit(solution)/shard_map/ppermute | solution.py:20
  504.3 13.5 %collective-permute-start.9 = (bf16[1024,1280]{1,0:T(8,128)(2,1)}, bf16[1024,1280]{1,0:T(8,128)(2,1)}, u32[]{:S(2)}, u32[]{:S(2)}) collective-permute-start(bf16[1024,1280]{1,0:T(8,128)(2,1)} %convolution_convert_fusion.7), channel_id=1, source_target_pairs={{0,4},{4,0},{1,5},{5,1},{2,6},{6,2},{3,7},{7,3},{8,12},{12,8},{9,1... | collective-permute-start | bytes 7864328 | tf_op jit(solution)/shard_map/ppermute | solution.py:20
  505.7 6.2 %collective-permute-start.11 = (bf16[256,3072]{1,0:T(8,128)(2,1)S(1)}, bf16[256,3072]{1,0:T(8,128)(2,1)}, u32[]{:S(2)}, u32[]{:S(2)}) collective-permute-start(bf16[256,3072]{1,0:T(8,128)(2,1)S(1)} %copy-done.11), channel_id=1, source_target_pairs={{0,4},{4,0},{1,5},{5,1},{2,6},{6,2},{3,7},{7,3},{8,12},{12,8},{9,1... | collective-permute-start | bytes 4718600 | tf_op jit(solution)/shard_map/ppermute | solution.py:20
  524.6 44.5 %copy-start.23 = (f32[640]{0:T(1024)S(1)}, f32[640]{0:T(1024)}, u32[]{:S(2)}) copy-start(f32[640]{0:T(1024)} %param.35) | copy-start | bytes 7684
  (34 other events, 211.6 us)
Sparse Core Ops, SparseCore 0:
  47.1 28.9 all-gather.2
  242.9 74.8 reduce-scatter.5
  321.4 45.0 reduce-scatter.7
  369.4 70.0 reduce-scatter.9
  458.5 29.3 reduce-scatter.11
  495.7 77.1 reduce-scatter.13

commit v9 on v8

--- a/solution.py
+++ b/solution.py
@@ -328,6 +328,8 @@
     for k, owner in enumerate(others):
         gain_copy(k, owner, owner).wait_recv()
 
+    steps = tokens.shape[0] // CHUNK
+
     def norm(t, carry):
         rows = pl.ds(pl.multiple_of(t * CHUNK, CHUNK), CHUNK)
         block = tokens[rows, :].astype(F32)
@@ -337,11 +339,14 @@
         normed[rows, :] = block
         put_split(halves, rows, block)
         put_split(upstream_halves, rows, upstream[rows, :])
+        for w in range(2):
+            @pl.when(t == (3 + 3 * w) * steps // 8)
+            def _():
+                gather.forward(w)
+
         return carry
 
-    lax.fori_loop(0, tokens.shape[0] // CHUNK, norm, 0)
-    for w in range(2):
-        gather.forward(w)
+    lax.fori_loop(0, steps, norm, 0)
     for w in range(2):
         gather.hand_over(w)
     for w in range(2):

time: 590 us -> 590 us (level)
  no operation moved by 1% of the time
where the time goes in v9:
time: 590 us; the launch traced here: 584 us
  Pallas kernels  365 us (62%)
  matrix products  144 us (24%)
  other arithmetic  28 us (5%)
  local copies, waits for them, and re-layouts  18.6 us (3%)
  between operations  15.1 us (3%)
  starting transfers between devices  9.36 us (2%)
    pallas_call x1, Pallas kernels, middle(): pl.pallas_call(lambda *refs: middle_kernel(bool(shards), *refs), out_shap...  119 us
    pallas_call x1, Pallas kernels, turn(): pl.pallas_call(lambda *refs: turn_kernel(split, *refs), out_shape=tuple(o...  114 us
    dot_general x8, matrix products, product(): return lax.dot_general(*pair, rows_to_rows, preferred_element_type=F32)  56.7 us
    pallas_call x1, Pallas kernels, leave(): pl.pallas_call(leave_kernel, out_shape=(shape((part_in.shape[0] // 2, par...  38.4 us
    pallas_call x1, Pallas kernels, enter(): pl.pallas_call(enter_kernel, out_shape=(shape((rows, features), BF16), sh...  36.9 us
    dot_general x1, matrix products, shards(): lax.dot_general(d_mid, whole_mid, rows_to_features, preferred_element_typ...  20.1 us
    pallas_call x1, Pallas kernels, recur_backward(): pl.pallas_call(backward_kernel, grid=(count,), out_shape=(jax.ShapeDtypeS...  19.3 us
    dot_general x1, matrix products, shards(): jnp.dot(normed_two, whole_mid, preferred_element_type=F32).astype(BF16)  17.1 us
  transfers between devices with their start and end apart: 18, of which 3 were waited for; matrix products, arithmetic and copies ran while one was open for 25% of the time, Pallas kernels for 34%

profile of v9, /device:TPU:0, one launch (start us, length us, event | category | flops | bytes accessed | tf_op | source)
XLA Modules:
  0.0 583.8 jit_solution(11410800577329023597)
XLA Ops:
  10.0 36.9 %enter.1 = (bf16[1024,2048]{1,0:T(8,128)(2,1)}, bf16[2,1024,1024]{2,1,0:T(8,128)(2,1)}, bf16[2,1024,1024]{2,1,0:T(8,128)(2,1)}, f32[8,2048]{1,0:T(8,128)}, f32[1...) custom-call(bf16[1024,2048]{1,0:T(8,128)(2,1)} %refs_1_.3, bf16[1024,2048]{1,0:T(8,128)(2,1)} %refs_3_.3, ...), custom_call_target="tpu_custom_call" | custom-call | tf_op jit(solution)/shard_map/enter/pallas_call | solution.py:373
  47.1 8.9 %convolution_convert_fusion.5.branch_ref.pre_ref = bf16[1024,1280]{1,0:T(8,128)(2,1)S(1)} fusion(bf16[1024,2048]{1,0:T(8,128)(2,1)} %get-tuple-element.73, bf16[2048,1280]{1,0:T(8,128)(2,1)} %get-tuple-element.74), kind=kOutput, calls=%fused_computation.43 | convolution fusion | flops 5370019840 | bytes 12058624 | tf_op jit(solution)/shard_map/dot_general | solution.py:1251
  62.0 14.4 %recur_forward.1 = (bf16[1024,640]{1,0:T(8,128)(2,1)}, f32[1024,640]{1,0:T(8,128)}, f32[1024,640]{1,0:T(8,128)}, f32[1024,640]{1,0:T(8,128)}, f32[1024,640]{1,0:...) custom-call(bf16[1024,1280]{1,0:T(8,128)(2,1)} %copy-done.3, bf16[8,640]{1,0:T(8,128)(2,1)} %copy-done.24, ...), custom_call_target="tpu_custom_call" | custom-call | flops 1677721600 | bytes 15728640 | tf_op jit(solution)/shard_map/recur_forward/pallas_call | solution.py:917
  81.0 11.6 %merge_states.1 = (f32[1024,640]{1,0:T(8,128)}, bf16[1024,640]{1,0:T(8,128)(2,1)}, bf16[1024,2048]{1,0:T(8,128)(2,1)}, bf16[640,2048]{1,0:T(8,128)(2,1)}) custom-call(f32[1024,640]{1,0:T(8,128)} %get-tuple-element.75.local_ref, f32[1024,640]{1,0:T(8,128)} %get-tuple-element.76.run_ref, f32[8,640]{1,0:T(8,128)} %copy-done.20, bf16[1024,1280]{1,0:T(8,128)(2,1)} %copy-done.3, ...), custom_call_target="tpu_custom_call" | custom-call | flops 2684354560 | bytes 10485760 | tf_op jit(solution)/shard_map/merge_states/pallas_call | solution.py:974
  92.6 118.6 %middle.1 = (bf16[1024,2048]{1,0:T(8,128)(2,1)}, bf16[1024,2048]{1,0:T(8,128)(2,1)}, bf16[2,1024,1024]{2,1,0:T(8,128)(2,1)}, bf16[2048,3072]{1,0:T(8,128)(2,1)}, bf16[1536,2048]{1,0:T(8,128)(2,1)}) custom-call(bf16[1024,2048]{1,0:T(8,128)(2,1)} %get-tuple-element.81.refs_0_, bf16[1024,2048]{1,0:T(8,128)(2,1)} %refs_1_.3, ...), custom_call_target="tpu_custom_call" | custom-call | bytes 400000000 | tf_op jit(solution)/shard_map/middle/pallas_call | solution.py:473
  211.2 17.1 %convolution_convert_fusion.1 = bf16[1024,3072]{1,0:T(8,128)(2,1)S(1)} fusion(bf16[1024,2048]{1,0:T(8,128)(2,1)} %get-tuple-element.84, bf16[2048,3072]{1,0:T(8,128)(2,1)} %get-tuple-element.90), kind=kOutput, calls=%fused_computation.38 | convolution fusion | flops 12888047616 | bytes 23068672 | tf_op jit(solution)/shard_map/dot_general | solution.py:1271
  234.5 8.3 %convolution_convert_fusion.4 = bf16[1024,2048]{1,0:T(8,128)(2,1)} fusion(bf16[1024,1536]{1,0:T(8,128)(2,1)S(1)} %fusion.10, bf16[1536,2048]{1,0:T(8,128)(2,1)S(1)} %copy-done.31), kind=kOutput, calls=%fused_computation.42 | convolution fusion | flops 6444548096 | bytes 13631488 | tf_op jit(solution)/shard_map/dot_general | solution.py:1274
  242.9 6.2 %convolution_convert_fusion.8 = bf16[1536,1024]{1,0:T(8,128)(2,1)S(1)} fusion(bf16[1024,1536]{1,0:T(8,128)(2,1)} %copy-done.8, bf16[2,1024,1024]{2,1,0:T(8,128)(2,1)} %get-tuple-element.92), kind=kOutput, calls=%fused_computation.46 | convolution fusion | flops 3222798336 | bytes 8388608 | tf_op jit(solution)/shard_map/dot_general | solution.py:56
  249.2 14.5 %fusion.6 = (bf16[1024,1536]{1,0:T(8,128)(2,1)}, bf16[1024,1536]{1,0:T(8,128)(2,1)}) fusion(bf16[1024,3072]{1,0:T(8,128)(2,1)S(1)} %bitcast.76, bf16[1024,2048]{1,0:T(8,128)(2,1)S(1)} %copy-done.5, bf16[1536,2048]{1,0:T(8,128)(2,1)} %get-tuple-element.86), kind=kOutput, calls=%fused_computation.24 | convolution fusion | flops 6484918272 | bytes 23068672 | tf_op jit(solution)/shard_map/dot_general | solution.py:1279
  263.8 11.8 %convolution_convert_fusion = bf16[1024,3072]{1,0:T(8,128)(2,1)} fusion(bf16[2,1024,1024]{2,1,0:T(8,128)(2,1)S(1)} %copy-done.34, bf16[1024,1536]{1,0:T(8,128)(2,1)} %get-tuple-element.138, bf16[1024,1536]{1,0:T(8,128)(2,1)} %get-tuple-element.137), kind=kOutput, calls=%fused_computation.37 | convolution fusion | flops 6458179584 | bytes 14680064 | tf_op jit(solution)/shard_map/dot_general | solution.py:56
  275.9 4.9 add_convert_fusion.1
  280.8 20.1 %convolution_convert_fusion.2.refs_0_ = bf16[1024,2048]{1,0:T(8,128)(2,1)} fusion(bf16[2048,3072]{1,0:T(8,128)(2,1)} %get-tuple-element.90, bf16[1024,1536]{1,0:T(8,128)(2,1)} %get-tuple-element.138, bf16[1024,1536]{1,0:T(8,128)(2,1)} %get-tuple-element.137), kind=kOutput, calls=%fused_computation.40 | convolution fusion | flops 12899581952 | bytes 23068672 | tf_op jit(solution)/shard_map/dot_general | solution.py:1286
  301.0 12.5 %add_convert_fusion = bf16[1024,3072]{1,0:T(8,128)(2,1)} fusion(bf16[1024,3072]{1,0:T(8,128)(2,1)} %collective-permute-done.4, bf16[2,1024,1024]{2,1,0:T(8,128)(2,1)S(1)} %copy-done.35, bf16[1024,1536]{1,0:T(8,128)(2,1)} %get-tuple-element.138, bf16[1024,1536]{1,0:T(8,128)(2,1)} %get-tuple-element.137), kind=kOutput, calls=%fused_computation.7 | convolution fusion | flops 6464471040 | bytes 20971520 | tf_op jit(solution)/shard_map/dot_general | solution.py:56
  313.6 114.4 %turn.1 = (f32[1024,512]{1,0:T(8,128)}, bf16[1024,2048]{1,0:T(8,128)(2,1)}, f32[8,2048]{1,0:T(8,128)}, bf16[2,1024,1024]{2,1,0:T(8,128)(2,1)}) custom-call(bf16[1024,2048]{1,0:T(8,128)(2,1)} %convolution_convert_fusion.2.refs_0_, bf16[1024,2048]{1,0:T(8,128)(2,1)} %refs_1_.3, bf16[1024,2048]{1,0:T(8,128)(2,1)} %get-tuple-element.83.refs_2_, ...), custom_call_target="tpu_custom_call" | custom-call | bytes 400000000 | tf_op jit(solution)/shard_map/turn/pallas_call | solution.py:529
  428.1 4.2 fusion.49
  432.8 8.0 %fusion.71.up_ref = f32[1024,640]{1,0:T(8,128)} fusion(bf16[1024,2048]{1,0:T(8,128)(2,1)} %get-tuple-element.103, bf16[640,2048]{1,0:T(8,128)(2,1)} %get-tuple-element.104), kind=kOutput, calls=%fused_computation.141 | convolution fusion | flops 2684354560 | bytes 9437184 | tf_op jit(solution)/shard_map/dot_general | solution.py:1300
  440.8 11.6 %recur_adjoint.1 = (f32[1024,640]{1,0:T(8,128)}, f32[1024,640]{1,0:T(8,128)}, f32[8,640]{1,0:T(8,128)}, bf16[1024,640]{1,0:T(8,128)(2,1)}) custom-call(f32[1024,640]{1,0:T(8,128)} %get-tuple-element.100.rate_ref, f32[1024,640]{1,0:T(8,128)} %fusion.71.up_ref, bf16[1024,1280]{1,0:T(8,128)(2,1)} %copy-done.3, f32[1024,640]{1,0:T(8,128)} %get-tuple-element.105.state_ref, ...), custom_call_target="tpu_custom_call" | custom-call | flops 5242880 | bytes 10485760 | tf_op jit(solution)/shard_map/recur_adjoint/pallas_call | solution.py:1031
  453.8 4.6 add_convert_fusion.3
  461.3 19.3 %recur_backward.1 = (bf16[1024,1280]{1,0:T(8,128)(2,1)}, f32[8,640]{1,0:T(8,128)}, f32[8,640]{1,0:T(8,128)}, f32[640,1280]{1,0:T(8,128)}, f32[8,640]{1,0:T(8,128)}) custom-call(f32[1024,640]{1,0:T(8,128)} %get-tuple-element.106.grad_ref, f32[1024,640]{1,0:T(8,128)} %get-tuple-element.107.run_ref, f32[8,640]{1,0:T(8,128)} %copy-done.19, ...), custom_call_target="tpu_custom_call" | custom-call | flops 3355443200 | bytes 18350080 | tf_op jit(solution)/shard_map/recur_backward/pallas_call | solution.py:1146
  485.2 10.4 %convolution_convert_fusion.6 = bf16[1024,2048]{1,0:T(8,128)(2,1)} fusion(bf16[1024,1280]{1,0:T(8,128)(2,1)} %fusion.57, bf16[2048,1280]{1,0:T(8,128)(2,1)} %get-tuple-element.74), kind=kOutput, calls=%fused_computation.44 | convolution fusion | flops 5370806272 | bytes 12058624 | tf_op jit(solution)/shard_map/dot_general | solution.py:1309
  497.3 7.0 %convolution_convert_fusion.7 = bf16[1024,1280]{1,0:T(8,128)(2,1)} fusion(bf16[1024,1280]{1,0:T(8,128)(2,1)} %fusion.57, bf16[2,1024,1024]{2,1,0:T(8,128)(2,1)} %get-tuple-element.119), kind=kOutput, calls=%fused_computation.45 | convolution fusion | flops 2685665280 | bytes 7340032 | tf_op jit(solution)/shard_map/dot_general | solution.py:56
  513.7 4.1 slice_convert_fusion
  519.0 5.6 add_convert_fusion.2.part_in
  524.6 38.4 %leave.1 = (bf16[512,1280]{1,0:T(8,128)(2,1)}, bf16[160,1280]{1,0:T(8,128)(2,1)}, f32[8,640]{1,0:T(8,128)}, f32[32,128]{1,0:T(8,128)}, f32[8,128]{1,0:T(8,128)}) custom-call(bf16[1024,1280]{1,0:T(8,128)(2,1)} %add_convert_fusion.2.part_in, bf16[160,1280]{1,0:T(8,128)(2,1)} %add_convert_fusion.4.gates, f32[8,640]{1,0:T(8,128)} %get-tuple-element.122.sums, ...), custom_call_target="tpu_custom_call" | custom-call | bytes 160000000 | tf_op jit(solution)/shard_map/leave/pallas_call | solution.py:751
  (173 shorter events, 55.5 us)
Async XLA Ops:
  7.2 69.2 %all-gather.3.cloned.1.call-start = ((), (), s32[]{:S(2)}) async-start(), calls=%async_computation.10 | async-start | bytes 1638400 | tf_op jit(solution)/shard_map/all_gather | solution.py:1225
  47.0 381.1 %reduce-scatter.6.cloned.1.call-start = ((), (), s32[]{:S(2)}) async-start(), calls=%async_computation.5 | async-start | bytes 5242880 | tf_op jit(solution)/shard_map/reduce_scatter | solution.py:1275
  47.1 12.5 %copy-start.30 = (bf16[640]{0:T(1024)(128)(2,1)S(1)}, bf16[640]{0:T(1024)(128)(2,1)}, u32[]{:S(2)}) copy-start(bf16[640]{0:T(1024)(128)(2,1)} %param.34) | copy-start | bytes 3844
  47.1 13.7 %copy-start.26 = (bf16[4,640]{1,0:T(4,128)(2,1)S(1)}, bf16[4,640]{1,0:T(4,128)(2,1)}, u32[]{:S(2)}) copy-start(bf16[4,640]{1,0:T(4,128)(2,1)} %param.29) | copy-start | bytes 15364
  56.1 5.3 collective-permute-start
  76.4 3.5 collective-permute-start.2
  76.5 3.4 collective-permute-start.1
  242.8 189.4 %reduce-scatter.8.cloned.1.call-start = ((), (), s32[]{:S(2)}) async-start(), calls=%async_computation.6 | async-start | bytes 3932160 | tf_op jit(solution)/shard_map/reduce_scatter | solution.py:65
  249.1 14.7 %copy-start.34 = (bf16[2,1024,1024]{2,1,0:T(8,128)(2,1)S(1)}, bf16[2,1024,1024]{2,1,0:T(8,128)(2,1)}, u32[]{:S(2)}) copy-start(bf16[2,1024,1024]{2,1,0:T(8,128)(2,1)} %get-tuple-element.94) | copy-start | bytes 12582916
  249.1 26.8 %collective-permute-start.3 = (bf16[1536,1024]{1,0:T(8,128)(2,1)S(1)}, bf16[1536,1024]{1,0:T(8,128)(2,1)S(1)}, u32[]{:S(2)}, u32[]{:S(2)}) collective-permute-start(bf16[1536,1024]{1,0:T(8,128)(2,1)S(1)} %convolution_convert_fusion.8), channel_id=1, source_target_pairs={{0,4},{4,0},{1,5},{5,1},{2,6},{6,2},{3,7},{7,3},{8,12},{12,8},{9,1... | collective-permute-start | bytes 9437192 | tf_op jit(solution)/shard_map/ppermute | solution.py:20
  275.5 25.4 %collective-permute-start.4 = (bf16[1024,3072]{1,0:T(8,128)(2,1)}, bf16[1024,3072]{1,0:T(8,128)(2,1)}, u32[]{:S(2)}, u32[]{:S(2)}) collective-permute-start(bf16[1024,3072]{1,0:T(8,128)(2,1)} %convolution_convert_fusion), channel_id=1, source_target_pairs={{0,4},{4,0},{1,5},{5,1},{2,6},{6,2},{3,7},{7,3},{8,12},{12,8},{9,1... | collective-permute-start | bytes 18874376 | tf_op jit(solution)/shard_map/ppermute | solution.py:20
  280.8 179.9 %reduce-scatter.10.cloned.1.call-start = ((), (), s32[]{:S(2)}) async-start(), calls=%async_computation.7 | async-start | bytes 7864320 | tf_op jit(solution)/shard_map/reduce_scatter | solution.py:65
  280.8 20.1 %copy-start.35 = (bf16[2,1024,1024]{2,1,0:T(8,128)(2,1)S(1)}, bf16[2,1024,1024]{2,1,0:T(8,128)(2,1)}, u32[]{:S(2)}) copy-start(bf16[2,1024,1024]{2,1,0:T(8,128)(2,1)} %get-tuple-element.94) | copy-start | bytes 12582916
  313.5 182.1 %reduce-scatter.12.cloned.1.call-start = ((), (), s32[]{:S(2)}) async-start(), calls=%async_computation.8 | async-start | bytes 1638400 | tf_op jit(solution)/shard_map/reduce_scatter | solution.py:65
  313.5 114.5 %copy-start.37 = (bf16[1024,640]{1,0:T(8,128)(2,1)S(1)}, bf16[1024,640]{1,0:T(8,128)(2,1)}, u32[]{:S(2)}) copy-start(bf16[1024,640]{1,0:T(8,128)(2,1)} %get-tuple-element.110) | copy-start | bytes 3932164
  432.3 21.5 %collective-permute-start.7 = (bf16[640,1024]{1,0:T(8,128)(2,1)}, bf16[640,1024]{1,0:T(8,128)(2,1)}, u32[]{:S(2)}, u32[]{:S(2)}) collective-permute-start(bf16[640,1024]{1,0:T(8,128)(2,1)} %fusion.49), channel_id=1, source_target_pairs={{0,4},{4,0},{1,5},{5,1},{2,6},{6,2},{3,7},{7,3},{8,12},{12,8},{9,1... | collective-permute-start | bytes 3932168 | tf_op jit(solution)/shard_map/ppermute | solution.py:20
  432.3 26.2 %collective-permute-start.6 = (bf16[1536,256]{1,0:T(8,128)(2,1)}, bf16[1536,256]{1,0:T(8,128)(2,1)S(1)}, u32[]{:S(2)}, u32[]{:S(2)}) collective-permute-start(bf16[1536,256]{1,0:T(8,128)(2,1)} %reduce-scatter.8.cloned.1.call-done), channel_id=1, source_target_pairs={{0,4},{4,0},{1,5},{5,1},{2,6},{6,2},{3,7},{7,3},{8,12},{12,8},{9,1... | collective-permute-start | bytes 2359304 | tf_op jit(solution)/shard_map/ppermute | solution.py:20
  452.3 8.3 %collective-permute-start.5 = (f32[8,640]{1,0:T(8,128)}, f32[8,640]{1,0:T(8,128)S(1)}, u32[]{:S(2)}, u32[]{:S(2)}) collective-permute-start(f32[8,640]{1,0:T(8,128)} %get-tuple-element.108), channel_id=1, source_target_pairs={{4,0},{5,1},{6,2},{7,3},{12,8},{13,9},{14,10},{15,11},{20,16},{21,... | collective-permute-start | bytes 61448 | tf_op jit(solution)/shard_map/ppermute | solution.py:26
  458.4 114.6 %reduce-scatter.14.cloned.1.call-start = ((), (), s32[]{:S(2)}) async-start(), calls=%async_computation.9 | async-start | bytes 5242880 | tf_op jit(solution)/shard_map/reduce_scatter | solution.py:1311
  480.5 3.3 collective-permute-start.8
  497.0 8.8 %collective-permute-start.10 = (bf16[640,256]{1,0:T(8,128)(2,1)S(1)}, bf16[640,256]{1,0:T(8,128)(2,1)S(1)}, u32[]{:S(2)}, u32[]{:S(2)}) collective-permute-start(bf16[640,256]{1,0:T(8,128)(2,1)S(1)} %copy-done.18), channel_id=1, source_target_pairs={{0,4},{4,0},{1,5},{5,1},{2,6},{6,2},{3,7},{7,3},{8,12},{12,8},{9,1... | collective-permute-start | bytes 983048 | tf_op jit(solution)/shard_map/ppermute | solution.py:20
  504.3 13.5 %collective-permute-start.9 = (bf16[1024,1280]{1,0:T(8,128)(2,1)}, bf16[1024,1280]{1,0:T(8,128)(2,1)}, u32[]{:S(2)}, u32[]{:S(2)}) collective-permute-start(bf16[1024,1280]{1,0:T(8,128)(2,1)} %convolution_convert_fusion.7), channel_id=1, source_target_pairs={{0,4},{4,0},{1,5},{5,1},{2,6},{6,2},{3,7},{7,3},{8,12},{12,8},{9,1... | collective-permute-start | bytes 7864328 | tf_op jit(solution)/shard_map/ppermute | solution.py:20
  505.7 6.2 %collective-permute-start.11 = (bf16[256,3072]{1,0:T(8,128)(2,1)S(1)}, bf16[256,3072]{1,0:T(8,128)(2,1)}, u32[]{:S(2)}, u32[]{:S(2)}) collective-permute-start(bf16[256,3072]{1,0:T(8,128)(2,1)S(1)} %copy-done.11), channel_id=1, source_target_pairs={{0,4},{4,0},{1,5},{5,1},{2,6},{6,2},{3,7},{7,3},{8,12},{12,8},{9,1... | collective-permute-start | bytes 4718600 | tf_op jit(solution)/shard_map/ppermute | solution.py:20
  524.6 44.5 %copy-start.23 = (f32[640]{0:T(1024)S(1)}, f32[640]{0:T(1024)}, u32[]{:S(2)}) copy-start(f32[640]{0:T(1024)} %param.35) | copy-start | bytes 7684
  (34 other events, 211.6 us)
Sparse Core Ops, SparseCore 0:
  47.1 28.9 all-gather.2
  242.9 74.8 reduce-scatter.5
  321.4 45.0 reduce-scatter.7
  369.4 70.0 reduce-scatter.9
  458.5 29.3 reduce-scatter.11
  495.7 77.1 reduce-scatter.13
